TPU v7x, 512 devices: a whole 4x8x8 slice. The times are simulated.
512 devices in a mesh: au: 32 (over z, y_lo), ia: 16 (over x, y_hi, core).
Axes of the slice: x: 4, y: 8 (y_hi: 2, y_lo: 4; y = y_hi * 4 + y_lo), z: 8, core: 2. Of those that a mesh axis runs over, the one named last changes fastest.
Arguments:
- user_emb: bfloat16 [32, 2048, 256], P('au', 'ia'), may hold values from -6 to 6
- item_emb: bfloat16 [16, 1024, 256], P('ia', 'au'), may hold values from -6 to 6
- weight: bfloat16 [256, 256], replicated, may hold values from -0.375 to 0.375
- grad_user: bfloat16 [32, 2048, 256], P('au', 'ia'), may hold values from -6 to 6
- grad_item: bfloat16 [16, 1024, 256], P('ia', 'au'), may hold values from -6 to 6
- tile_values: bfloat16 [32, 2048, 128, 128], P('au', 'ia'), may hold values from 0 to 1
- tile_rows: int32 [32, 2048], P('au', 'ia'), may hold values from 0 to 15
- tile_cols: int32 [32, 2048], P('au', 'ia'), may hold values from 0 to 7
- tile_norm: int32 [32, 2048], P('au', 'ia'), may hold values from 32 to 128
- tile_count: int32 [32, 16], P('au', 'ia'), may hold values from 64 to 128, as said below
Outputs:
- grad_user_emb: bfloat16 [32, 2048, 256], P('au', 'ia')
- grad_item_emb: bfloat16 [16, 1024, 256], P('ia', 'au')
- grad_weight: float32 [256, 256], replicated
Inputs may be any that keep to these rules, and one draw needn't show every extreme that they name: `tile_rows`: slots of one block pair may name the same tile position; their terms add. Slots at and after tile_count[a, b] are unused; some block pair has exactly 128 live slots in every draw.
All inputs are finite; a program needn't handle non-finite values.
Results may differ from a plain program's by a relative error of at most 0.025.
Values may be sent and summed in bfloat16 or wider, within the bound.
No kernel may reach another device: no remote copies, remote signals or barrier semaphores. Data moves between devices by JAX's collectives and lax.ppermute only.
A program may use at most 64 MiB of HBM per device.

v0:
```python
import math

import jax
import jax.numpy as jnp
from jax import lax
from jax.sharding import PartitionSpec as P

slot_group = 8


def from_everyone(value, axis):
    copies = jnp.broadcast_to(value, (lax.axis_size(axis), *value.shape))
    return lax.all_to_all(copies, axis, split_axis=0, concat_axis=0, tiled=True)


def in_order(pieces, dim):
    pieces = jnp.moveaxis(pieces, 0, dim)
    shape = pieces.shape
    return pieces.reshape(*shape[:dim], shape[dim] * shape[dim + 1], *shape[dim + 2 :])


def collect(value, axis, dim):
    pieces = from_everyone(value, axis)
    return in_order(pieces, dim)


def in_blocks(value, dim, peers):
    shape = value.shape
    pieces = value.reshape(*shape[:dim], peers, shape[dim] // peers, *shape[dim + 1 :])
    return jnp.moveaxis(pieces, dim, 0)


def summed_on_arrival(value, axis, dim):
    pieces = in_blocks(value, dim, lax.axis_size(axis))
    arrived = lax.all_to_all(pieces, axis, split_axis=0, concat_axis=0, tiled=True)
    return arrived.astype(jnp.float32).sum(axis=0)


def split_tiles(block, edge):
    return block.reshape(-1, edge, block.shape[-1])


def fetch_items(grad_item, edge):
    cotangent = collect(grad_item, "au", 1)
    return (split_tiles(cotangent[0], edge), None)


def fetch_users(grad_user, edge):
    cotangent = collect(grad_user, "ia", 1)
    return (split_tiles(cotangent[0], edge), None)


def sweep(
    tile_block,
    row_ids,
    col_ids,
    norm_ids,
    live_count,
    item_source,
    user_source,
    user_shape,
    item_shape,
):
    turn_count = (live_count + slot_group - 1) // slot_group
    placeholder = jnp.zeros((1,), jnp.float32)

    def one_turn(turn_index, totals):
        user_total, item_total = totals
        first_slot = turn_index * slot_group
        values = lax.dynamic_slice_in_dim(tile_block, first_slot, slot_group, 0)
        row_pick = lax.dynamic_slice_in_dim(row_ids, first_slot, slot_group, 0)
        col_pick = lax.dynamic_slice_in_dim(col_ids, first_slot, slot_group, 0)
        norm_pick = lax.dynamic_slice_in_dim(norm_ids, first_slot, slot_group, 0)
        live_mask = first_slot + jnp.arange(slot_group, dtype=jnp.int32) < live_count
        inverse = jnp.where(live_mask, 1.0 / norm_pick.astype(jnp.float32), 0.0)[:, None, None]
        if item_source is not None:
            forward = jnp.einsum(
                "gic,gcd->gid", values, item_source[col_pick], preferred_element_type=jnp.float32
            )
            user_total = user_total.at[row_pick].add(forward * inverse)
        if user_source is not None:
            backward = jnp.einsum(
                "gic,gid->gcd", values, user_source[row_pick], preferred_element_type=jnp.float32
            )
            item_total = item_total.at[col_pick].add(backward * inverse)
        return (user_total, item_total)

    start = (
        jnp.zeros(user_shape, jnp.float32) if item_source is not None else placeholder,
        jnp.zeros(item_shape, jnp.float32) if user_source is not None else placeholder,
    )
    return lax.fori_loop(0, turn_count, one_turn, start)


def reduce_users(user_total, width):
    return summed_on_arrival(user_total.reshape(-1, width).astype(jnp.bfloat16), "ia", 0)


def reduce_items(item_total, width):
    return summed_on_arrival(item_total.reshape(-1, width).astype(jnp.bfloat16), "au", 0)


def block_product(embedded, total):
    return jnp.einsum(
        "rd,re->de", embedded.astype(jnp.float32), total, precision=lax.Precision.HIGHEST
    )


def per_device(
    user_emb,
    item_emb,
    weight,
    grad_user,
    grad_item,
    tile_values,
    tile_rows,
    tile_cols,
    tile_norm,
    tile_count,
):
    width = weight.shape[0]
    edge = tile_values.shape[2]
    user_shape = (user_emb.shape[1] * lax.axis_size("ia") // edge, edge, width)
    item_shape = (item_emb.shape[1] * lax.axis_size("au") // edge, edge, width)
    tile_block = tile_values[0]
    row_ids = tile_rows[0]
    col_ids = tile_cols[0]
    norm_ids = tile_norm[0]
    live_count = tile_count[0, 0]
    item_source, item_rows = fetch_items(grad_item, edge)
    user_total, unused = sweep(
        tile_block,
        row_ids,
        col_ids,
        norm_ids,
        live_count,
        item_source,
        None,
        user_shape,
        item_shape,
    )
    q_user = reduce_users(user_total, width)
    user_source, user_rows = fetch_users(grad_user, edge)
    unused, item_total = sweep(
        tile_block,
        row_ids,
        col_ids,
        norm_ids,
        live_count,
        None,
        user_source,
        user_shape,
        item_shape,
    )
    q_item = reduce_items(item_total, width)
    weight_part = block_product(user_emb[0], q_user) + block_product(item_emb[0], q_item)
    user_count = user_emb.shape[1] * lax.axis_size("ia") * lax.axis_size("au")
    item_count = item_emb.shape[1] * lax.axis_size("au") * lax.axis_size("ia")
    grad_weight = lax.psum(weight_part, ("au", "ia")) / math.sqrt(user_count + item_count)
    grad_user_emb = jnp.einsum(
        "re,de->rd", q_user.astype(jnp.bfloat16), weight, preferred_element_type=jnp.float32
    ).astype(jnp.bfloat16)
    grad_item_emb = jnp.einsum(
        "re,de->rd", q_item.astype(jnp.bfloat16), weight, preferred_element_type=jnp.float32
    ).astype(jnp.bfloat16)
    return (grad_user_emb[None], grad_item_emb[None], grad_weight)


def solution(mesh):
    return jax.shard_map(
        per_device,
        mesh=mesh,
        in_specs=(
            P("au", "ia", None),
            P("ia", "au", None),
            P(),
            P("au", "ia", None),
            P("ia", "au", None),
            P("au", "ia", None, None),
            P("au", "ia"),
            P("au", "ia"),
            P("au", "ia"),
            P("au", "ia"),
        ),
        out_specs=(P("au", "ia", None), P("ia", "au", None), P()),
        check_vma=False,
    )
```

profile of v0, /device:TPU:1, one launch (start us, length us, event | category | flops | bytes accessed | tf_op | source)
XLA Modules:
  0.0 565.6 jit_solution(4700820097756876434)
XLA Ops:
  7.2 2.0 broadcast_in_dim.43
  9.2 11.1 %all-to-all-start.2 = ((bf16[16,1,128,256]{3,2,1,0:T(8,128)(2,1)}), bf16[16,1,128,256]{3,2,1,0:T(8,128)(2,1)}, u32[]{:S(2)}, u32[]{:S(2)}) async-start(bf16[16,1,128,256]{3,2,1,0:T(8,128)(2,1)} %broadcast_in_dim.43), calls=%async_computation.2 | async-start | bytes 2097152 | tf_op jit(solution)/shard_map/all_to_all | solution.py:13
  20.9 6.4 %copy.16 = bf16[1,128,128,128]{2,3,1,0:T(8,128)(2,1)} copy(bf16[1,128,128,128]{3,2,1,0:T(8,128)(2,1)} %param.19) | data formatting | bytes 8388608 | tf_op args[5]
  27.3 18.3 %all-to-all-done.2 = bf16[16,1,128,256]{3,2,1,0:T(8,128)(2,1)} async-done(((bf16[16,1,128,256]{3,2,1,0:T(8,128)(2,1)}), bf16[16,1,128,256]{3,2,1,0:T(8,128)(2,1)}, u32[]{:S(2)}, u32[]{:S(2)}) %all-to-all-start.2) | async-done | bytes 1048608 | tf_op jit(solution)/shard_map/all_to_all | solution.py:13
  46.4 16.3 %all-to-all-start = ((bf16[32,1,32,256]{3,2,1,0:T(8,128)(2,1)}), bf16[32,1,32,256]{3,2,1,0:T(8,128)(2,1)S(1)}, u32[]{:S(2)}, u32[]{:S(2)}) async-start(bf16[32,1,32,256]{3,2,1,0:T(8,128)(2,1)} %broadcast_in_dim.40), calls=%async_computation | async-start | bytes 1048576 | tf_op jit(solution)/shard_map/all_to_all | solution.py:13
  62.8 73.2 %while.21 = (s32[]{:T(128)}, f32[8,128,256]{2,1,0:T(8,128)S(1)}, s32[]{:T(128)}, s32[128]{0:T(128)S(1)}, bf16[128,128,128]{1,2,0:T(8,128)(2,1)}, /*index=5*/s32[...) while((s32[]{:T(128)}, f32[8,128,256]{2,1,0:T(8,128)S(1)}, ...), condition=%wide.region_6.7_spmd, body=%wide.region_4.6_spmd.sunk | while | flops 67634272 | bytes 6033919 | solution.py:92
  63.7 1.8 gather_fusion.1
  68.9 1.8 gather_fusion.1
  72.0 1.3 scatter_fusion.1
  74.1 1.8 gather_fusion.1
  79.4 1.8 gather_fusion.1
  84.6 1.8 gather_fusion.1
  87.7 1.3 scatter_fusion.1
  89.8 1.8 gather_fusion.1
  95.1 1.8 gather_fusion.1
  98.1 1.3 scatter_fusion.1
  100.3 1.8 gather_fusion.1
  103.3 1.3 scatter_fusion.1
  105.5 1.8 gather_fusion.1
  108.6 1.3 scatter_fusion.1
  110.8 1.8 gather_fusion.1
  116.0 1.8 gather_fusion.1
  121.2 1.8 gather_fusion.1
  124.3 1.3 scatter_fusion.1
  126.4 1.8 gather_fusion.1
  131.7 1.8 gather_fusion.1
  134.7 1.3 scatter_fusion.1
  136.9 16.9 %all-to-all-start.3 = ((bf16[32,32,256]{2,1,0:T(8,128)(2,1)}), bf16[32,32,256]{2,1,0:T(8,128)(2,1)S(1)}, u32[]{:S(2)}, u32[]{:S(2)}) async-start(bf16[32,32,256]{2,1,0:T(8,128)(2,1)} %bitcast.11), calls=%async_computation.3 | async-start | bytes 1048576 | tf_op jit(solution)/shard_map/all_to_all | solution.py:35
  153.9 1.6 broadcast_in_dim.39
  155.4 83.1 %while.20 = (s32[]{:T(128)}, f32[16,128,256]{2,1,0:T(8,128)}, s32[]{:T(128)}, s32[128]{0:T(128)S(1)}, bf16[128,128,128]{2,1,0:T(8,128)(2,1)}, /*index=5*/s32[128...) while((s32[]{:T(128)}, f32[16,128,256]{2,1,0:T(8,128)}, ...), condition=%wide.region_2.3_spmd, body=%wide.region_0.2_spmd.sunk | while | flops 67634272 | bytes 6033919 | solution.py:92
  158.1 3.3 scatter_fusion
  164.0 3.4 scatter_fusion
  170.1 3.3 scatter_fusion
  176.0 3.4 scatter_fusion
  182.0 3.3 scatter_fusion
  188.0 3.3 scatter_fusion
  193.9 3.3 scatter_fusion
  199.8 3.2 scatter_fusion
  205.7 3.3 scatter_fusion
  211.6 3.3 scatter_fusion
  217.6 3.3 scatter_fusion
  223.5 3.3 scatter_fusion
  229.5 3.2 scatter_fusion
  235.3 3.2 scatter_fusion
  238.6 2.7 convert_element_type.37
  241.3 15.7 %all-to-all-start.1 = ((bf16[16,128,256]{2,1,0:T(8,128)(2,1)}), bf16[16,128,256]{2,1,0:T(8,128)(2,1)S(1)}, u32[]{:S(2)}, u32[]{:S(2)}) async-start(bf16[16,128,256]{2,1,0:T(8,128)(2,1)} %convert_element_type.37), calls=%async_computation.1 | async-start | bytes 2097152 | tf_op jit(solution)/shard_map/all_to_all | solution.py:35
  257.5 19.2 %all-to-all-done.1 = bf16[16,128,256]{2,1,0:T(8,128)(2,1)S(1)} async-done(((bf16[16,128,256]{2,1,0:T(8,128)(2,1)}), bf16[16,128,256]{2,1,0:T(8,128)(2,1)S(1)}, u32[]{:S(2)}, u32[]{:S(2)}) %all-to-all-start.1) | async-done | bytes 1048608 | tf_op jit(solution)/shard_map/all_to_all | solution.py:35
  279.5 277.5 %all-reduce.2.cloned.1.call-done = f32[256,256]{0,1:T(8,128)} async-done(((f32[256,256]{0,1:T(8,128)}), f32[256,256]{0,1:T(8,128)}) %all-reduce.2.cloned.1.call-update) | async-done | bytes 262160 | tf_op jit(solution)/shard_map/psum | solution.py:159
  (162 shorter events, 81.5 us)
Async XLA Ops:
  7.2 270.7 %copy-start = (bf16[256,256]{1,0:T(8,128)(2,1)S(1)}, bf16[256,256]{1,0:T(8,128)(2,1)}, u32[]{:S(2)}) copy-start(bf16[256,256]{1,0:T(8,128)(2,1)} %param.16) | copy-start | bytes 393220
  9.2 36.4 %all-to-all-start.2 = ((bf16[16,1,128,256]{3,2,1,0:T(8,128)(2,1)}), bf16[16,1,128,256]{3,2,1,0:T(8,128)(2,1)}, u32[]{:S(2)}, u32[]{:S(2)}) async-start(bf16[16,1,128,256]{3,2,1,0:T(8,128)(2,1)} %broadcast_in_dim.43), calls=%async_computation.2 | async-start | bytes 2097152 | tf_op jit(solution)/shard_map/all_to_all | solution.py:13
  20.9 24.7 %copy-start.5 = (bf16[1,32,256]{2,1,0:T(8,128)(2,1)S(1)}, bf16[1,32,256]{2,1,0:T(8,128)(2,1)}, u32[]{:S(2)}) copy-start(bf16[1,32,256]{2,1,0:T(8,128)(2,1)} %param.18) | copy-start | bytes 49156
  27.3 35.5 %copy-start.2 = (s32[1,128]{1,0:T(1,128)S(1)}, s32[1,128]{1,0:T(1,128)}, u32[]{:S(2)}) copy-start(s32[1,128]{1,0:T(1,128)} %param.20) | copy-start | bytes 1540
  27.3 35.6 %copy-start.3 = (s32[1,128]{1,0:T(1,128)S(1)}, s32[1,128]{1,0:T(1,128)}, u32[]{:S(2)}) copy-start(s32[1,128]{1,0:T(1,128)} %param.21) | copy-start | bytes 1540
  27.3 35.6 %copy-start.4 = (s32[1,128]{1,0:T(1,128)S(1)}, s32[1,128]{1,0:T(1,128)}, u32[]{:S(2)}) copy-start(s32[1,128]{1,0:T(1,128)} %param.22) | copy-start | bytes 1540
  46.4 90.5 %all-to-all-start = ((bf16[32,1,32,256]{3,2,1,0:T(8,128)(2,1)}), bf16[32,1,32,256]{3,2,1,0:T(8,128)(2,1)S(1)}, u32[]{:S(2)}, u32[]{:S(2)}) async-start(bf16[32,1,32,256]{3,2,1,0:T(8,128)(2,1)} %broadcast_in_dim.40), calls=%async_computation | async-start | bytes 1048576 | tf_op jit(solution)/shard_map/all_to_all | solution.py:13
  136.9 104.4 %all-to-all-start.3 = ((bf16[32,32,256]{2,1,0:T(8,128)(2,1)}), bf16[32,32,256]{2,1,0:T(8,128)(2,1)S(1)}, u32[]{:S(2)}, u32[]{:S(2)}) async-start(bf16[32,32,256]{2,1,0:T(8,128)(2,1)} %bitcast.11), calls=%async_computation.3 | async-start | bytes 1048576 | tf_op jit(solution)/shard_map/all_to_all | solution.py:35
  241.3 15.9 %copy-start.6 = (bf16[1,32,256]{2,1,0:T(8,128)(2,1)S(1)}, bf16[1,32,256]{2,1,0:T(8,128)(2,1)}, u32[]{:S(2)}) copy-start(bf16[1,32,256]{2,1,0:T(8,128)(2,1)} %param.15) | copy-start | bytes 49156
  241.3 35.5 %copy-start.1 = (bf16[1,128,256]{2,1,0:T(8,128)(2,1)S(1)}, bf16[1,128,256]{2,1,0:T(8,128)(2,1)}, u32[]{:S(2)}) copy-start(bf16[1,128,256]{2,1,0:T(8,128)(2,1)} %param.14) | copy-start | bytes 196612
  241.3 35.4 %all-to-all-start.1 = ((bf16[16,128,256]{2,1,0:T(8,128)(2,1)}), bf16[16,128,256]{2,1,0:T(8,128)(2,1)S(1)}, u32[]{:S(2)}, u32[]{:S(2)}) async-start(bf16[16,128,256]{2,1,0:T(8,128)(2,1)} %convert_element_type.37), calls=%async_computation.1 | async-start | bytes 2097152 | tf_op jit(solution)/shard_map/all_to_all | solution.py:35
  257.0 299.9 %all-reduce.2.cloned.1.call-start = ((), (), s32[]{:S(2)}) async-start(), calls=%async_computation.4 | async-start | bytes 524288 | tf_op jit(solution)/shard_map/psum | solution.py:159
Sparse Core Ops, SparseCore 0:
  278.0 278.9 all-reduce.1
where the time goes:
time: 570 us; the launch traced here: 566 us
  waiting for transfers between devices  315 us (55%)
  other arithmetic  92.1 us (16%)
  starting transfers between devices  60.1 us (11%)
  local copies, waits for them, and re-layouts  45.3 us (8%)
  matrix products  37.6 us (7%)
  between operations  14.8 us (3%)
    psum x1, waiting for transfers between devices, per_device(): lax.psum(weight_part, ('au', 'ia')) / math.sqrt(user_count + item_count)  277 us
    scatter-add x14, other arithmetic, one_turn(): user_total = user_total.at[row_pick].add(forward * inverse)  46.2 us
    all_to_all x2, starting transfers between devices, summed_on_arrival(): lax.all_to_all(pieces, axis, split_axis=0, concat_axis=0, tiled=True)  32.7 us
    all_to_all x2, starting transfers between devices, from_everyone(): return lax.all_to_all(copies, axis, split_axis=0, concat_axis=0, tiled=True)  27.3 us
    gather x14, local copies, waits for them, and re-layouts, one_turn(): user_source[row_pick]  25.3 us
    select_n x28, other arithmetic, one_turn(): jnp.where(live_mask, 1.0 / norm_pick.astype(jnp.float32), 0.0)  20.3 us
    all_to_all x2, waiting for transfers between devices, summed_on_arrival(): lax.all_to_all(pieces, axis, split_axis=0, concat_axis=0, tiled=True)  19.2 us
    scatter-add x14, other arithmetic, one_turn(): item_total = item_total.at[col_pick].add(backward * inverse)  18.6 us
  transfers between devices with their start and end apart: 5, of which 3 were waited for; matrix products, arithmetic and copies ran while one was open for 30% of the time, Pallas kernels for 0%

commit v1 on v0

v1 whole, which is shorter than its diff:
```python
import math

import jax
import jax.numpy as jnp
from jax import lax
from jax.experimental import pallas as pl
from jax.experimental.pallas import tpu as pltpu
from jax.sharding import PartitionSpec as P

slot_block = 16
unroll = 4


def from_everyone(value, axis):
    copies = jnp.broadcast_to(value, (lax.axis_size(axis), *value.shape))
    return lax.all_to_all(copies, axis, split_axis=0, concat_axis=0, tiled=True)


def to_owners(value, axis):
    peers = lax.axis_size(axis)
    pieces = value.reshape(peers, value.shape[0] // peers, *value.shape[1:])
    return lax.all_to_all(pieces, axis, split_axis=0, concat_axis=0, tiled=True)


def summed(pieces):
    return pieces.astype(jnp.float32).sum(axis=0)


def dense_kernel(rows, cols, norms, count, tiles, dense, total):
    step = pl.program_id(0)
    edge = tiles.shape[1]
    user_tiles = dense.shape[0] // edge
    item_tiles = dense.shape[1] // edge

    @pl.when(step == 0)
    def clear():
        def clear_one(index, carry):
            total[index] = jnp.zeros((edge, edge), jnp.float32)
            return carry

        lax.fori_loop(0, total.shape[0], clear_one, 0)

    first = step * slot_block
    live = jnp.clip(count[0] - first, 0, slot_block)

    def add_group(group, carry):
        for lane in range(unroll):
            local = group * unroll + lane
            slot = first + local
            place = rows[slot] * item_tiles + cols[slot]
            norm = jnp.full((8, edge), norms[slot], jnp.int32).astype(jnp.float32)
            scale = jnp.where(slot < count[0], 1.0 / norm, 0.0)
            term = tiles[local].astype(jnp.float32).reshape(edge // 8, 8, edge) * scale[None]
            total[place] = total[place] + term.reshape(edge, edge)
        return carry

    lax.fori_loop(0, (live + unroll - 1) // unroll, add_group, 0)

    @pl.when(step == pl.num_programs(0) - 1)
    def finish():
        def finish_row(row, carry):
            start = pl.multiple_of(row * edge, edge)
            for col in range(item_tiles):
                dense[pl.ds(start, edge), col * edge : (col + 1) * edge] = total[
                    row * item_tiles + col
                ].astype(jnp.bfloat16)
            return carry

        lax.fori_loop(0, user_tiles, finish_row, 0)


def dense_block(tile_block, row_ids, col_ids, norm_ids, count, user_rows, item_rows):
    slots, edge, _ = tile_block.shape
    positions = (user_rows // edge) * (item_rows // edge)
    return pl.pallas_call(
        dense_kernel,
        out_shape=jax.ShapeDtypeStruct((user_rows, item_rows), jnp.bfloat16),
        grid_spec=pltpu.PrefetchScalarGridSpec(
            num_scalar_prefetch=4,
            grid=(slots // slot_block,),
            in_specs=[pl.BlockSpec((slot_block, edge, edge), lambda i, *_: (i, 0, 0))],
            out_specs=pl.BlockSpec((user_rows, item_rows), lambda i, *_: (0, 0)),
            scratch_shapes=[pltpu.VMEM((positions, edge, edge), jnp.float32)],
        ),
        compiler_params=pltpu.CompilerParams(
            dimension_semantics=("arbitrary",), vmem_limit_bytes=40 << 20
        ),
        cost_estimate=pl.CostEstimate(
            flops=4 * slots * edge * edge,
            bytes_accessed=2 * slots * edge * edge + 2 * user_rows * item_rows,
            transcendentals=0,
        ),
        name="dense_block",
    )(row_ids, col_ids, norm_ids, count, tile_block)


def block_product(embedded, total):
    return jnp.einsum(
        "rd,re->de", embedded.astype(jnp.float32), total, precision=lax.Precision.HIGHEST
    )


def per_device(
    user_emb,
    item_emb,
    weight,
    grad_user,
    grad_item,
    tile_values,
    tile_rows,
    tile_cols,
    tile_norm,
    tile_count,
):
    width = weight.shape[0]
    user_rows = user_emb.shape[1] * lax.axis_size("ia")
    item_rows = item_emb.shape[1] * lax.axis_size("au")
    low = jnp.bfloat16
    users = from_everyone(grad_user[0], "ia").reshape(user_rows, width)
    items = from_everyone(grad_item[0], "au").reshape(item_rows, width)
    dense = dense_block(
        tile_values[0],
        tile_rows[0],
        tile_cols[0],
        tile_norm[0],
        tile_count[0],
        user_rows,
        item_rows,
    )
    user_part = jnp.einsum("ui,id->ud", dense, items, preferred_element_type=jnp.float32)
    item_part = jnp.einsum("ui,ud->id", dense, users, preferred_element_type=jnp.float32)
    q_user = summed(to_owners(user_part.astype(low), "ia"))
    q_item = summed(to_owners(item_part.astype(low), "au"))
    weight_part = block_product(user_emb[0], q_user) + block_product(item_emb[0], q_item)
    strip = summed(to_owners(weight_part.astype(low), "ia"))
    strip = summed(from_everyone(strip.astype(low), "au"))
    user_count = user_rows * lax.axis_size("au")
    item_count = item_rows * lax.axis_size("ia")
    strip = strip / math.sqrt(user_count + item_count)
    grad_weight = from_everyone(strip, "ia").reshape(width, width)
    grad_user_emb = jnp.einsum(
        "re,de->rd", q_user.astype(low), weight, preferred_element_type=jnp.float32
    ).astype(low)
    grad_item_emb = jnp.einsum(
        "re,de->rd", q_item.astype(low), weight, preferred_element_type=jnp.float32
    ).astype(low)
    return (grad_user_emb[None], grad_item_emb[None], grad_weight)


def solution(mesh):
    return jax.shard_map(
        per_device,
        mesh=mesh,
        in_specs=(
            P("au", "ia", None),
            P("ia", "au", None),
            P(),
            P("au", "ia", None),
            P("ia", "au", None),
            P("au", "ia", None, None),
            P("au", "ia"),
            P("au", "ia"),
            P("au", "ia"),
            P("au", "ia"),
        ),
        out_specs=(P("au", "ia", None), P("ia", "au", None), P()),
        check_vma=False,
    )
```

time: 570 us -> 181 us (0.32)
  waiting for transfers between devices: 315 us -> 46.6 us
  other arithmetic: 92.1 us -> 0.3 us
  blocking collectives: 0 us -> 74.7 us
  local copies, waits for them, and re-layouts: 45.3 us -> 8.16 us
  matrix products: 37.6 us -> 8.84 us
  starting transfers between devices: 60.1 us -> 35.5 us
  between operations: 14.8 us -> 1.46 us
    psum x1 -> x0, waiting for transfers between devices: 277 us -> none  [per_device(): lax.psum(weight_part, ('au', 'ia')) / math.sqrt(user_count + item_count)]
    all_to_all x0 -> x3, blocking collectives: none -> 74.7 us  [the longest x2 55 us: from_everyone(): return lax.all_to_all(copies, axis, split_axis=0, concat_axis=0, tiled=True)]
    scatter-add x28 -> x0, other arithmetic: 64.7 us -> none  [the longest x14 46.2 us: one_turn(): user_total = user_total.at[row_pick].add(forward * inverse)]
    gather x28 -> x0, local copies, waits for them, and re-layouts: 33.5 us -> none  [the longest x14 25.3 us: one_turn(): user_source[row_pick]]
    dot_general x30 -> x4, matrix products: 36.2 us -> 8.22 us  [the longest x1 4.46 us: per_device(): jnp.einsum('ui,id->ud', dense, items, preferred_element_type=jnp.float32)]
    select_n x56 -> x0, other arithmetic: 22.4 us -> none  [the longest x28 20.3 us: one_turn(): jnp.where(live_mask, 1.0 / norm_pick.astype(jnp.float32), 0.0)]
    all_to_all x2, starting transfers between devices: 32.7 us -> 13.1 us  [to_owners(): return lax.all_to_all(pieces, axis, split_axis=0, concat_axis=0, tiled=True)]
    all_to_all x2, waiting for transfers between devices: 19.2 us -> 32 us  [to_owners(): return lax.all_to_all(pieces, axis, split_axis=0, concat_axis=0, tiled=True)]
  transfers between devices with their start and end apart: 5 -> 4, of which waited for: 3 -> 4; matrix products, arithmetic and copies ran while one was open for 30% -> 5% of each run, Pallas kernels for 0% -> 2%
where the time goes in v1:
time: 181 us; the launch traced here: 179 us
  blocking collectives  74.7 us (41%)
  waiting for transfers between devices  46.6 us (26%)
  starting transfers between devices  35.5 us (20%)
  matrix products  8.84 us (5%)
  local copies, waits for them, and re-layouts  8.16 us (5%)
  Pallas kernels  3.19 us (2%)
    all_to_all x2, blocking collectives, from_everyone(): return lax.all_to_all(copies, axis, split_axis=0, concat_axis=0, tiled=True)  55 us
    all_to_all x2, waiting for transfers between devices, to_owners(): return lax.all_to_all(pieces, axis, split_axis=0, concat_axis=0, tiled=True)  32 us
    all_to_all x2, starting transfers between devices, from_everyone(): return lax.all_to_all(copies, axis, split_axis=0, concat_axis=0, tiled=True)  22.4 us
    all_to_all x1, blocking collectives, to_owners(): return lax.all_to_all(pieces, axis, split_axis=0, concat_axis=0, tiled=True)  19.7 us
    all_to_all x2, waiting for transfers between devices, from_everyone(): return lax.all_to_all(copies, axis, split_axis=0, concat_axis=0, tiled=True)  14.6 us
    all_to_all x2, starting transfers between devices, to_owners(): return lax.all_to_all(pieces, axis, split_axis=0, concat_axis=0, tiled=True)  13.1 us
    unnamed x17, local copies, waits for them, and re-layouts  4.85 us
    dot_general x1, matrix products, per_device(): jnp.einsum('ui,id->ud', dense, items, preferred_element_type=jnp.float32)  4.46 us
  transfers between devices with their start and end apart: 4, of which 4 were waited for; matrix products, arithmetic and copies ran while one was open for 5% of the time, Pallas kernels for 2%

profile of v1, /device:TPU:1, one launch (start us, length us, event | category | flops | bytes accessed | tf_op | source)
XLA Modules:
  0.0 178.7 jit_solution(15164820414656418104)
XLA Ops:
  0.6 0.0 copy-start
  0.6 0.0 copy-start.5
  0.7 0.0 copy-start.4
  0.7 0.0 copy-start.3
  0.7 1.0 broadcast_in_dim.20
  1.6 35.7 %all_to_all.35 = bf16[16,128,256]{2,1,0:T(8,128)(2,1)S(1)} all-to-all(bf16[16,128,256]{2,1,0:T(8,128)(2,1)S(1)} %broadcast_in_dim.20), channel_id=1, replica_groups=mesh['au'=32,'ia'=16] {'ia'}, dimensions={0} | all-to-all | bytes 2097152 | tf_op jit(solution)/shard_map/all_to_all | solution.py:16
  37.4 1.6 broadcast_in_dim.18
  39.0 16.6 %all-to-all-start = ((bf16[32,32,256]{2,1,0:T(8,128)(2,1)}), bf16[32,32,256]{2,1,0:T(8,128)(2,1)S(1)}, u32[]{:S(2)}, u32[]{:S(2)}) async-start(bf16[32,32,256]{2,1,0:T(8,128)(2,1)} %broadcast_in_dim.18), calls=%async_computation | async-start | bytes 1048576 | tf_op jit(solution)/shard_map/all_to_all | solution.py:16
  56.3 0.0 copy-done.5
  56.3 0.0 copy-done.4
  56.3 0.0 copy-done.3
  56.3 0.0 copy-start.1
  56.3 2.2 %copy-done.1 = bf16[1,128,128,128]{3,2,1,0:T(8,128)(2,1)S(1)} copy-done((bf16[1,128,128,128]{3,2,1,0:T(8,128)(2,1)S(1)}, bf16[1,128,128,128]{3,2,1,0:T(8,128)(2,1)}, u32[]{:S(2)}) %copy-start.1) | copy-done | bytes 4194328
  58.5 3.2 %dense_block.1 = bf16[2048,1024]{1,0:T(8,128)(2,1)S(1)} custom-call(s32[128]{0:T(128)S(1)} %bitcast.35, s32[128]{0:T(128)S(1)} %bitcast.36, s32[128]{0:T(128)S(1)} %bitcast.37, s32[1]{0:T(128)} %bitcast.33.count, bf16[128,128,128]{2,1,0:T(8,128)(2,1)S(1)} %bitcast.34), custom_call_target="tpu_custom_call" | custom-call | flops 8388608 | bytes 8388608 | tf_op jit(solution)/shard_map/dense_block/pallas_call | solution.py:75
  61.7 0.0 copy-start.2
  61.7 1.9 %copy-done.2 = bf16[2048,1024]{1,0:T(8,128)(2,1)} copy-done((bf16[2048,1024]{1,0:T(8,128)(2,1)}, bf16[2048,1024]{1,0:T(8,128)(2,1)S(1)}, u32[]{:S(2)}) %copy-start.2) | copy-done | bytes 4194328
  63.6 2.1 %convolution_convert_fusion.1 = bf16[1024,256]{1,0:T(8,128)(2,1)} fusion(bf16[2048,1024]{1,0:T(8,128)(2,1)S(1)} %dense_block.1, bf16[2048,256]{1,0:T(8,128)(2,1)S(1)} %bitcast.38), kind=kOutput, calls=%fused_computation.2 | convolution fusion | flops 1074003968 | bytes 5767168 | tf_op jit(solution)/shard_map/ui,ud->id/dot_general | solution.py:131
  65.8 5.0 %all-to-all-done = bf16[32,32,256]{2,1,0:T(8,128)(2,1)S(1)} async-done(((bf16[32,32,256]{2,1,0:T(8,128)(2,1)}), bf16[32,32,256]{2,1,0:T(8,128)(2,1)S(1)}, u32[]{:S(2)}, u32[]{:S(2)}) %all-to-all-start) | async-done | bytes 524320 | tf_op jit(solution)/shard_map/all_to_all | solution.py:16
  70.8 6.7 %all-to-all-start.3 = ((bf16[32,32,256]{2,1,0:T(8,128)(2,1)}), bf16[32,32,256]{2,1,0:T(8,128)(2,1)S(1)}, u32[]{:S(2)}, u32[]{:S(2)}) async-start(bf16[32,32,256]{2,1,0:T(8,128)(2,1)} %bitcast.11), calls=%async_computation.3 | async-start | bytes 1048576 | tf_op jit(solution)/shard_map/all_to_all | solution.py:22
  77.5 0.0 copy-start.7
  77.5 0.0 copy-start.6
  77.5 4.5 %convolution_convert_fusion = bf16[2048,256]{1,0:T(8,128)(2,1)} fusion(bf16[2048,1024]{1,0:T(8,128)(2,1)} %copy-done.2, bf16[1024,256]{1,0:T(8,128)(2,1)S(1)} %bitcast.40), kind=kOutput, calls=%fused_computation | convolution fusion | flops 1074266112 | bytes 5767168 | tf_op jit(solution)/shard_map/ui,id->ud/dot_general | solution.py:130
  81.9 10.7 %all-to-all-done.3 = bf16[32,32,256]{2,1,0:T(8,128)(2,1)S(1)} async-done(((bf16[32,32,256]{2,1,0:T(8,128)(2,1)}), bf16[32,32,256]{2,1,0:T(8,128)(2,1)S(1)}, u32[]{:S(2)}, u32[]{:S(2)}) %all-to-all-start.3) | async-done | bytes 524320 | tf_op jit(solution)/shard_map/all_to_all | solution.py:22
  92.6 6.4 %all-to-all-start.1 = ((bf16[16,128,256]{2,1,0:T(8,128)(2,1)}), bf16[16,128,256]{2,1,0:T(8,128)(2,1)S(1)}, u32[]{:S(2)}, u32[]{:S(2)}) async-start(bf16[16,128,256]{2,1,0:T(8,128)(2,1)} %bitcast.7), calls=%async_computation.1 | async-start | bytes 2097152 | tf_op jit(solution)/shard_map/all_to_all | solution.py:22
  99.1 0.1 convert_reduce_fusion.1
  99.1 0.0 copy-done.7
  99.1 0.3 fusion.5
  99.5 21.3 %all-to-all-done.1 = bf16[16,128,256]{2,1,0:T(8,128)(2,1)S(1)} async-done(((bf16[16,128,256]{2,1,0:T(8,128)(2,1)}), bf16[16,128,256]{2,1,0:T(8,128)(2,1)S(1)}, u32[]{:S(2)}, u32[]{:S(2)}) %all-to-all-start.1) | async-done | bytes 1048608 | tf_op jit(solution)/shard_map/all_to_all | solution.py:22
  120.8 0.1 convert_reduce_fusion
  120.9 0.0 copy-done.6
  120.9 0.3 fusion
  121.3 19.7 %all_to_all.36 = bf16[16,16,256]{2,1,0:T(8,128)(2,1)S(1)} all-to-all(bf16[16,16,256]{2,1,0:T(8,128)(2,1)S(1)} %bitcast.41), channel_id=1, replica_groups=mesh['au'=32,'ia'=16] {'ia'}, dimensions={0} | all-to-all | bytes 262144 | tf_op jit(solution)/shard_map/all_to_all | solution.py:22
  141.0 19.3 %all_to_all.37 = bf16[32,16,256]{2,1,0:T(8,128)(2,1)S(1)} all-to-all(bf16[32,16,256]{2,1,0:T(8,128)(2,1)S(1)} %broadcast_in_dim.22), channel_id=1, replica_groups=mesh['au'=32,'ia'=16] {'au'}, dimensions={0} | all-to-all | bytes 524288 | tf_op jit(solution)/shard_map/all_to_all | solution.py:16
  160.4 0.7 broadcast_in_dim.23
  161.1 5.7 %all-to-all-start.6 = ((f32[16,16,256]{2,1,0:T(8,128)}), f32[16,16,256]{2,1,0:T(8,128)S(1)}, u32[]{:S(2)}, u32[]{:S(2)}) async-start(f32[16,16,256]{2,1,0:T(8,128)} %broadcast_in_dim.23), calls=%async_computation.6 | async-start | bytes 524288 | tf_op jit(solution)/shard_map/all_to_all | solution.py:16
  166.8 0.0 copy-done
  166.8 0.8 fusion.2
  167.6 0.8 fusion.1
  168.4 9.6 %all-to-all-done.6 = f32[16,16,256]{2,1,0:T(8,128)S(1)} async-done(((f32[16,16,256]{2,1,0:T(8,128)}), f32[16,16,256]{2,1,0:T(8,128)S(1)}, u32[]{:S(2)}, u32[]{:S(2)}) %all-to-all-start.6) | async-done | bytes 262176 | tf_op jit(solution)/shard_map/all_to_all | solution.py:16
  178.0 0.7 copy.15
  (4 shorter events, 0.1 us)
Async XLA Ops:
  0.6 166.2 %copy-start = (bf16[256,256]{1,0:T(8,128)(2,1)S(1)}, bf16[256,256]{1,0:T(8,128)(2,1)}, u32[]{:S(2)}) copy-start(bf16[256,256]{1,0:T(8,128)(2,1)} %param.12) | copy-start | bytes 393220
  0.6 55.6 %copy-start.5 = (s32[1,128]{1,0:T(1,128)S(1)}, s32[1,128]{1,0:T(1,128)}, u32[]{:S(2)}) copy-start(s32[1,128]{1,0:T(1,128)} %param.18) | copy-start | bytes 1540
  0.7 55.6 %copy-start.4 = (s32[1,128]{1,0:T(1,128)S(1)}, s32[1,128]{1,0:T(1,128)}, u32[]{:S(2)}) copy-start(s32[1,128]{1,0:T(1,128)} %param.17) | copy-start | bytes 1540
  0.7 55.6 %copy-start.3 = (s32[1,128]{1,0:T(1,128)S(1)}, s32[1,128]{1,0:T(1,128)}, u32[]{:S(2)}) copy-start(s32[1,128]{1,0:T(1,128)} %param.16) | copy-start | bytes 1540
  39.0 31.8 %all-to-all-start = ((bf16[32,32,256]{2,1,0:T(8,128)(2,1)}), bf16[32,32,256]{2,1,0:T(8,128)(2,1)S(1)}, u32[]{:S(2)}, u32[]{:S(2)}) async-start(bf16[32,32,256]{2,1,0:T(8,128)(2,1)} %broadcast_in_dim.18), calls=%async_computation | async-start | bytes 1048576 | tf_op jit(solution)/shard_map/all_to_all | solution.py:16
  56.3 2.2 %copy-start.1 = (bf16[1,128,128,128]{3,2,1,0:T(8,128)(2,1)S(1)}, bf16[1,128,128,128]{3,2,1,0:T(8,128)(2,1)}, u32[]{:S(2)}) copy-start(bf16[1,128,128,128]{3,2,1,0:T(8,128)(2,1)} %param.15) | copy-start | bytes 12582916
  61.7 1.9 %copy-start.2 = (bf16[2048,1024]{1,0:T(8,128)(2,1)}, bf16[2048,1024]{1,0:T(8,128)(2,1)S(1)}, u32[]{:S(2)}) copy-start(bf16[2048,1024]{1,0:T(8,128)(2,1)S(1)} %dense_block.1) | copy-start | bytes 12582916
  70.8 21.8 %all-to-all-start.3 = ((bf16[32,32,256]{2,1,0:T(8,128)(2,1)}), bf16[32,32,256]{2,1,0:T(8,128)(2,1)S(1)}, u32[]{:S(2)}, u32[]{:S(2)}) async-start(bf16[32,32,256]{2,1,0:T(8,128)(2,1)} %bitcast.11), calls=%async_computation.3 | async-start | bytes 1048576 | tf_op jit(solution)/shard_map/all_to_all | solution.py:22
  77.5 21.7 %copy-start.7 = (bf16[1,32,256]{2,1,0:T(8,128)(2,1)S(1)}, bf16[1,32,256]{2,1,0:T(8,128)(2,1)}, u32[]{:S(2)}) copy-start(bf16[1,32,256]{2,1,0:T(8,128)(2,1)} %param.11) | copy-start | bytes 49156
  77.5 43.5 %copy-start.6 = (bf16[1,128,256]{2,1,0:T(8,128)(2,1)S(1)}, bf16[1,128,256]{2,1,0:T(8,128)(2,1)}, u32[]{:S(2)}) copy-start(bf16[1,128,256]{2,1,0:T(8,128)(2,1)} %param.10) | copy-start | bytes 196612
  92.6 28.2 %all-to-all-start.1 = ((bf16[16,128,256]{2,1,0:T(8,128)(2,1)}), bf16[16,128,256]{2,1,0:T(8,128)(2,1)S(1)}, u32[]{:S(2)}, u32[]{:S(2)}) async-start(bf16[16,128,256]{2,1,0:T(8,128)(2,1)} %bitcast.7), calls=%async_computation.1 | async-start | bytes 2097152 | tf_op jit(solution)/shard_map/all_to_all | solution.py:22
  161.1 16.9 %all-to-all-start.6 = ((f32[16,16,256]{2,1,0:T(8,128)}), f32[16,16,256]{2,1,0:T(8,128)S(1)}, u32[]{:S(2)}, u32[]{:S(2)}) async-start(f32[16,16,256]{2,1,0:T(8,128)} %broadcast_in_dim.23), calls=%async_computation.6 | async-start | bytes 524288 | tf_op jit(solution)/shard_map/all_to_all | solution.py:16

commit v2 on v1

--- a/solution.py
+++ b/solution.py
@@ -9,6 +9,9 @@
 
 slot_block = 16
 unroll = 4
+core_bit = 1
+side_bit = 2
+ring_step = 4
 
 
 def from_everyone(value, axis):
@@ -22,15 +25,43 @@
     return lax.all_to_all(pieces, axis, split_axis=0, concat_axis=0, tiled=True)
 
 
+def partner(value, bit):
+    return lax.ppermute(value, "ia", [(i, i ^ bit) for i in range(lax.axis_size("ia"))])
+
+
+def ahead(index, distance):
+    ring = lax.axis_size("ia") // ring_step
+    return (index // ring_step + distance) % ring * ring_step + index % ring_step
+
+
+def from_ahead(value, distance):
+    size = lax.axis_size("ia")
+    return lax.ppermute(value, "ia", [(ahead(i, distance), i) for i in range(size)])
+
+
+def send_ahead(value, distance):
+    size = lax.axis_size("ia")
+    return lax.ppermute(value, "ia", [(i, ahead(i, distance)) for i in range(size)])
+
+
+def relative_rows(row_ids):
+    ring = lax.axis_size("ia") // ring_step
+    here = lax.axis_index("ia").astype(jnp.int32)
+    core = (row_ids ^ here) & 1
+    side = ((row_ids ^ here) >> 1) & 1
+    along = ((row_ids >> 2) - (here >> 2)) & (ring - 1)
+    return core * (2 * ring) + along * 2 + side
+
+
 def summed(pieces):
     return pieces.astype(jnp.float32).sum(axis=0)
 
 
-def dense_kernel(rows, cols, norms, count, tiles, dense, total):
+def dense_kernel(rows, cols, norms, count, tiles, near, far, total):
     step = pl.program_id(0)
     edge = tiles.shape[1]
-    user_tiles = dense.shape[0] // edge
-    item_tiles = dense.shape[1] // edge
+    half_tiles = near.shape[0] // edge
+    item_tiles = near.shape[1] // edge
 
     @pl.when(step == 0)
     def clear():
@@ -60,13 +91,15 @@
     def finish():
         def finish_row(row, carry):
             start = pl.multiple_of(row * edge, edge)
-            for col in range(item_tiles):
-                dense[pl.ds(start, edge), col * edge : (col + 1) * edge] = total[
-                    row * item_tiles + col
-                ].astype(jnp.bfloat16)
+            for half, dense in enumerate((near, far)):
+                for col in range(item_tiles):
+                    place = (half * half_tiles + row) * item_tiles + col
+                    dense[pl.ds(start, edge), col * edge : (col + 1) * edge] = total[
+                        place
+                    ].astype(jnp.bfloat16)
             return carry
 
-        lax.fori_loop(0, user_tiles, finish_row, 0)
+        lax.fori_loop(0, half_tiles, finish_row, 0)
 
 
 def dense_block(tile_block, row_ids, col_ids, norm_ids, count, user_rows, item_rows):
@@ -74,12 +107,12 @@
     positions = (user_rows // edge) * (item_rows // edge)
     return pl.pallas_call(
         dense_kernel,
-        out_shape=jax.ShapeDtypeStruct((user_rows, item_rows), jnp.bfloat16),
+        out_shape=[jax.ShapeDtypeStruct((user_rows // 2, item_rows), jnp.bfloat16)] * 2,
         grid_spec=pltpu.PrefetchScalarGridSpec(
             num_scalar_prefetch=4,
             grid=(slots // slot_block,),
             in_specs=[pl.BlockSpec((slot_block, edge, edge), lambda i, *_: (i, 0, 0))],
-            out_specs=pl.BlockSpec((user_rows, item_rows), lambda i, *_: (0, 0)),
+            out_specs=[pl.BlockSpec((user_rows // 2, item_rows), lambda i, *_: (0, 0))] * 2,
             scratch_shapes=[pltpu.VMEM((positions, edge, edge), jnp.float32)],
         ),
         compiler_params=pltpu.CompilerParams(
@@ -94,10 +127,12 @@
     )(row_ids, col_ids, norm_ids, count, tile_block)
 
 
-def block_product(embedded, total):
-    return jnp.einsum(
-        "rd,re->de", embedded.astype(jnp.float32), total, precision=lax.Precision.HIGHEST
-    )
+def product(spec, left, right):
+    return jnp.einsum(spec, left, right, preferred_element_type=jnp.float32)
+
+
+def wide(value):
+    return value.astype(jnp.float32)
 
 
 def per_device(
@@ -116,34 +151,64 @@
     user_rows = user_emb.shape[1] * lax.axis_size("ia")
     item_rows = item_emb.shape[1] * lax.axis_size("au")
     low = jnp.bfloat16
-    users = from_everyone(grad_user[0], "ia").reshape(user_rows, width)
-    items = from_everyone(grad_item[0], "au").reshape(item_rows, width)
-    dense = dense_block(
+    ring = lax.axis_size("ia") // ring_step
+
+    mine = jnp.stack([grad_user[0], user_emb[0]])
+    pair = jnp.stack([mine, partner(mine, side_bit)], axis=1)
+    near = jnp.concatenate([pair] + [from_ahead(pair, d) for d in range(1, ring)], axis=1)
+    near = near.reshape(2, user_rows // 2, width)
+    far = partner(near, core_bit)
+
+    item_pieces = from_everyone(jnp.stack([grad_item[0], item_emb[0]]), "au")
+    items = item_pieces[:, 0].reshape(item_rows, width)
+    item_table = item_pieces[:, 1].reshape(item_rows, width)
+
+    dense_near, dense_far = dense_block(
         tile_values[0],
-        tile_rows[0],
+        relative_rows(tile_rows[0]),
         tile_cols[0],
         tile_norm[0],
         tile_count[0],
         user_rows,
         item_rows,
     )
-    user_part = jnp.einsum("ui,id->ud", dense, items, preferred_element_type=jnp.float32)
-    item_part = jnp.einsum("ui,ud->id", dense, users, preferred_element_type=jnp.float32)
-    q_user = summed(to_owners(user_part.astype(low), "ia"))
-    q_item = summed(to_owners(item_part.astype(low), "au"))
-    weight_part = block_product(user_emb[0], q_user) + block_product(item_emb[0], q_item)
-    strip = summed(to_owners(weight_part.astype(low), "ia"))
-    strip = summed(from_everyone(strip.astype(low), "au"))
+    user_far = product("ui,id->ud", dense_far, items).astype(low)
+    user_near = product("ui,id->ud", dense_near, items).astype(low)
+    item_part = product("ui,ud->id", dense_near, near[0]) + product(
+        "ui,ud->id", dense_far, far[0]
+    )
+    item_part = item_part.astype(low)
+    weight_part = (
+        product("rd,re->de", near[1], user_near)
+        + product("rd,re->de", far[1], user_far)
+        + product("rd,re->de", item_table, item_part)
+    )
+
+    peers = lax.axis_size("au")
+    pieces = jnp.concatenate(
+        [
+            item_part.reshape(peers, item_rows // peers, width),
+            weight_part.astype(low).reshape(peers, width // peers, width),
+        ],
+        axis=1,
+    )
+    arrived = summed(lax.all_to_all(pieces, "au", split_axis=0, concat_axis=0, tiled=True))
+    q_item = arrived[: item_rows // peers]
+    strip = summed(from_everyone(arrived[item_rows // peers :].astype(low), "ia"))
     user_count = user_rows * lax.axis_size("au")
     item_count = item_rows * lax.axis_size("ia")
     strip = strip / math.sqrt(user_count + item_count)
-    grad_weight = from_everyone(strip, "ia").reshape(width, width)
-    grad_user_emb = jnp.einsum(
-        "re,de->rd", q_user.astype(low), weight, preferred_element_type=jnp.float32
-    ).astype(low)
-    grad_item_emb = jnp.einsum(
-        "re,de->rd", q_item.astype(low), weight, preferred_element_type=jnp.float32
-    ).astype(low)
+    grad_weight = wide(from_everyone(strip.astype(low), "au")).reshape(width, width)
+
+    along = wide(user_near) + wide(partner(user_far, core_bit))
+    along = along.reshape(ring, user_rows // (2 * ring), width)
+    sent = along.astype(low)
+    both = along[0] + sum(wide(send_ahead(sent[d], d)) for d in range(1, ring))
+    own_rows = user_emb.shape[1]
+    q_user = both[:own_rows] + wide(partner(both[own_rows:].astype(low), side_bit))
+
+    grad_user_emb = product("re,de->rd", q_user.astype(low), weight).astype(low)
+    grad_item_emb = product("re,de->rd", q_item.astype(low), weight).astype(low)
     return (grad_user_emb[None], grad_item_emb[None], grad_weight)
 
 

time: 181 us -> 133 us (0.73)
  blocking collectives: 74.7 us -> 0 us
  starting transfers between devices: 35.5 us -> 70.4 us
  waiting for transfers between devices: 46.6 us -> 30 us
  local copies, waits for them, and re-layouts: 8.16 us -> 14.6 us
  other arithmetic: 0.3 us -> 2.57 us
    all_to_all x3 -> x0, blocking collectives: 74.7 us -> none  [the longest x2 55 us: from_everyone(): return lax.all_to_all(copies, axis, split_axis=0, concat_axis=0, tiled=True)]
    ppermute x0 -> x10, starting transfers between devices: none -> 37.7 us  [the longest x4 20 us: partner(): lax.ppermute(value, 'ia', [(i, i ^ bit) for i in range(lax.axis_size('ia'...]
    all_to_all x2 -> x1, waiting for transfers between devices: 32 us -> 9.42 us  [per_device(): lax.all_to_all(pieces, 'au', split_axis=0, concat_axis=0, tiled=True)]
    ppermute x0 -> x10, waiting for transfers between devices: none -> 9.88 us  [the longest x3 9.86 us: from_ahead(): lax.ppermute(value, 'ia', [(ahead(i, distance), i) for i in range(size)])]
    all_to_all x2 -> x3, waiting for transfers between devices: 14.6 us -> 10.7 us  [from_everyone(): return lax.all_to_all(copies, axis, split_axis=0, concat_axis=0, tiled=True)]
    all_to_all x2 -> x1, starting transfers between devices: 13.1 us -> 9.54 us  [per_device(): lax.all_to_all(pieces, 'au', split_axis=0, concat_axis=0, tiled=True)]
    slice x0 -> x5, local copies, waits for them, and re-layouts: none -> 3.14 us  [the longest x1 3.03 us: per_device(): near[1]]
    unnamed x17 -> x27, local copies, waits for them, and re-layouts: 4.85 us -> 7.45 us
  transfers between devices with their start and end apart: 4 -> 14, of which waited for: 4 -> 5; matrix products, arithmetic and copies ran while one was open for 5% -> 13% of each run, Pallas kernels for 2% -> 3%
where the time goes in v2:
time: 133 us; the launch traced here: 132 us
  starting transfers between devices  70.4 us (53%)
  waiting for transfers between devices  30 us (23%)
  local copies, waits for them, and re-layouts  14.6 us (11%)
  matrix products  9.49 us (7%)
  Pallas kernels  3.68 us (3%)
  other arithmetic  2.57 us (2%)
  between operations  1.63 us (1%)
    all_to_all x3, starting transfers between devices, from_everyone(): return lax.all_to_all(copies, axis, split_axis=0, concat_axis=0, tiled=True)  23.1 us
    ppermute x4, starting transfers between devices, partner(): lax.ppermute(value, 'ia', [(i, i ^ bit) for i in range(lax.axis_size('ia'...  20 us
    all_to_all x3, waiting for transfers between devices, from_everyone(): return lax.all_to_all(copies, axis, split_axis=0, concat_axis=0, tiled=True)  10.7 us
    ppermute x3, waiting for transfers between devices, from_ahead(): lax.ppermute(value, 'ia', [(ahead(i, distance), i) for i in range(size)])  9.86 us
    all_to_all x1, starting transfers between devices, per_device(): lax.all_to_all(pieces, 'au', split_axis=0, concat_axis=0, tiled=True)  9.54 us
    dot_general x9, matrix products, product(): return jnp.einsum(spec, left, right, preferred_element_type=jnp.float32)  9.49 us
    all_to_all x1, waiting for transfers between devices, per_device(): lax.all_to_all(pieces, 'au', split_axis=0, concat_axis=0, tiled=True)  9.42 us
    ppermute x3, starting transfers between devices, from_ahead(): lax.ppermute(value, 'ia', [(ahead(i, distance), i) for i in range(size)])  9.32 us
  transfers between devices with their start and end apart: 14, of which 5 were waited for; matrix products, arithmetic and copies ran while one was open for 13% of the time, Pallas kernels for 3%

profile of v2, /device:TPU:1, one launch (start us, length us, event | category | flops | bytes accessed | tf_op | source)
XLA Modules:
  0.0 132.3 jit_solution(16342240819189448517)
XLA Ops:
  0.6 0.9 constant_dynamic-update-slice_fusion.1
  1.5 0.8 constant_dynamic-update-slice_fusion
  2.4 8.3 %collective-permute-start.5 = (bf16[2,128,256]{2,1,0:T(8,128)(2,1)S(1)}, bf16[2,128,256]{2,1,0:T(8,128)(2,1)S(1)}, u32[]{:S(2)}, u32[]{:S(2)}) collective-permute-start(bf16[2,128,256]{2,1,0:T(8,128)(2,1)S(1)} %constant_dynamic-update-slice_fusion), channel_id=1, source_target_pairs={{0,2},{1,3},{2,0},{3,1},{4,6},{5,7},{6,4},{7,5},{8,10},{9,11},{10,... | collective-permute-start | bytes 393224 | tf_op jit(solution)/shard_map/ppermute | solution.py:29
  10.6 0.7 pad_maximum_fusion.2
  11.4 1.1 broadcast_in_dim.15
  12.5 10.9 %all-to-all-start = ((bf16[32,2,32,256]{3,2,1,0:T(8,128)(2,1)}), bf16[32,2,32,256]{3,2,1,0:T(8,128)(2,1)S(1)}, u32[]{:S(2)}, u32[]{:S(2)}) async-start(bf16[32,2,32,256]{3,2,1,0:T(8,128)(2,1)} %broadcast_in_dim.15), calls=%async_computation | async-start | bytes 2097152 | tf_op jit(solution)/shard_map/all_to_all | solution.py:19
  23.5 4.4 %collective-permute-start.6 = (bf16[2,2,128,256]{3,2,1,0:T(8,128)(2,1)S(1)}, bf16[2,2,128,256]{3,2,1,0:T(8,128)(2,1)S(1)}, u32[]{:S(2)}, u32[]{:S(2)}) collective-permute-start(bf16[2,2,128,256]{3,2,1,0:T(8,128)(2,1)S(1)} %pad_maximum_fusion.1), channel_id=1, source_target_pairs={{4,0},{5,1},{6,2},{7,3},{8,4},{9,5},{10,6},{11,7},{12,8},{13,9},{1... | collective-permute-start | bytes 786440 | tf_op jit(solution)/shard_map/ppermute | solution.py:39
  27.9 0.7 constant_dynamic-update-slice_fusion.6
  28.5 2.4 %collective-permute-start.7 = (bf16[2,2,128,256]{3,2,1,0:T(8,128)(2,1)S(1)}, bf16[2,2,128,256]{3,2,1,0:T(8,128)(2,1)S(1)}, u32[]{:S(2)}, u32[]{:S(2)}) collective-permute-start(bf16[2,2,128,256]{3,2,1,0:T(8,128)(2,1)S(1)} %pad_maximum_fusion.1), channel_id=1, source_target_pairs={{8,0},{9,1},{10,2},{11,3},{12,4},{13,5},{14,6},{15,7},{0,8},{1,9},... | collective-permute-start | bytes 786440 | tf_op jit(solution)/shard_map/ppermute | solution.py:39
  31.0 2.5 %collective-permute-start.8 = (bf16[2,2,128,256]{3,2,1,0:T(8,128)(2,1)S(1)}, bf16[2,2,128,256]{3,2,1,0:T(8,128)(2,1)S(1)}, u32[]{:S(2)}, u32[]{:S(2)}) collective-permute-start(bf16[2,2,128,256]{3,2,1,0:T(8,128)(2,1)S(1)} %pad_maximum_fusion.1), channel_id=1, source_target_pairs={{12,0},{13,1},{14,2},{15,3},{0,4},{1,5},{2,6},{3,7},{4,8},{5,9},{6... | collective-permute-start | bytes 786440 | tf_op jit(solution)/shard_map/ppermute | solution.py:39
  33.5 0.7 constant_dynamic-update-slice_fusion.5
  34.2 0.7 constant_dynamic-update-slice_fusion.4
  34.9 3.4 %collective-permute-done.7 = bf16[2,2,128,256]{3,2,1,0:T(8,128)(2,1)S(1)} collective-permute-done((bf16[2,2,128,256]{3,2,1,0:T(8,128)(2,1)S(1)}, bf16[2,2,128,256]{3,2,1,0:T(8,128)(2,1)S(1)}, u32[]{:S(2)}, u32[]{:S(2)}) %collective-permute-start.7) | collective-permute-done | bytes 262176 | tf_op jit(solution)/shard_map/ppermute | solution.py:39
  38.3 0.7 constant_dynamic-update-slice_fusion.3
  39.0 6.5 %collective-permute-done.8 = bf16[2,2,128,256]{3,2,1,0:T(8,128)(2,1)S(1)} collective-permute-done((bf16[2,2,128,256]{3,2,1,0:T(8,128)(2,1)S(1)}, bf16[2,2,128,256]{3,2,1,0:T(8,128)(2,1)S(1)}, u32[]{:S(2)}, u32[]{:S(2)}) %collective-permute-start.8) | collective-permute-done | bytes 262176 | tf_op jit(solution)/shard_map/ppermute | solution.py:39
  45.5 0.8 constant_dynamic-update-slice_fusion.2
  46.2 2.7 %collective-permute-start.9 = (bf16[2,1024,256]{2,1,0:T(8,128)(2,1)}, bf16[2,1024,256]{2,1,0:T(8,128)(2,1)}, u32[]{:S(2)}, u32[]{:S(2)}) collective-permute-start(bf16[2,1024,256]{2,1,0:T(8,128)(2,1)} %bitcast.12), channel_id=1, source_target_pairs={{0,1},{1,0},{2,3},{3,2},{4,5},{5,4},{6,7},{7,6},{8,9},{9,8},{10,11... | collective-permute-start | bytes 3145736 | tf_op jit(solution)/shard_map/ppermute | solution.py:29
  49.6 2.2 %copy-done.1 = bf16[1,128,128,128]{3,2,1,0:T(8,128)(2,1)S(1)} copy-done((bf16[1,128,128,128]{3,2,1,0:T(8,128)(2,1)S(1)}, bf16[1,128,128,128]{3,2,1,0:T(8,128)(2,1)}, u32[]{:S(2)}) %copy-start.1) | copy-done | bytes 4194328
  51.8 3.7 %dense_block.1 = (bf16[1024,1024]{1,0:T(8,128)(2,1)S(1)}, bf16[1024,1024]{1,0:T(8,128)(2,1)S(1)}) custom-call(s32[128]{0:T(128)S(1)} %add_bitcast_fusion.rows, s32[128]{0:T(128)S(1)} %bitcast.50, s32[128]{0:T(128)S(1)} %bitcast.51, s32[1]{0:T(128)} %bitcast.48.count, bf16[128,128,128]{2,1,0:T(8,128)(2,1)S(1)} %bitcast.49), custom_call_target="tpu_custom_call" | custom-call | flops 8388608 | bytes 8388608 | tf_op jit(solution)/shard_map/dense_block/pallas_call | solution.py:108
  55.5 3.0 %fusion.12 = (bf16[1,8,128,256]{3,2,1,0:T(8,128)(2,1)}, bf16[1,8,128,256]{3,2,1,0:T(8,128)(2,1)}) fusion(bf16[2,8,128,256]{3,2,1,0:T(8,128)(2,1)} %constant_dynamic-update-slice_fusion.2), kind=kLoop, calls=%fused_computation.37 | loop fusion | bytes 2097152 | tf_op jit(solution)/shard_map/slice | solution.py:182
  58.5 2.8 %fusion.7 = f32[1024,256]{1,0:T(8,128)} fusion(bf16[1024,1024]{1,0:T(8,128)(2,1)S(1)} %get-tuple-element.6, bf16[2,1024,256]{2,1,0:T(8,128)(2,1)} %collective-permute-done.9), kind=kOutput, calls=%fused_computation.17 | convolution fusion | flops 536870912 | bytes 3670016 | tf_op jit(solution)/shard_map/ui,ud->id/dot_general | solution.py:131
  61.4 0.1 fusion.13
  61.4 1.5 %copy-done.5 = bf16[1024,1024]{1,0:T(8,128)(2,1)S(1)} copy-done((bf16[1024,1024]{1,0:T(8,128)(2,1)S(1)}, bf16[1024,1024]{1,0:T(8,128)(2,1)}, u32[]{:S(2)}) %copy-start.5) | copy-done | bytes 2097176
  62.9 0.7 convolution_convert_fusion
  63.7 1.9 %collective-permute-start = (bf16[1024,256]{1,0:T(8,128)(2,1)S(1)}, bf16[1024,256]{1,0:T(8,128)(2,1)S(1)}, u32[]{:S(2)}, u32[]{:S(2)}) collective-permute-start(bf16[1024,256]{1,0:T(8,128)(2,1)S(1)} %convolution_convert_fusion), channel_id=1, source_target_pairs={{0,1},{1,0},{2,3},{3,2},{4,5},{5,4},{6,7},{7,6},{8,9},{9,8},{10,11... | collective-permute-start | bytes 1572872 | tf_op jit(solution)/shard_map/ppermute | solution.py:29
  65.6 0.8 fusion
  66.4 0.3 fusion.15
  66.7 1.4 %fusion.6 = f32[256,256]{1,0:T(8,128)S(1)} fusion(bf16[1024,256]{1,0:T(8,128)(2,1)S(1)} %convolution_convert_fusion, bf16[2,1024,256]{2,1,0:T(8,128)(2,1)} %collective-permute-done.9), kind=kOutput, calls=%fused_computation.15 | convolution fusion | flops 134217728 | bytes 1310720 | tf_op jit(solution)/shard_map/rd,re->de/dot_general | solution.py:131
  68.1 1.5 %fusion.11 = (bf16[1024,256]{1,0:T(8,128)(2,1)}, f32[1024,256]{1,0:T(8,128)S(1)}, bf16[1024,256]{1,0:T(8,128)(2,1)S(1)}) fusion(bf16[1024,256]{1,0:T(8,128)(2,1)S(1)} %collective-permute-done, bf16[1024,1024]{1,0:T(8,128)(2,1)S(1)} %get-tuple-element.5, bf16[1024,256]{1,0:T(8,128)(2,1)S(1)} %bitcast.53), kind=kOutput, calls=%fused_computation.36 | convolution fusion | flops 538181632 | bytes 5242880 | tf_op jit(solution)/shard_map/ui,id->ud/dot_general | solution.py:131
  69.7 0.3 fusion.3
  70.0 0.9 pad_maximum_fusion
  70.9 9.5 %all-to-all-start.1 = ((bf16[32,40,256]{2,1,0:T(8,128)(2,1)}), bf16[32,40,256]{2,1,0:T(8,128)(2,1)S(1)}, u32[]{:S(2)}, u32[]{:S(2)}) async-start(bf16[32,40,256]{2,1,0:T(8,128)(2,1)} %pad_maximum_fusion), calls=%async_computation.1 | async-start | bytes 1310720 | tf_op jit(solution)/shard_map/all_to_all | solution.py:195
  80.5 1.9 %collective-permute-start.1 = (bf16[256,256]{1,0:T(8,128)(2,1)S(1)}, bf16[256,256]{1,0:T(8,128)(2,1)S(1)}, u32[]{:S(2)}, u32[]{:S(2)}) collective-permute-start(bf16[256,256]{1,0:T(8,128)(2,1)S(1)} %get-tuple-element.13), channel_id=1, source_target_pairs={{0,4},{1,5},{2,6},{3,7},{4,8},{5,9},{6,10},{7,11},{8,12},{9,13},{1... | collective-permute-start | bytes 393224 | tf_op jit(solution)/shard_map/ppermute | solution.py:44
  82.4 3.2 %collective-permute-start.2 = (bf16[256,256]{1,0:T(8,128)(2,1)S(1)}, bf16[256,256]{1,0:T(8,128)(2,1)S(1)}, u32[]{:S(2)}, u32[]{:S(2)}) collective-permute-start(bf16[256,256]{1,0:T(8,128)(2,1)S(1)} %get-tuple-element.15), channel_id=1, source_target_pairs={{0,8},{1,9},{2,10},{3,11},{4,12},{5,13},{6,14},{7,15},{8,0},{9,1},... | collective-permute-start | bytes 393224 | tf_op jit(solution)/shard_map/ppermute | solution.py:44
  85.7 3.3 %collective-permute-start.3 = (bf16[256,256]{1,0:T(8,128)(2,1)S(1)}, bf16[256,256]{1,0:T(8,128)(2,1)S(1)}, u32[]{:S(2)}, u32[]{:S(2)}) collective-permute-start(bf16[256,256]{1,0:T(8,128)(2,1)S(1)} %get-tuple-element.14), channel_id=1, source_target_pairs={{0,12},{1,13},{2,14},{3,15},{4,0},{5,1},{6,2},{7,3},{8,4},{9,5},{1... | collective-permute-start | bytes 393224 | tf_op jit(solution)/shard_map/ppermute | solution.py:44
  88.9 9.4 %all-to-all-done.1 = bf16[32,40,256]{2,1,0:T(8,128)(2,1)S(1)} async-done(((bf16[32,40,256]{2,1,0:T(8,128)(2,1)}), bf16[32,40,256]{2,1,0:T(8,128)(2,1)S(1)}, u32[]{:S(2)}, u32[]{:S(2)}) %all-to-all-start.1) | async-done | bytes 655392 | tf_op jit(solution)/shard_map/all_to_all | solution.py:195
  98.4 0.1 reduce
  98.5 0.6 broadcast_in_dim.18
  99.1 7.1 %all-to-all-start.2 = ((bf16[16,8,256]{2,1,0:T(8,128)(2,1)}), bf16[16,8,256]{2,1,0:T(8,128)(2,1)S(1)}, u32[]{:S(2)}, u32[]{:S(2)}) async-start(bf16[16,8,256]{2,1,0:T(8,128)(2,1)} %broadcast_in_dim.18), calls=%async_computation.2 | async-start | bytes 131072 | tf_op jit(solution)/shard_map/all_to_all | solution.py:19
  106.3 0.1 slice_add_fusion
  106.4 7.2 %collective-permute-start.4 = (bf16[128,256]{1,0:T(8,128)(2,1)S(1)}, bf16[128,256]{1,0:T(8,128)(2,1)S(1)}, u32[]{:S(2)}, u32[]{:S(2)}) collective-permute-start(bf16[128,256]{1,0:T(8,128)(2,1)S(1)} %slice.91), channel_id=1, source_target_pairs={{0,2},{1,3},{2,0},{3,1},{4,6},{5,7},{6,4},{7,5},{8,10},{9,11},{10,... | collective-permute-start | bytes 196616 | tf_op jit(solution)/shard_map/ppermute | solution.py:29
  113.5 2.4 %all-to-all-done.2 = bf16[16,8,256]{2,1,0:T(8,128)(2,1)S(1)} async-done(((bf16[16,8,256]{2,1,0:T(8,128)(2,1)}), bf16[16,8,256]{2,1,0:T(8,128)(2,1)S(1)}, u32[]{:S(2)}, u32[]{:S(2)}) %all-to-all-start.2) | async-done | bytes 65568 | tf_op jit(solution)/shard_map/all_to_all | solution.py:19
  116.0 0.7 broadcast_in_dim.19
  116.7 5.0 %all-to-all-start.3 = ((bf16[32,8,256]{2,1,0:T(8,128)(2,1)}), bf16[32,8,256]{2,1,0:T(8,128)(2,1)S(1)}, u32[]{:S(2)}, u32[]{:S(2)}) async-start(bf16[32,8,256]{2,1,0:T(8,128)(2,1)} %broadcast_in_dim.19), calls=%async_computation.3 | async-start | bytes 262144 | tf_op jit(solution)/shard_map/all_to_all | solution.py:19
  121.8 0.8 fusion.4
  122.6 0.8 fusion.5
  123.4 8.2 %all-to-all-done.3 = bf16[32,8,256]{2,1,0:T(8,128)(2,1)S(1)} async-done(((bf16[32,8,256]{2,1,0:T(8,128)(2,1)}), bf16[32,8,256]{2,1,0:T(8,128)(2,1)S(1)}, u32[]{:S(2)}, u32[]{:S(2)}) %all-to-all-start.3) | async-done | bytes 131104 | tf_op jit(solution)/shard_map/all_to_all | solution.py:19
  131.6 0.7 bitcast_convert_fusion
  (36 shorter events, 0.2 us)
Async XLA Ops:
  0.6 121.1 %copy-start = (bf16[256,256]{1,0:T(8,128)(2,1)S(1)}, bf16[256,256]{1,0:T(8,128)(2,1)}, u32[]{:S(2)}) copy-start(bf16[256,256]{1,0:T(8,128)(2,1)} %param.12) | copy-start | bytes 393220
  2.4 21.0 %collective-permute-start.5 = (bf16[2,128,256]{2,1,0:T(8,128)(2,1)S(1)}, bf16[2,128,256]{2,1,0:T(8,128)(2,1)S(1)}, u32[]{:S(2)}, u32[]{:S(2)}) collective-permute-start(bf16[2,128,256]{2,1,0:T(8,128)(2,1)S(1)} %constant_dynamic-update-slice_fusion), channel_id=1, source_target_pairs={{0,2},{1,3},{2,0},{3,1},{4,6},{5,7},{6,4},{7,5},{8,10},{9,11},{10,... | collective-permute-start | bytes 393224 | tf_op jit(solution)/shard_map/ppermute | solution.py:29
  12.5 37.1 %copy-start.9 = (s32[1,128]{1,0:T(1,128)S(1)}, s32[1,128]{1,0:T(1,128)}, u32[]{:S(2)}) copy-start(s32[1,128]{1,0:T(1,128)} %param.16) | copy-start | bytes 1540
  12.5 37.1 %copy-start.2 = (s32[1,128]{1,0:T(1,128)S(1)}, s32[1,128]{1,0:T(1,128)}, u32[]{:S(2)}) copy-start(s32[1,128]{1,0:T(1,128)} %param.17) | copy-start | bytes 1540
  12.5 37.1 %copy-start.3 = (s32[1,128]{1,0:T(1,128)S(1)}, s32[1,128]{1,0:T(1,128)}, u32[]{:S(2)}) copy-start(s32[1,128]{1,0:T(1,128)} %param.18) | copy-start | bytes 1540
  12.5 48.8 %all-to-all-start = ((bf16[32,2,32,256]{3,2,1,0:T(8,128)(2,1)}), bf16[32,2,32,256]{3,2,1,0:T(8,128)(2,1)S(1)}, u32[]{:S(2)}, u32[]{:S(2)}) async-start(bf16[32,2,32,256]{3,2,1,0:T(8,128)(2,1)} %broadcast_in_dim.15), calls=%async_computation | async-start | bytes 2097152 | tf_op jit(solution)/shard_map/all_to_all | solution.py:19
  23.5 10.7 %collective-permute-start.6 = (bf16[2,2,128,256]{3,2,1,0:T(8,128)(2,1)S(1)}, bf16[2,2,128,256]{3,2,1,0:T(8,128)(2,1)S(1)}, u32[]{:S(2)}, u32[]{:S(2)}) collective-permute-start(bf16[2,2,128,256]{3,2,1,0:T(8,128)(2,1)S(1)} %pad_maximum_fusion.1), channel_id=1, source_target_pairs={{4,0},{5,1},{6,2},{7,3},{8,4},{9,5},{10,6},{11,7},{12,8},{13,9},{1... | collective-permute-start | bytes 786440 | tf_op jit(solution)/shard_map/ppermute | solution.py:39
  28.5 9.7 %collective-permute-start.7 = (bf16[2,2,128,256]{3,2,1,0:T(8,128)(2,1)S(1)}, bf16[2,2,128,256]{3,2,1,0:T(8,128)(2,1)S(1)}, u32[]{:S(2)}, u32[]{:S(2)}) collective-permute-start(bf16[2,2,128,256]{3,2,1,0:T(8,128)(2,1)S(1)} %pad_maximum_fusion.1), channel_id=1, source_target_pairs={{8,0},{9,1},{10,2},{11,3},{12,4},{13,5},{14,6},{15,7},{0,8},{1,9},... | collective-permute-start | bytes 786440 | tf_op jit(solution)/shard_map/ppermute | solution.py:39
  31.0 14.5 %collective-permute-start.8 = (bf16[2,2,128,256]{3,2,1,0:T(8,128)(2,1)S(1)}, bf16[2,2,128,256]{3,2,1,0:T(8,128)(2,1)S(1)}, u32[]{:S(2)}, u32[]{:S(2)}) collective-permute-start(bf16[2,2,128,256]{3,2,1,0:T(8,128)(2,1)S(1)} %pad_maximum_fusion.1), channel_id=1, source_target_pairs={{12,0},{13,1},{14,2},{15,3},{0,4},{1,5},{2,6},{3,7},{4,8},{5,9},{6... | collective-permute-start | bytes 786440 | tf_op jit(solution)/shard_map/ppermute | solution.py:39
  46.2 12.3 %collective-permute-start.9 = (bf16[2,1024,256]{2,1,0:T(8,128)(2,1)}, bf16[2,1024,256]{2,1,0:T(8,128)(2,1)}, u32[]{:S(2)}, u32[]{:S(2)}) collective-permute-start(bf16[2,1024,256]{2,1,0:T(8,128)(2,1)} %bitcast.12), channel_id=1, source_target_pairs={{0,1},{1,0},{2,3},{3,2},{4,5},{5,4},{6,7},{7,6},{8,9},{9,8},{10,11... | collective-permute-start | bytes 3145736 | tf_op jit(solution)/shard_map/ppermute | solution.py:29
  49.6 2.2 %copy-start.1 = (bf16[1,128,128,128]{3,2,1,0:T(8,128)(2,1)S(1)}, bf16[1,128,128,128]{3,2,1,0:T(8,128)(2,1)}, u32[]{:S(2)}) copy-start(bf16[1,128,128,128]{3,2,1,0:T(8,128)(2,1)} %param.15) | copy-start | bytes 12582916
  55.5 3.0 %copy-start.4 = (bf16[1024,1024]{1,0:T(8,128)(2,1)}, bf16[1024,1024]{1,0:T(8,128)(2,1)S(1)}, u32[]{:S(2)}) copy-start(bf16[1024,1024]{1,0:T(8,128)(2,1)S(1)} %get-tuple-element.6) | copy-start | bytes 6291460
  61.4 1.6 %copy-start.5 = (bf16[1024,1024]{1,0:T(8,128)(2,1)S(1)}, bf16[1024,1024]{1,0:T(8,128)(2,1)}, u32[]{:S(2)}) copy-start(bf16[1024,1024]{1,0:T(8,128)(2,1)} %copy-done.4) | copy-start | bytes 6291460
  62.9 2.6 %copy-start.8 = (bf16[1,8,128,256]{3,2,1,0:T(8,128)(2,1)S(1)}, bf16[1,8,128,256]{3,2,1,0:T(8,128)(2,1)}, u32[]{:S(2)}) copy-start(bf16[1,8,128,256]{3,2,1,0:T(8,128)(2,1)} %get-tuple-element.8) | copy-start | bytes 1572868
  62.9 2.7 %copy-start.10 = (f32[1024,256]{1,0:T(8,128)S(1)}, f32[1024,256]{1,0:T(8,128)}, u32[]{:S(2)}) copy-start(f32[1024,256]{1,0:T(8,128)} %fusion.7) | copy-start | bytes 3145732
  63.7 4.5 %collective-permute-start = (bf16[1024,256]{1,0:T(8,128)(2,1)S(1)}, bf16[1024,256]{1,0:T(8,128)(2,1)S(1)}, u32[]{:S(2)}, u32[]{:S(2)}) collective-permute-start(bf16[1024,256]{1,0:T(8,128)(2,1)S(1)} %convolution_convert_fusion), channel_id=1, source_target_pairs={{0,1},{1,0},{2,3},{3,2},{4,5},{5,4},{6,7},{7,6},{8,9},{9,8},{10,11... | collective-permute-start | bytes 1572872 | tf_op jit(solution)/shard_map/ppermute | solution.py:29
  68.1 1.5 %copy-start.7 = (bf16[1,8,128,256]{3,2,1,0:T(8,128)(2,1)S(1)}, bf16[1,8,128,256]{3,2,1,0:T(8,128)(2,1)}, u32[]{:S(2)}) copy-start(bf16[1,8,128,256]{3,2,1,0:T(8,128)(2,1)} %get-tuple-element.7) | copy-start | bytes 1572868
  69.7 10.8 %copy-start.6 = (bf16[1024,256]{1,0:T(8,128)(2,1)S(1)}, bf16[1024,256]{1,0:T(8,128)(2,1)}, u32[]{:S(2)}) copy-start(bf16[1024,256]{1,0:T(8,128)(2,1)} %get-tuple-element.11) | copy-start | bytes 1572868
  70.9 27.5 %all-to-all-start.1 = ((bf16[32,40,256]{2,1,0:T(8,128)(2,1)}), bf16[32,40,256]{2,1,0:T(8,128)(2,1)S(1)}, u32[]{:S(2)}, u32[]{:S(2)}) async-start(bf16[32,40,256]{2,1,0:T(8,128)(2,1)} %pad_maximum_fusion), calls=%async_computation.1 | async-start | bytes 1310720 | tf_op jit(solution)/shard_map/all_to_all | solution.py:195
  80.5 25.7 %collective-permute-start.1 = (bf16[256,256]{1,0:T(8,128)(2,1)S(1)}, bf16[256,256]{1,0:T(8,128)(2,1)S(1)}, u32[]{:S(2)}, u32[]{:S(2)}) collective-permute-start(bf16[256,256]{1,0:T(8,128)(2,1)S(1)} %get-tuple-element.13), channel_id=1, source_target_pairs={{0,4},{1,5},{2,6},{3,7},{4,8},{5,9},{6,10},{7,11},{8,12},{9,13},{1... | collective-permute-start | bytes 393224 | tf_op jit(solution)/shard_map/ppermute | solution.py:44
  82.4 23.8 %collective-permute-start.2 = (bf16[256,256]{1,0:T(8,128)(2,1)S(1)}, bf16[256,256]{1,0:T(8,128)(2,1)S(1)}, u32[]{:S(2)}, u32[]{:S(2)}) collective-permute-start(bf16[256,256]{1,0:T(8,128)(2,1)S(1)} %get-tuple-element.15), channel_id=1, source_target_pairs={{0,8},{1,9},{2,10},{3,11},{4,12},{5,13},{6,14},{7,15},{8,0},{9,1},... | collective-permute-start | bytes 393224 | tf_op jit(solution)/shard_map/ppermute | solution.py:44
  85.7 20.6 %collective-permute-start.3 = (bf16[256,256]{1,0:T(8,128)(2,1)S(1)}, bf16[256,256]{1,0:T(8,128)(2,1)S(1)}, u32[]{:S(2)}, u32[]{:S(2)}) collective-permute-start(bf16[256,256]{1,0:T(8,128)(2,1)S(1)} %get-tuple-element.14), channel_id=1, source_target_pairs={{0,12},{1,13},{2,14},{3,15},{4,0},{5,1},{6,2},{7,3},{8,4},{9,5},{1... | collective-permute-start | bytes 393224 | tf_op jit(solution)/shard_map/ppermute | solution.py:44
  99.1 16.9 %all-to-all-start.2 = ((bf16[16,8,256]{2,1,0:T(8,128)(2,1)}), bf16[16,8,256]{2,1,0:T(8,128)(2,1)S(1)}, u32[]{:S(2)}, u32[]{:S(2)}) async-start(bf16[16,8,256]{2,1,0:T(8,128)(2,1)} %broadcast_in_dim.18), calls=%async_computation.2 | async-start | bytes 131072 | tf_op jit(solution)/shard_map/all_to_all | solution.py:19
  106.4 15.4 %collective-permute-start.4 = (bf16[128,256]{1,0:T(8,128)(2,1)S(1)}, bf16[128,256]{1,0:T(8,128)(2,1)S(1)}, u32[]{:S(2)}, u32[]{:S(2)}) collective-permute-start(bf16[128,256]{1,0:T(8,128)(2,1)S(1)} %slice.91), channel_id=1, source_target_pairs={{0,2},{1,3},{2,0},{3,1},{4,6},{5,7},{6,4},{7,5},{8,10},{9,11},{10,... | collective-permute-start | bytes 196616 | tf_op jit(solution)/shard_map/ppermute | solution.py:29
  116.7 14.9 %all-to-all-start.3 = ((bf16[32,8,256]{2,1,0:T(8,128)(2,1)}), bf16[32,8,256]{2,1,0:T(8,128)(2,1)S(1)}, u32[]{:S(2)}, u32[]{:S(2)}) async-start(bf16[32,8,256]{2,1,0:T(8,128)(2,1)} %broadcast_in_dim.19), calls=%async_computation.3 | async-start | bytes 262144 | tf_op jit(solution)/shard_map/all_to_all | solution.py:19

commit v3 on v2

--- a/solution.py
+++ b/solution.py
@@ -17,12 +17,6 @@
 def from_everyone(value, axis):
     copies = jnp.broadcast_to(value, (lax.axis_size(axis), *value.shape))
     return lax.all_to_all(copies, axis, split_axis=0, concat_axis=0, tiled=True)
-
-
-def to_owners(value, axis):
-    peers = lax.axis_size(axis)
-    pieces = value.reshape(peers, value.shape[0] // peers, *value.shape[1:])
-    return lax.all_to_all(pieces, axis, split_axis=0, concat_axis=0, tiled=True)
 
 
 def partner(value, bit):
@@ -116,7 +110,7 @@
             scratch_shapes=[pltpu.VMEM((positions, edge, edge), jnp.float32)],
         ),
         compiler_params=pltpu.CompilerParams(
-            dimension_semantics=("arbitrary",), vmem_limit_bytes=40 << 20
+            dimension_semantics=("arbitrary",), vmem_limit_bytes=24 << 20
         ),
         cost_estimate=pl.CostEstimate(
             flops=4 * slots * edge * edge,
@@ -124,7 +118,34 @@
             transcendentals=0,
         ),
         name="dense_block",
-    )(row_ids, col_ids, norm_ids, count, tile_block)
+    )(
+        row_ids,
+        col_ids,
+        norm_ids,
+        count,
+        pltpu.with_memory_space_constraint(tile_block, pltpu.HBM),
+    )
+
+
+def lay_out_kernel(grad_user, user_emb, grad_item, item_emb, mine, pieces):
+    rows = grad_user.shape[0]
+    mine[:rows] = grad_user[...]
+    mine[rows:] = user_emb[...]
+    for peer in range(pieces.shape[0]):
+        pieces[peer, 0] = grad_item[...]
+        pieces[peer, 1] = item_emb[...]
+
+
+def lay_out(grad_user, user_emb, grad_item, item_emb):
+    peers = lax.axis_size("au")
+    return pl.pallas_call(
+        lay_out_kernel,
+        out_shape=[
+            jax.ShapeDtypeStruct((2 * grad_user.shape[0], grad_user.shape[1]), grad_user.dtype),
+            jax.ShapeDtypeStruct((peers, 2, *grad_item.shape), grad_item.dtype),
+        ],
+        name="lay_out",
+    )(grad_user, user_emb, grad_item, item_emb)
 
 
 def product(spec, left, right):
@@ -135,7 +156,7 @@
     return value.astype(jnp.float32)
 
 
-def per_device(
+def device_step(
     user_emb,
     item_emb,
     weight,
@@ -153,13 +174,19 @@
     low = jnp.bfloat16
     ring = lax.axis_size("ia") // ring_step
 
-    mine = jnp.stack([grad_user[0], user_emb[0]])
-    pair = jnp.stack([mine, partner(mine, side_bit)], axis=1)
-    near = jnp.concatenate([pair] + [from_ahead(pair, d) for d in range(1, ring)], axis=1)
-    near = near.reshape(2, user_rows // 2, width)
+    mine, item_sent = lay_out(grad_user[0], user_emb[0], grad_item[0], item_emb[0])
+    beside = partner(mine, side_bit)
+    pair = jnp.concatenate([mine, beside])
+    own_rows = user_emb.shape[1]
+    item_pieces = lax.all_to_all(item_sent, "au", split_axis=0, concat_axis=0, tiled=True)
+    parts = [pair]
+    for distance in range(1, ring):
+        parts.append(from_ahead(pair, distance))
+    quarters = [part[i * own_rows : (i + 1) * own_rows] for part in parts for i in range(4)]
+    near = jnp.concatenate(quarters[0::2])
+    near_emb = jnp.concatenate(quarters[1::2])
     far = partner(near, core_bit)
 
-    item_pieces = from_everyone(jnp.stack([grad_item[0], item_emb[0]]), "au")
     items = item_pieces[:, 0].reshape(item_rows, width)
     item_table = item_pieces[:, 1].reshape(item_rows, width)
 
@@ -174,14 +201,13 @@
     )
     user_far = product("ui,id->ud", dense_far, items).astype(low)
     user_near = product("ui,id->ud", dense_near, items).astype(low)
-    item_part = product("ui,ud->id", dense_near, near[0]) + product(
-        "ui,ud->id", dense_far, far[0]
-    )
+    user_sum = wide(user_near) + wide(partner(user_far, core_bit))
+    user_sent = user_sum.astype(low)
+
+    item_part = product("ui,ud->id", dense_near, near) + product("ui,ud->id", dense_far, far)
     item_part = item_part.astype(low)
-    weight_part = (
-        product("rd,re->de", near[1], user_near)
-        + product("rd,re->de", far[1], user_far)
-        + product("rd,re->de", item_table, item_part)
+    weight_part = product("rd,re->de", near_emb, user_sent) + product(
+        "rd,re->de", item_table, item_part
     )
 
     peers = lax.axis_size("au")
@@ -200,11 +226,9 @@
     strip = strip / math.sqrt(user_count + item_count)
     grad_weight = wide(from_everyone(strip.astype(low), "au")).reshape(width, width)
 
-    along = wide(user_near) + wide(partner(user_far, core_bit))
-    along = along.reshape(ring, user_rows // (2 * ring), width)
-    sent = along.astype(low)
+    along = user_sum.reshape(ring, user_rows // (2 * ring), width)
+    sent = user_sent.reshape(along.shape)
     both = along[0] + sum(wide(send_ahead(sent[d], d)) for d in range(1, ring))
-    own_rows = user_emb.shape[1]
     q_user = both[:own_rows] + wide(partner(both[own_rows:].astype(low), side_bit))
 
     grad_user_emb = product("re,de->rd", q_user.astype(low), weight).astype(low)
@@ -214,7 +238,7 @@
 
 def solution(mesh):
     return jax.shard_map(
-        per_device,
+        device_step,
         mesh=mesh,
         in_specs=(
             P("au", "ia", None),

time: 133 us -> 132 us (level)
  Pallas kernels: 3.68 us -> 9.04 us
  local copies, waits for them, and re-layouts: 14.6 us -> 9.34 us
  waiting for transfers between devices: 30 us -> 25.8 us
  starting transfers between devices: 70.4 us -> 73.5 us
    all_to_all x1 -> x2, starting transfers between devices: 9.54 us -> 20.3 us  [the longest x1 10.9 us: device_step(): lax.all_to_all(item_sent, 'au', split_axis=0, concat_axis=0, tiled=True)]
    all_to_all x3 -> x2, starting transfers between devices: 23.1 us -> 12.7 us  [from_everyone(): return lax.all_to_all(copies, axis, split_axis=0, concat_axis=0, tiled=True)]
    pallas_call x1, Pallas kernels: 3.68 us -> 7.05 us  [dense_block(): pl.pallas_call(dense_kernel, out_shape=[jax.ShapeDtypeStruct((user_rows /...]
    ppermute x3, waiting for transfers between devices: 9.86 us -> 6.72 us  [from_ahead(): lax.ppermute(value, 'ia', [(ahead(i, distance), i) for i in range(size)])]
    slice x5 -> x4, local copies, waits for them, and re-layouts: 3.14 us -> 0.11 us  [the longest x1 0.07 us: device_step(): item_table = item_pieces[:, 1].reshape(item_rows, width)]
    ppermute x4, starting transfers between devices: 20 us -> 22.1 us  [partner(): lax.ppermute(value, 'ia', [(i, i ^ bit) for i in range(lax.axis_size('ia'...]
    pallas_call x0 -> x1, Pallas kernels: none -> 1.99 us  [lay_out(): pl.pallas_call(lay_out_kernel, out_shape=[jax.ShapeDtypeStruct((2 * grad_...]
    all_to_all x3 -> x2, waiting for transfers between devices: 10.7 us -> 9.71 us  [from_everyone(): return lax.all_to_all(copies, axis, split_axis=0, concat_axis=0, tiled=True)]
  transfers between devices with their start and end apart: 14 -> 14, of which waited for: 5 -> 4; matrix products, arithmetic and copies ran while one was open for 13% -> 11% of each run, Pallas kernels for 3% -> 5%
where the time goes in v3:
time: 132 us; the launch traced here: 131 us
  starting transfers between devices  73.5 us (56%)
  waiting for transfers between devices  25.8 us (20%)
  local copies, waits for them, and re-layouts  9.34 us (7%)
  matrix products  9.27 us (7%)
  Pallas kernels  9.04 us (7%)
  other arithmetic  2.75 us (2%)
  between operations  1.64 us (1%)
    ppermute x4, starting transfers between devices, partner(): lax.ppermute(value, 'ia', [(i, i ^ bit) for i in range(lax.axis_size('ia'...  22.1 us
    all_to_all x2, starting transfers between devices, from_everyone(): return lax.all_to_all(copies, axis, split_axis=0, concat_axis=0, tiled=True)  12.7 us
    all_to_all x1, starting transfers between devices, device_step(): lax.all_to_all(item_sent, 'au', split_axis=0, concat_axis=0, tiled=True)  10.9 us
    ppermute x3, starting transfers between devices, from_ahead(): lax.ppermute(value, 'ia', [(ahead(i, distance), i) for i in range(size)])  9.92 us
    all_to_all x2, waiting for transfers between devices, from_everyone(): return lax.all_to_all(copies, axis, split_axis=0, concat_axis=0, tiled=True)  9.71 us
    all_to_all x1, waiting for transfers between devices, device_step(): lax.all_to_all(pieces, 'au', split_axis=0, concat_axis=0, tiled=True)  9.37 us
    all_to_all x1, starting transfers between devices, device_step(): lax.all_to_all(pieces, 'au', split_axis=0, concat_axis=0, tiled=True)  9.35 us
    dot_general x8, matrix products, product(): return jnp.einsum(spec, left, right, preferred_element_type=jnp.float32)  9.27 us
  transfers between devices with their start and end apart: 14, of which 4 were waited for; matrix products, arithmetic and copies ran while one was open for 11% of the time, Pallas kernels for 5%

profile of v3, /device:TPU:1, one launch (start us, length us, event | category | flops | bytes accessed | tf_op | source)
XLA Modules:
  0.0 131.3 jit_solution(9655925162045367366)
XLA Ops:
  0.6 0.0 copy-start
  0.6 2.0 %lay_out.1 = (bf16[256,256]{1,0:T(8,128)(2,1)}, bf16[32,2,32,256]{3,2,1,0:T(8,128)(2,1)}) custom-call(bf16[128,256]{1,0:T(8,128)(2,1)} %bitcast.44, bf16[128,256]{1,0:T(8,128)(2,1)} %bitcast.45, bf16[32,256]{1,0:T(8,128)(2,1)} %bitcast.46, bf16[32,256]{1,0:T(8,128)(2,1)} %bitcast.47), custom_call_target="tpu_custom_call" | custom-call | tf_op jit(solution)/shard_map/lay_out/pallas_call | solution.py:141
  2.6 8.4 %collective-permute-start.5 = (bf16[256,256]{1,0:T(8,128)(2,1)}, bf16[256,256]{1,0:T(8,128)(2,1)S(1)}, u32[]{:S(2)}, u32[]{:S(2)}) collective-permute-start(bf16[256,256]{1,0:T(8,128)(2,1)} %get-tuple-element.10), channel_id=1, source_target_pairs={{0,2},{1,3},{2,0},{3,1},{4,6},{5,7},{6,4},{7,5},{8,10},{9,11},{10,... | collective-permute-start | bytes 393224 | tf_op jit(solution)/shard_map/ppermute | solution.py:23
  11.0 0.0 copy-start.8
  11.1 0.0 copy-start.1
  11.1 10.9 %all-to-all-start = ((bf16[32,2,32,256]{3,2,1,0:T(8,128)(2,1)}), bf16[32,2,32,256]{3,2,1,0:T(8,128)(2,1)S(1)}, u32[]{:S(2)}, u32[]{:S(2)}) async-start(bf16[32,2,32,256]{3,2,1,0:T(8,128)(2,1)} %get-tuple-element.8), calls=%async_computation | async-start | bytes 2097152 | tf_op jit(solution)/shard_map/all_to_all | solution.py:181
  22.1 4.4 %collective-permute-start.6 = (bf16[512,256]{1,0:T(8,128)(2,1)S(1)}, bf16[512,256]{1,0:T(8,128)(2,1)S(1)}, u32[]{:S(2)}, u32[]{:S(2)}) collective-permute-start(bf16[512,256]{1,0:T(8,128)(2,1)S(1)} %constant_dynamic-update-slice_fusion), channel_id=1, source_target_pairs={{4,0},{5,1},{6,2},{7,3},{8,4},{9,5},{10,6},{11,7},{12,8},{13,9},{1... | collective-permute-start | bytes 786440 | tf_op jit(solution)/shard_map/ppermute | solution.py:33
  26.4 0.6 slice_dynamic-update-slice_fusion.14
  27.1 1.9 %collective-permute-start.8 = (bf16[512,256]{1,0:T(8,128)(2,1)S(1)}, bf16[512,256]{1,0:T(8,128)(2,1)S(1)}, u32[]{:S(2)}, u32[]{:S(2)}) collective-permute-start(bf16[512,256]{1,0:T(8,128)(2,1)S(1)} %constant_dynamic-update-slice_fusion), channel_id=1, source_target_pairs={{12,0},{13,1},{14,2},{15,3},{0,4},{1,5},{2,6},{3,7},{4,8},{5,9},{6... | collective-permute-start | bytes 786440 | tf_op jit(solution)/shard_map/ppermute | solution.py:33
  29.0 3.6 %collective-permute-start.7 = (bf16[512,256]{1,0:T(8,128)(2,1)S(1)}, bf16[512,256]{1,0:T(8,128)(2,1)S(1)}, u32[]{:S(2)}, u32[]{:S(2)}) collective-permute-start(bf16[512,256]{1,0:T(8,128)(2,1)S(1)} %constant_dynamic-update-slice_fusion), channel_id=1, source_target_pairs={{8,0},{9,1},{10,2},{11,3},{12,4},{13,5},{14,6},{15,7},{0,8},{1,9},... | collective-permute-start | bytes 786440 | tf_op jit(solution)/shard_map/ppermute | solution.py:33
  32.6 0.6 slice_dynamic-update-slice_fusion.6
  33.3 0.6 slice_dynamic-update-slice_fusion.5
  33.9 0.6 slice_dynamic-update-slice_fusion.4
  34.5 6.7 %collective-permute-done.7 = bf16[512,256]{1,0:T(8,128)(2,1)S(1)} collective-permute-done((bf16[512,256]{1,0:T(8,128)(2,1)S(1)}, bf16[512,256]{1,0:T(8,128)(2,1)S(1)}, u32[]{:S(2)}, u32[]{:S(2)}) %collective-permute-start.7) | collective-permute-done | bytes 262176 | tf_op jit(solution)/shard_map/ppermute | solution.py:33
  41.2 0.6 slice_dynamic-update-slice_fusion.3
  41.9 0.6 slice_dynamic-update-slice_fusion.2
  42.5 0.6 slice_dynamic-update-slice_fusion.1
  43.1 0.6 slice_dynamic-update-slice_fusion
  43.7 4.3 %collective-permute-start.9 = (bf16[1024,256]{1,0:T(8,128)(2,1)}, bf16[1024,256]{1,0:T(8,128)(2,1)}, u32[]{:S(2)}, u32[]{:S(2)}) collective-permute-start(bf16[1024,256]{1,0:T(8,128)(2,1)} %get-tuple-element.19), channel_id=1, source_target_pairs={{0,1},{1,0},{2,3},{3,2},{4,5},{5,4},{6,7},{7,6},{8,9},{9,8},{10,11... | collective-permute-start | bytes 1572872 | tf_op jit(solution)/shard_map/ppermute | solution.py:23
  48.8 7.0 %dense_block.1 = (bf16[1024,1024]{1,0:T(8,128)(2,1)S(1)}, bf16[1024,1024]{1,0:T(8,128)(2,1)S(1)}) custom-call(s32[128]{0:T(128)S(1)} %add_bitcast_fusion.rows, s32[128]{0:T(128)S(1)} %bitcast.37, s32[128]{0:T(128)S(1)} %bitcast.38, s32[1]{0:T(128)} %bitcast.36.count, bf16[128,128,128]{2,1,0:T(8,128)(2,1)} %bitcast.39), custom_call_target="tpu_custom_call" | custom-call | flops 8388608 | bytes 8388608 | tf_op jit(solution)/shard_map/dense_block/pallas_call | solution.py:102
  55.9 1.3 %copy-done.3 = bf16[1024,1024]{1,0:T(8,128)(2,1)} copy-done((bf16[1024,1024]{1,0:T(8,128)(2,1)}, bf16[1024,1024]{1,0:T(8,128)(2,1)S(1)}, u32[]{:S(2)}) %copy-start.3) | copy-done | bytes 2097176
  57.2 2.8 %fusion.12 = f32[1024,256]{1,0:T(8,128)} fusion(bf16[1024,1024]{1,0:T(8,128)(2,1)S(1)} %get-tuple-element.9, bf16[1024,256]{1,0:T(8,128)(2,1)} %collective-permute-done.9), kind=kOutput, calls=%fused_computation.44 | convolution fusion | flops 536870912 | bytes 3670016 | tf_op jit(solution)/shard_map/ui,ud->id/dot_general | solution.py:152
  60.0 0.1 fusion.10
  60.0 1.5 %copy-done.4 = bf16[1024,1024]{1,0:T(8,128)(2,1)S(1)} copy-done((bf16[1024,1024]{1,0:T(8,128)(2,1)S(1)}, bf16[1024,1024]{1,0:T(8,128)(2,1)}, u32[]{:S(2)}) %copy-start.4) | copy-done | bytes 2097176
  61.6 0.7 convolution_convert_fusion
  62.3 2.2 %collective-permute-start = (bf16[1024,256]{1,0:T(8,128)(2,1)S(1)}, bf16[1024,256]{1,0:T(8,128)(2,1)S(1)}, u32[]{:S(2)}, u32[]{:S(2)}) collective-permute-start(bf16[1024,256]{1,0:T(8,128)(2,1)S(1)} %convolution_convert_fusion), channel_id=1, source_target_pairs={{0,1},{1,0},{2,3},{3,2},{4,5},{5,4},{6,7},{7,6},{8,9},{9,8},{10,11... | collective-permute-start | bytes 1572872 | tf_op jit(solution)/shard_map/ppermute | solution.py:23
  64.5 1.8 %fusion.1 = bf16[1024,256]{1,0:T(8,128)(2,1)S(1)} fusion(f32[1024,256]{1,0:T(8,128)S(1)} %copy-done.9, bf16[1024,1024]{1,0:T(8,128)(2,1)S(1)} %get-tuple-element.7, bf16[1024,256]{1,0:T(8,128)(2,1)} %get-tuple-element.19), kind=kOutput, calls=%fused_computation.4 | convolution fusion | flops 537395200 | bytes 4194304 | tf_op jit(solution)/shard_map/ui,ud->id/dot_general | solution.py:152
  66.3 0.3 fusion.13
  66.7 1.7 %fusion.9 = (bf16[1024,256]{1,0:T(8,128)(2,1)S(1)}, f32[1024,256]{1,0:T(8,128)}) fusion(bf16[1024,256]{1,0:T(8,128)(2,1)S(1)} %collective-permute-done, bf16[1024,1024]{1,0:T(8,128)(2,1)S(1)} %get-tuple-element.7, bf16[1024,256]{1,0:T(8,128)(2,1)S(1)} %bitcast.43), kind=kOutput, calls=%fused_computation.41 | convolution fusion | flops 538181632 | bytes 4718592 | tf_op jit(solution)/shard_map/ui,id->ud/dot_general | solution.py:152
  68.4 0.3 fusion.3
  68.7 0.9 pad_maximum_fusion
  69.6 9.3 %all-to-all-start.1 = ((bf16[32,40,256]{2,1,0:T(8,128)(2,1)}), bf16[32,40,256]{2,1,0:T(8,128)(2,1)S(1)}, u32[]{:S(2)}, u32[]{:S(2)}) async-start(bf16[32,40,256]{2,1,0:T(8,128)(2,1)} %pad_maximum_fusion), calls=%async_computation.1 | async-start | bytes 1310720 | tf_op jit(solution)/shard_map/all_to_all | solution.py:221
  79.0 1.9 %collective-permute-start.1 = (bf16[256,256]{1,0:T(8,128)(2,1)S(1)}, bf16[256,256]{1,0:T(8,128)(2,1)S(1)}, u32[]{:S(2)}, u32[]{:S(2)}) collective-permute-start(bf16[256,256]{1,0:T(8,128)(2,1)S(1)} %get-tuple-element.15), channel_id=1, source_target_pairs={{0,4},{1,5},{2,6},{3,7},{4,8},{5,9},{6,10},{7,11},{8,12},{9,13},{1... | collective-permute-start | bytes 393224 | tf_op jit(solution)/shard_map/ppermute | solution.py:38
  80.9 4.6 %collective-permute-start.3 = (bf16[256,256]{1,0:T(8,128)(2,1)S(1)}, bf16[256,256]{1,0:T(8,128)(2,1)S(1)}, u32[]{:S(2)}, u32[]{:S(2)}) collective-permute-start(bf16[256,256]{1,0:T(8,128)(2,1)S(1)} %get-tuple-element.16), channel_id=1, source_target_pairs={{0,12},{1,13},{2,14},{3,15},{4,0},{5,1},{6,2},{7,3},{8,4},{9,5},{1... | collective-permute-start | bytes 393224 | tf_op jit(solution)/shard_map/ppermute | solution.py:38
  85.5 2.0 %collective-permute-start.2 = (bf16[256,256]{1,0:T(8,128)(2,1)S(1)}, bf16[256,256]{1,0:T(8,128)(2,1)S(1)}, u32[]{:S(2)}, u32[]{:S(2)}) collective-permute-start(bf16[256,256]{1,0:T(8,128)(2,1)S(1)} %get-tuple-element.17), channel_id=1, source_target_pairs={{0,8},{1,9},{2,10},{3,11},{4,12},{5,13},{6,14},{7,15},{8,0},{9,1},... | collective-permute-start | bytes 393224 | tf_op jit(solution)/shard_map/ppermute | solution.py:38
  87.5 9.4 %all-to-all-done.1 = bf16[32,40,256]{2,1,0:T(8,128)(2,1)S(1)} async-done(((bf16[32,40,256]{2,1,0:T(8,128)(2,1)}), bf16[32,40,256]{2,1,0:T(8,128)(2,1)S(1)}, u32[]{:S(2)}, u32[]{:S(2)}) %all-to-all-start.1) | async-done | bytes 655392 | tf_op jit(solution)/shard_map/all_to_all | solution.py:221
  96.9 0.1 reduce
  97.0 0.6 broadcast_in_dim.14
  97.6 7.7 %all-to-all-start.2 = ((bf16[16,8,256]{2,1,0:T(8,128)(2,1)}), bf16[16,8,256]{2,1,0:T(8,128)(2,1)S(1)}, u32[]{:S(2)}, u32[]{:S(2)}) async-start(bf16[16,8,256]{2,1,0:T(8,128)(2,1)} %broadcast_in_dim.14), calls=%async_computation.2 | async-start | bytes 131072 | tf_op jit(solution)/shard_map/all_to_all | solution.py:19
  105.3 1.0 slice_add_fusion
  106.3 7.2 %collective-permute-start.4 = (bf16[128,256]{1,0:T(8,128)(2,1)S(1)}, bf16[128,256]{1,0:T(8,128)(2,1)S(1)}, u32[]{:S(2)}, u32[]{:S(2)}) collective-permute-start(bf16[128,256]{1,0:T(8,128)(2,1)S(1)} %slice.159), channel_id=1, source_target_pairs={{0,2},{1,3},{2,0},{3,1},{4,6},{5,7},{6,4},{7,5},{8,10},{9,11},{10,... | collective-permute-start | bytes 196616 | tf_op jit(solution)/shard_map/ppermute | solution.py:23
  113.5 1.5 %all-to-all-done.2 = bf16[16,8,256]{2,1,0:T(8,128)(2,1)S(1)} async-done(((bf16[16,8,256]{2,1,0:T(8,128)(2,1)}), bf16[16,8,256]{2,1,0:T(8,128)(2,1)S(1)}, u32[]{:S(2)}, u32[]{:S(2)}) %all-to-all-start.2) | async-done | bytes 65568 | tf_op jit(solution)/shard_map/all_to_all | solution.py:19
  115.1 0.7 broadcast_in_dim.15
  115.7 5.0 %all-to-all-start.3 = ((bf16[32,8,256]{2,1,0:T(8,128)(2,1)}), bf16[32,8,256]{2,1,0:T(8,128)(2,1)S(1)}, u32[]{:S(2)}, u32[]{:S(2)}) async-start(bf16[32,8,256]{2,1,0:T(8,128)(2,1)} %broadcast_in_dim.15), calls=%async_computation.3 | async-start | bytes 262144 | tf_op jit(solution)/shard_map/all_to_all | solution.py:19
  120.8 0.8 fusion.4
  121.6 0.8 fusion.5
  122.4 8.2 %all-to-all-done.3 = bf16[32,8,256]{2,1,0:T(8,128)(2,1)S(1)} async-done(((bf16[32,8,256]{2,1,0:T(8,128)(2,1)}), bf16[32,8,256]{2,1,0:T(8,128)(2,1)S(1)}, u32[]{:S(2)}, u32[]{:S(2)}) %all-to-all-start.3) | async-done | bytes 131104 | tf_op jit(solution)/shard_map/all_to_all | solution.py:19
  130.6 0.7 bitcast_convert_fusion
  (33 shorter events, 0.2 us)
Async XLA Ops:
  0.6 120.1 %copy-start = (bf16[256,256]{1,0:T(8,128)(2,1)S(1)}, bf16[256,256]{1,0:T(8,128)(2,1)}, u32[]{:S(2)}) copy-start(bf16[256,256]{1,0:T(8,128)(2,1)} %param.12) | copy-start | bytes 393220
  2.6 19.4 %copy-start.7 = (bf16[256,256]{1,0:T(8,128)(2,1)S(1)}, bf16[256,256]{1,0:T(8,128)(2,1)}, u32[]{:S(2)}) copy-start(bf16[256,256]{1,0:T(8,128)(2,1)} %get-tuple-element.10) | copy-start | bytes 393220
  2.6 19.4 %collective-permute-start.5 = (bf16[256,256]{1,0:T(8,128)(2,1)}, bf16[256,256]{1,0:T(8,128)(2,1)S(1)}, u32[]{:S(2)}, u32[]{:S(2)}) collective-permute-start(bf16[256,256]{1,0:T(8,128)(2,1)} %get-tuple-element.10), channel_id=1, source_target_pairs={{0,2},{1,3},{2,0},{3,1},{4,6},{5,7},{6,4},{7,5},{8,10},{9,11},{10,... | collective-permute-start | bytes 393224 | tf_op jit(solution)/shard_map/ppermute | solution.py:23
  11.0 37.7 %copy-start.8 = (s32[1,128]{1,0:T(1,128)S(1)}, s32[1,128]{1,0:T(1,128)}, u32[]{:S(2)}) copy-start(s32[1,128]{1,0:T(1,128)} %param.16) | copy-start | bytes 1540
  11.1 37.7 %copy-start.1 = (s32[1,128]{1,0:T(1,128)S(1)}, s32[1,128]{1,0:T(1,128)}, u32[]{:S(2)}) copy-start(s32[1,128]{1,0:T(1,128)} %param.17) | copy-start | bytes 1540
  11.1 37.7 %copy-start.2 = (s32[1,128]{1,0:T(1,128)S(1)}, s32[1,128]{1,0:T(1,128)}, u32[]{:S(2)}) copy-start(s32[1,128]{1,0:T(1,128)} %param.18) | copy-start | bytes 1540
  11.1 48.9 %all-to-all-start = ((bf16[32,2,32,256]{3,2,1,0:T(8,128)(2,1)}), bf16[32,2,32,256]{3,2,1,0:T(8,128)(2,1)S(1)}, u32[]{:S(2)}, u32[]{:S(2)}) async-start(bf16[32,2,32,256]{3,2,1,0:T(8,128)(2,1)} %get-tuple-element.8), calls=%async_computation | async-start | bytes 2097152 | tf_op jit(solution)/shard_map/all_to_all | solution.py:181
  22.1 11.2 %collective-permute-start.6 = (bf16[512,256]{1,0:T(8,128)(2,1)S(1)}, bf16[512,256]{1,0:T(8,128)(2,1)S(1)}, u32[]{:S(2)}, u32[]{:S(2)}) collective-permute-start(bf16[512,256]{1,0:T(8,128)(2,1)S(1)} %constant_dynamic-update-slice_fusion), channel_id=1, source_target_pairs={{4,0},{5,1},{6,2},{7,3},{8,4},{9,5},{10,6},{11,7},{12,8},{13,9},{1... | collective-permute-start | bytes 786440 | tf_op jit(solution)/shard_map/ppermute | solution.py:33
  27.1 15.4 %collective-permute-start.8 = (bf16[512,256]{1,0:T(8,128)(2,1)S(1)}, bf16[512,256]{1,0:T(8,128)(2,1)S(1)}, u32[]{:S(2)}, u32[]{:S(2)}) collective-permute-start(bf16[512,256]{1,0:T(8,128)(2,1)S(1)} %constant_dynamic-update-slice_fusion), channel_id=1, source_target_pairs={{12,0},{13,1},{14,2},{15,3},{0,4},{1,5},{2,6},{3,7},{4,8},{5,9},{6... | collective-permute-start | bytes 786440 | tf_op jit(solution)/shard_map/ppermute | solution.py:33
  29.0 12.2 %collective-permute-start.7 = (bf16[512,256]{1,0:T(8,128)(2,1)S(1)}, bf16[512,256]{1,0:T(8,128)(2,1)S(1)}, u32[]{:S(2)}, u32[]{:S(2)}) collective-permute-start(bf16[512,256]{1,0:T(8,128)(2,1)S(1)} %constant_dynamic-update-slice_fusion), channel_id=1, source_target_pairs={{8,0},{9,1},{10,2},{11,3},{12,4},{13,5},{14,6},{15,7},{0,8},{1,9},... | collective-permute-start | bytes 786440 | tf_op jit(solution)/shard_map/ppermute | solution.py:33
  43.7 5.0 %copy-start.5 = (bf16[1024,256]{1,0:T(8,128)(2,1)}, bf16[1024,256]{1,0:T(8,128)(2,1)S(1)}, u32[]{:S(2)}) copy-start(bf16[1024,256]{1,0:T(8,128)(2,1)S(1)} %get-tuple-element.18) | copy-start | bytes 1572868
  43.7 12.1 %collective-permute-start.9 = (bf16[1024,256]{1,0:T(8,128)(2,1)}, bf16[1024,256]{1,0:T(8,128)(2,1)}, u32[]{:S(2)}, u32[]{:S(2)}) collective-permute-start(bf16[1024,256]{1,0:T(8,128)(2,1)} %get-tuple-element.19), channel_id=1, source_target_pairs={{0,1},{1,0},{2,3},{3,2},{4,5},{5,4},{6,7},{7,6},{8,9},{9,8},{10,11... | collective-permute-start | bytes 1572872 | tf_op jit(solution)/shard_map/ppermute | solution.py:23
  55.8 1.3 %copy-start.3 = (bf16[1024,1024]{1,0:T(8,128)(2,1)}, bf16[1024,1024]{1,0:T(8,128)(2,1)S(1)}, u32[]{:S(2)}) copy-start(bf16[1024,1024]{1,0:T(8,128)(2,1)S(1)} %get-tuple-element.9) | copy-start | bytes 6291460
  60.0 1.6 %copy-start.4 = (bf16[1024,1024]{1,0:T(8,128)(2,1)S(1)}, bf16[1024,1024]{1,0:T(8,128)(2,1)}, u32[]{:S(2)}) copy-start(bf16[1024,1024]{1,0:T(8,128)(2,1)} %copy-done.3) | copy-start | bytes 6291460
  61.5 2.9 %copy-start.9 = (f32[1024,256]{1,0:T(8,128)S(1)}, f32[1024,256]{1,0:T(8,128)}, u32[]{:S(2)}) copy-start(f32[1024,256]{1,0:T(8,128)} %fusion.12) | copy-start | bytes 3145732
  62.3 4.4 %collective-permute-start = (bf16[1024,256]{1,0:T(8,128)(2,1)S(1)}, bf16[1024,256]{1,0:T(8,128)(2,1)S(1)}, u32[]{:S(2)}, u32[]{:S(2)}) collective-permute-start(bf16[1024,256]{1,0:T(8,128)(2,1)S(1)} %convolution_convert_fusion), channel_id=1, source_target_pairs={{0,1},{1,0},{2,3},{3,2},{4,5},{5,4},{6,7},{7,6},{8,9},{9,8},{10,11... | collective-permute-start | bytes 1572872 | tf_op jit(solution)/shard_map/ppermute | solution.py:23
  66.6 1.7 %copy-start.6 = (bf16[1024,256]{1,0:T(8,128)(2,1)S(1)}, bf16[1024,256]{1,0:T(8,128)(2,1)}, u32[]{:S(2)}) copy-start(bf16[1024,256]{1,0:T(8,128)(2,1)} %copy-done.5) | copy-start | bytes 1572868
  69.6 27.3 %all-to-all-start.1 = ((bf16[32,40,256]{2,1,0:T(8,128)(2,1)}), bf16[32,40,256]{2,1,0:T(8,128)(2,1)S(1)}, u32[]{:S(2)}, u32[]{:S(2)}) async-start(bf16[32,40,256]{2,1,0:T(8,128)(2,1)} %pad_maximum_fusion), calls=%async_computation.1 | async-start | bytes 1310720 | tf_op jit(solution)/shard_map/all_to_all | solution.py:221
  79.0 26.3 %collective-permute-start.1 = (bf16[256,256]{1,0:T(8,128)(2,1)S(1)}, bf16[256,256]{1,0:T(8,128)(2,1)S(1)}, u32[]{:S(2)}, u32[]{:S(2)}) collective-permute-start(bf16[256,256]{1,0:T(8,128)(2,1)S(1)} %get-tuple-element.15), channel_id=1, source_target_pairs={{0,4},{1,5},{2,6},{3,7},{4,8},{5,9},{6,10},{7,11},{8,12},{9,13},{1... | collective-permute-start | bytes 393224 | tf_op jit(solution)/shard_map/ppermute | solution.py:38
  80.9 24.4 %collective-permute-start.3 = (bf16[256,256]{1,0:T(8,128)(2,1)S(1)}, bf16[256,256]{1,0:T(8,128)(2,1)S(1)}, u32[]{:S(2)}, u32[]{:S(2)}) collective-permute-start(bf16[256,256]{1,0:T(8,128)(2,1)S(1)} %get-tuple-element.16), channel_id=1, source_target_pairs={{0,12},{1,13},{2,14},{3,15},{4,0},{5,1},{6,2},{7,3},{8,4},{9,5},{1... | collective-permute-start | bytes 393224 | tf_op jit(solution)/shard_map/ppermute | solution.py:38
  85.5 19.8 %collective-permute-start.2 = (bf16[256,256]{1,0:T(8,128)(2,1)S(1)}, bf16[256,256]{1,0:T(8,128)(2,1)S(1)}, u32[]{:S(2)}, u32[]{:S(2)}) collective-permute-start(bf16[256,256]{1,0:T(8,128)(2,1)S(1)} %get-tuple-element.17), channel_id=1, source_target_pairs={{0,8},{1,9},{2,10},{3,11},{4,12},{5,13},{6,14},{7,15},{8,0},{9,1},... | collective-permute-start | bytes 393224 | tf_op jit(solution)/shard_map/ppermute | solution.py:38
  97.6 17.4 %all-to-all-start.2 = ((bf16[16,8,256]{2,1,0:T(8,128)(2,1)}), bf16[16,8,256]{2,1,0:T(8,128)(2,1)S(1)}, u32[]{:S(2)}, u32[]{:S(2)}) async-start(bf16[16,8,256]{2,1,0:T(8,128)(2,1)} %broadcast_in_dim.14), calls=%async_computation.2 | async-start | bytes 131072 | tf_op jit(solution)/shard_map/all_to_all | solution.py:19
  106.3 14.4 %collective-permute-start.4 = (bf16[128,256]{1,0:T(8,128)(2,1)S(1)}, bf16[128,256]{1,0:T(8,128)(2,1)S(1)}, u32[]{:S(2)}, u32[]{:S(2)}) collective-permute-start(bf16[128,256]{1,0:T(8,128)(2,1)S(1)} %slice.159), channel_id=1, source_target_pairs={{0,2},{1,3},{2,0},{3,1},{4,6},{5,7},{6,4},{7,5},{8,10},{9,11},{10,... | collective-permute-start | bytes 196616 | tf_op jit(solution)/shard_map/ppermute | solution.py:23
  115.7 14.9 %all-to-all-start.3 = ((bf16[32,8,256]{2,1,0:T(8,128)(2,1)}), bf16[32,8,256]{2,1,0:T(8,128)(2,1)S(1)}, u32[]{:S(2)}, u32[]{:S(2)}) async-start(bf16[32,8,256]{2,1,0:T(8,128)(2,1)} %broadcast_in_dim.15), calls=%async_computation.3 | async-start | bytes 262144 | tf_op jit(solution)/shard_map/all_to_all | solution.py:19

commit v4 on v3

--- a/solution.py
+++ b/solution.py
@@ -51,80 +51,145 @@
     return pieces.astype(jnp.float32).sum(axis=0)
 
 
-def dense_kernel(rows, cols, norms, count, tiles, near, far, total):
-    step = pl.program_id(0)
+def in_main(value):
+    return pltpu.with_memory_space_constraint(value, pltpu.HBM)
+
+
+def dense_kernel(
+    rows, cols, norms, count, tiles_in, near, far, tiles, total, low, in_sems, out_sems
+):
     edge = tiles.shape[1]
+    item_tiles = near.shape[1] // edge
     half_tiles = near.shape[0] // edge
-    item_tiles = near.shape[1] // edge
-
-    @pl.when(step == 0)
-    def clear():
-        def clear_one(index, carry):
-            total[index] = jnp.zeros((edge, edge), jnp.float32)
+    chunks = (count[0] + slot_block - 1) // slot_block
+
+    def chunk_copy(chunk):
+        slots = pl.ds(chunk * slot_block, slot_block)
+        return pltpu.make_async_copy(tiles_in.at[slots], tiles.at[slots], in_sems.at[chunk])
+
+    def fetch(chunk, carry):
+        chunk_copy(chunk).start()
+        return carry
+
+    lax.fori_loop(0, chunks, fetch, 0)
+
+    def clear(index, carry):
+        total[pl.ds(index * 4, 4)] = jnp.zeros((4, edge, edge), jnp.float32)
+        return carry
+
+    lax.fori_loop(0, total.shape[0] // 4, clear, 0)
+
+    def add_chunk(chunk, carry):
+        chunk_copy(chunk).wait()
+
+        def add_group(group, inner):
+            for lane in range(unroll):
+                slot = chunk * slot_block + group * unroll + lane
+                place = rows[slot] * item_tiles + cols[slot]
+                norm = jnp.full((8, edge), norms[slot], jnp.int32).astype(jnp.float32)
+                scale = jnp.where(slot < count[0], 1.0 / norm, 0.0)
+                term = tiles[slot].astype(jnp.float32).reshape(edge // 8, 8, edge) * scale[None]
+                total[place] = total[place] + term.reshape(edge, edge)
+            return inner
+
+        return lax.fori_loop(0, slot_block // unroll, add_group, carry)
+
+    lax.fori_loop(0, chunks, add_chunk, 0)
+
+    def row_copy(half, row):
+        kept = pl.ds(pl.multiple_of((half * half_tiles + row) * edge, edge), edge)
+        out = pl.ds(pl.multiple_of(row * edge, edge), edge)
+        dense = near if half == 0 else far
+        return pltpu.make_async_copy(
+            low.at[kept], dense.at[out], out_sems.at[half * half_tiles + row]
+        )
+
+    for half in range(2):
+
+        def finish_row(row, carry):
+            start = pl.multiple_of((half * half_tiles + row) * edge, edge)
+            for col in range(item_tiles):
+                low[pl.ds(start, edge), col * edge : (col + 1) * edge] = total[
+                    (half * half_tiles + row) * item_tiles + col
+                ].astype(jnp.bfloat16)
+
+            @pl.when(row > 0)
+            def send():
+                row_copy(half, row - 1).start()
+
             return carry
 
-        lax.fori_loop(0, total.shape[0], clear_one, 0)
-
-    first = step * slot_block
-    live = jnp.clip(count[0] - first, 0, slot_block)
-
-    def add_group(group, carry):
-        for lane in range(unroll):
-            local = group * unroll + lane
-            slot = first + local
-            place = rows[slot] * item_tiles + cols[slot]
-            norm = jnp.full((8, edge), norms[slot], jnp.int32).astype(jnp.float32)
-            scale = jnp.where(slot < count[0], 1.0 / norm, 0.0)
-            term = tiles[local].astype(jnp.float32).reshape(edge // 8, 8, edge) * scale[None]
-            total[place] = total[place] + term.reshape(edge, edge)
-        return carry
-
-    lax.fori_loop(0, (live + unroll - 1) // unroll, add_group, 0)
-
-    @pl.when(step == pl.num_programs(0) - 1)
-    def finish():
-        def finish_row(row, carry):
-            start = pl.multiple_of(row * edge, edge)
-            for half, dense in enumerate((near, far)):
-                for col in range(item_tiles):
-                    place = (half * half_tiles + row) * item_tiles + col
-                    dense[pl.ds(start, edge), col * edge : (col + 1) * edge] = total[
-                        place
-                    ].astype(jnp.bfloat16)
+        lax.fori_loop(0, half_tiles, finish_row, 0)
+        if half == 1:
+            row_copy(0, half_tiles - 1).start()
+    row_copy(1, half_tiles - 1).start()
+    for half in range(2):
+
+        def wait_row(row, carry):
+            row_copy(half, row).wait()
             return carry
 
-        lax.fori_loop(0, half_tiles, finish_row, 0)
+        lax.fori_loop(0, half_tiles, wait_row, 0)
 
 
 def dense_block(tile_block, row_ids, col_ids, norm_ids, count, user_rows, item_rows):
     slots, edge, _ = tile_block.shape
-    positions = (user_rows // edge) * (item_rows // edge)
+    user_tiles = user_rows // edge
+    positions = user_tiles * (item_rows // edge)
+    in_place = pl.BlockSpec(memory_space=pltpu.HBM)
     return pl.pallas_call(
         dense_kernel,
-        out_shape=[jax.ShapeDtypeStruct((user_rows // 2, item_rows), jnp.bfloat16)] * 2,
+        out_shape=[pltpu.HBM((user_rows // 2, item_rows), jnp.bfloat16)] * 2,
         grid_spec=pltpu.PrefetchScalarGridSpec(
             num_scalar_prefetch=4,
-            grid=(slots // slot_block,),
-            in_specs=[pl.BlockSpec((slot_block, edge, edge), lambda i, *_: (i, 0, 0))],
-            out_specs=[pl.BlockSpec((user_rows // 2, item_rows), lambda i, *_: (0, 0))] * 2,
-            scratch_shapes=[pltpu.VMEM((positions, edge, edge), jnp.float32)],
+            grid=(),
+            in_specs=[in_place],
+            out_specs=[in_place] * 2,
+            scratch_shapes=[
+                pltpu.VMEM((slots, edge, edge), jnp.bfloat16),
+                pltpu.VMEM((positions, edge, edge), jnp.float32),
+                pltpu.VMEM((user_rows, item_rows), jnp.bfloat16),
+                pltpu.SemaphoreType.DMA((slots // slot_block,)),
+                pltpu.SemaphoreType.DMA((user_tiles,)),
+            ],
         ),
-        compiler_params=pltpu.CompilerParams(
-            dimension_semantics=("arbitrary",), vmem_limit_bytes=24 << 20
-        ),
+        compiler_params=pltpu.CompilerParams(vmem_limit_bytes=24 << 20),
         cost_estimate=pl.CostEstimate(
             flops=4 * slots * edge * edge,
             bytes_accessed=2 * slots * edge * edge + 2 * user_rows * item_rows,
             transcendentals=0,
         ),
         name="dense_block",
-    )(
-        row_ids,
-        col_ids,
-        norm_ids,
-        count,
-        pltpu.with_memory_space_constraint(tile_block, pltpu.HBM),
-    )
+    )(row_ids, col_ids, norm_ids, count, in_main(tile_block))
+
+
+def join_kernel(mine, beside, pair):
+    rows = mine.shape[0]
+    pair[:rows] = mine[...]
+    pair[rows:] = beside[...]
+
+
+def join(mine, beside):
+    rows, width = mine.shape
+    return pl.pallas_call(
+        join_kernel, out_shape=jax.ShapeDtypeStruct((2 * rows, width), mine.dtype), name="join"
+    )(in_main(mine), in_main(beside))
+
+
+def assemble_kernel(*refs):
+    *parts, near, near_emb = refs
+    rows = parts[0].shape[0] // 4
+    for index, part in enumerate(parts):
+        for side in range(2):
+            out = pl.ds((2 * index + side) * rows, rows)
+            near[out] = part[pl.ds(2 * side * rows, rows)]
+            near_emb[out] = part[pl.ds((2 * side + 1) * rows, rows)]
+
+
+def assemble(parts):
+    rows, width = parts[0].shape
+    shape = jax.ShapeDtypeStruct((len(parts) * rows // 2, width), parts[0].dtype)
+    return pl.pallas_call(assemble_kernel, out_shape=[shape] * 2, name="assemble")(*map(in_main, parts))
 
 
 def lay_out_kernel(grad_user, user_emb, grad_item, item_emb, mine, pieces):
@@ -176,15 +241,13 @@
 
     mine, item_sent = lay_out(grad_user[0], user_emb[0], grad_item[0], item_emb[0])
     beside = partner(mine, side_bit)
-    pair = jnp.concatenate([mine, beside])
+    pair = join(mine, beside)
     own_rows = user_emb.shape[1]
     item_pieces = lax.all_to_all(item_sent, "au", split_axis=0, concat_axis=0, tiled=True)
     parts = [pair]
     for distance in range(1, ring):
         parts.append(from_ahead(pair, distance))
-    quarters = [part[i * own_rows : (i + 1) * own_rows] for part in parts for i in range(4)]
-    near = jnp.concatenate(quarters[0::2])
-    near_emb = jnp.concatenate(quarters[1::2])
+    near, near_emb = assemble(parts)
     far = partner(near, core_bit)
 
     items = item_pieces[:, 0].reshape(item_rows, width)

time: 132 us -> 151 us (1.14)
  waiting for transfers between devices: 25.8 us -> 44.8 us
  starting transfers between devices: 73.5 us -> 79 us
  local copies, waits for them, and re-layouts: 9.34 us -> 4.35 us
  Pallas kernels: 9.04 us -> 10.9 us
    ppermute x4, waiting for transfers between devices: 0.01 us -> 18.8 us  [partner(): lax.ppermute(value, 'ia', [(i, i ^ bit) for i in range(lax.axis_size('ia'...]
    unnamed x28, local copies, waits for them, and re-layouts: 7.29 us -> 2.94 us
    ppermute x4, starting transfers between devices: 22.1 us -> 18.5 us  [partner(): lax.ppermute(value, 'ia', [(i, i ^ bit) for i in range(lax.axis_size('ia'...]
    all_to_all x1, starting transfers between devices: 10.9 us -> 14.4 us  [device_step(): lax.all_to_all(item_sent, 'au', split_axis=0, concat_axis=0, tiled=True)]
    all_to_all x1, starting transfers between devices: 9.35 us -> 11.4 us  [device_step(): lax.all_to_all(pieces, 'au', split_axis=0, concat_axis=0, tiled=True)]
    pallas_call x1 -> x3, Pallas kernels: 7.05 us -> 8.9 us  [the longest x1 4.98 us: dense_block(): pl.pallas_call(dense_kernel, out_shape=[pltpu.HBM((user_rows // 2, item_r...]
    all_to_all x2, starting transfers between devices: 12.7 us -> 14.3 us  [from_everyone(): return lax.all_to_all(copies, axis, split_axis=0, concat_axis=0, tiled=True)]
  transfers between devices with their start and end apart: 14 -> 14, of which waited for: 4 -> 7; matrix products, arithmetic and copies ran while one was open for 11% -> 5% of each run, Pallas kernels for 5% -> 6%
where the time goes in v4:
time: 151 us; the launch traced here: 150 us
  starting transfers between devices  79 us (52%)
  waiting for transfers between devices  44.8 us (30%)
  Pallas kernels  10.9 us (7%)
  matrix products  7.82 us (5%)
  local copies, waits for them, and re-layouts  4.35 us (3%)
  other arithmetic  1.8 us (1%)
  between operations  1.65 us (1%)
    ppermute x4, waiting for transfers between devices, partner(): lax.ppermute(value, 'ia', [(i, i ^ bit) for i in range(lax.axis_size('ia'...  18.8 us
    ppermute x4, starting transfers between devices, partner(): lax.ppermute(value, 'ia', [(i, i ^ bit) for i in range(lax.axis_size('ia'...  18.5 us
    all_to_all x1, starting transfers between devices, device_step(): lax.all_to_all(item_sent, 'au', split_axis=0, concat_axis=0, tiled=True)  14.4 us
    all_to_all x2, starting transfers between devices, from_everyone(): return lax.all_to_all(copies, axis, split_axis=0, concat_axis=0, tiled=True)  14.3 us
    all_to_all x1, starting transfers between devices, device_step(): lax.all_to_all(pieces, 'au', split_axis=0, concat_axis=0, tiled=True)  11.4 us
    all_to_all x2, waiting for transfers between devices, from_everyone(): return lax.all_to_all(copies, axis, split_axis=0, concat_axis=0, tiled=True)  10.7 us
    ppermute x3, starting transfers between devices, from_ahead(): lax.ppermute(value, 'ia', [(ahead(i, distance), i) for i in range(size)])  10.5 us
    ppermute x3, starting transfers between devices, send_ahead(): lax.ppermute(value, 'ia', [(i, ahead(i, distance)) for i in range(size)])  9.9 us
  transfers between devices with their start and end apart: 14, of which 7 were waited for; matrix products, arithmetic and copies ran while one was open for 5% of the time, Pallas kernels for 6%

profile of v4, /device:TPU:1, one launch (start us, length us, event | category | flops | bytes accessed | tf_op | source)
XLA Modules:
  0.0 150.3 jit_solution(12461200464870676612)
XLA Ops:
  0.6 0.0 copy-start
  0.7 2.0 %lay_out.1 = (bf16[256,256]{1,0:T(8,128)(2,1)}, bf16[32,2,32,256]{3,2,1,0:T(8,128)(2,1)}) custom-call(bf16[128,256]{1,0:T(8,128)(2,1)} %bitcast.44, bf16[128,256]{1,0:T(8,128)(2,1)} %bitcast.45, bf16[32,256]{1,0:T(8,128)(2,1)} %bitcast.46, bf16[32,256]{1,0:T(8,128)(2,1)} %bitcast.47), custom_call_target="tpu_custom_call" | custom-call | tf_op jit(solution)/shard_map/lay_out/pallas_call | solution.py:206
  2.7 14.4 %all-to-all-start = ((bf16[32,2,32,256]{3,2,1,0:T(8,128)(2,1)}), bf16[32,2,32,256]{3,2,1,0:T(8,128)(2,1)S(1)}, u32[]{:S(2)}, u32[]{:S(2)}) async-start(bf16[32,2,32,256]{3,2,1,0:T(8,128)(2,1)} %get-tuple-element.10), calls=%async_computation | async-start | bytes 2097152 | tf_op jit(solution)/shard_map/all_to_all | solution.py:246
  17.1 4.8 %collective-permute-start.5 = (bf16[256,256]{1,0:T(8,128)(2,1)S(1)}, bf16[256,256]{1,0:T(8,128)(2,1)S(1)}, u32[]{:S(2)}, u32[]{:S(2)}) collective-permute-start(bf16[256,256]{1,0:T(8,128)(2,1)S(1)} %copy-done.8), channel_id=1, source_target_pairs={{0,2},{1,3},{2,0},{3,1},{4,6},{5,7},{6,4},{7,5},{8,10},{9,11},{10,... | collective-permute-start | bytes 393224 | tf_op jit(solution)/shard_map/ppermute | solution.py:23
  21.9 18.4 %collective-permute-done.5.beside = bf16[256,256]{1,0:T(8,128)(2,1)S(1)} collective-permute-done((bf16[256,256]{1,0:T(8,128)(2,1)S(1)}, bf16[256,256]{1,0:T(8,128)(2,1)S(1)}, u32[]{:S(2)}, u32[]{:S(2)}) %collective-permute-start.5) | collective-permute-done | bytes 131104 | tf_op jit(solution)/shard_map/ppermute | solution.py:23
  40.3 0.7 copy-done.9
  40.9 1.7 %join.1.refs_0_ = bf16[512,256]{1,0:T(8,128)(2,1)} custom-call(bf16[256,256]{1,0:T(8,128)(2,1)} %get-tuple-element.12.mine, bf16[256,256]{1,0:T(8,128)(2,1)} %copy-done.9), custom_call_target="tpu_custom_call" | custom-call | tf_op jit(solution)/shard_map/join/pallas_call | solution.py:174
  42.6 3.1 %collective-permute-start.8 = (bf16[512,256]{1,0:T(8,128)(2,1)}, bf16[512,256]{1,0:T(8,128)(2,1)S(1)}, u32[]{:S(2)}, u32[]{:S(2)}) collective-permute-start(bf16[512,256]{1,0:T(8,128)(2,1)} %join.1.refs_0_), channel_id=1, source_target_pairs={{12,0},{13,1},{14,2},{15,3},{0,4},{1,5},{2,6},{3,7},{4,8},{5,9},{6... | collective-permute-start | bytes 786440 | tf_op jit(solution)/shard_map/ppermute | solution.py:33
  45.7 4.4 %collective-permute-start.7 = (bf16[512,256]{1,0:T(8,128)(2,1)}, bf16[512,256]{1,0:T(8,128)(2,1)S(1)}, u32[]{:S(2)}, u32[]{:S(2)}) collective-permute-start(bf16[512,256]{1,0:T(8,128)(2,1)} %join.1.refs_0_), channel_id=1, source_target_pairs={{8,0},{9,1},{10,2},{11,3},{12,4},{13,5},{14,6},{15,7},{0,8},{1,9},... | collective-permute-start | bytes 786440 | tf_op jit(solution)/shard_map/ppermute | solution.py:33
  50.1 3.1 %collective-permute-start.6 = (bf16[512,256]{1,0:T(8,128)(2,1)}, bf16[512,256]{1,0:T(8,128)(2,1)S(1)}, u32[]{:S(2)}, u32[]{:S(2)}) collective-permute-start(bf16[512,256]{1,0:T(8,128)(2,1)} %join.1.refs_0_), channel_id=1, source_target_pairs={{4,0},{5,1},{6,2},{7,3},{8,4},{9,5},{10,6},{11,7},{12,8},{13,9},{1... | collective-permute-start | bytes 786440 | tf_op jit(solution)/shard_map/ppermute | solution.py:33
  53.2 0.0 collective-permute-done.8.refs_3_
  53.2 5.4 %collective-permute-done.7.refs_2_ = bf16[512,256]{1,0:T(8,128)(2,1)S(1)} collective-permute-done((bf16[512,256]{1,0:T(8,128)(2,1)}, bf16[512,256]{1,0:T(8,128)(2,1)S(1)}, u32[]{:S(2)}, u32[]{:S(2)}) %collective-permute-start.7) | collective-permute-done | bytes 262176 | tf_op jit(solution)/shard_map/ppermute | solution.py:33
  58.6 2.0 %collective-permute-done.6.refs_1_ = bf16[512,256]{1,0:T(8,128)(2,1)S(1)} collective-permute-done((bf16[512,256]{1,0:T(8,128)(2,1)}, bf16[512,256]{1,0:T(8,128)(2,1)S(1)}, u32[]{:S(2)}, u32[]{:S(2)}) %collective-permute-start.6) | collective-permute-done | bytes 262176 | tf_op jit(solution)/shard_map/ppermute | solution.py:33
  60.5 0.7 copy-done.7
  61.3 2.2 %assemble.1 = (bf16[1024,256]{1,0:T(8,128)(2,1)}, bf16[1024,256]{1,0:T(8,128)(2,1)}) custom-call(bf16[512,256]{1,0:T(8,128)(2,1)} %join.1.refs_0_, bf16[512,256]{1,0:T(8,128)(2,1)} %copy-done.7, bf16[512,256]{1,0:T(8,128)(2,1)} %copy-done.6, bf16[512,256]{1,0:T(8,128)(2,1)} %copy-done.5), custom_call_target="tpu_custom_call" | custom-call | tf_op jit(solution)/shard_map/assemble/pallas_call | solution.py:192
  63.5 4.1 %collective-permute-start.9 = (bf16[1024,256]{1,0:T(8,128)(2,1)}, bf16[1024,256]{1,0:T(8,128)(2,1)S(1)}, u32[]{:S(2)}, u32[]{:S(2)}) collective-permute-start(bf16[1024,256]{1,0:T(8,128)(2,1)} %get-tuple-element.13), channel_id=1, source_target_pairs={{0,1},{1,0},{2,3},{3,2},{4,5},{5,4},{6,7},{7,6},{8,9},{9,8},{10,11... | collective-permute-start | bytes 1572872 | tf_op jit(solution)/shard_map/ppermute | solution.py:23
  68.3 5.0 %dense_block.1 = (bf16[1024,1024]{1,0:T(8,128)(2,1)}, bf16[1024,1024]{1,0:T(8,128)(2,1)}) custom-call(s32[128]{0:T(128)S(1)} %add_bitcast_fusion.rows, s32[128]{0:T(128)S(1)} %bitcast.37, s32[128]{0:T(128)S(1)} %bitcast.38, s32[1]{0:T(128)} %bitcast.36.count, bf16[128,128,128]{2,1,0:T(8,128)(2,1)} %bitcast.39), custom_call_target="tpu_custom_call" | custom-call | flops 8388608 | bytes 8388608 | tf_op jit(solution)/shard_map/dense_block/pallas_call | solution.py:140
  73.3 3.3 %fusion.12 = f32[1024,256]{1,0:T(8,128)} fusion(bf16[1024,1024]{1,0:T(8,128)(2,1)} %get-tuple-element.11, bf16[1024,256]{1,0:T(8,128)(2,1)S(1)} %collective-permute-done.9), kind=kOutput, calls=%fused_computation.26 | convolution fusion | flops 536870912 | bytes 3670016 | tf_op jit(solution)/shard_map/ui,ud->id/dot_general | solution.py:217
  76.7 0.0 all-to-all-done
  76.7 0.1 fusion.10
  76.7 1.5 %copy-done.11 = bf16[1024,1024]{1,0:T(8,128)(2,1)S(1)} copy-done((bf16[1024,1024]{1,0:T(8,128)(2,1)S(1)}, bf16[1024,1024]{1,0:T(8,128)(2,1)}, u32[]{:S(2)}) %copy-start.11) | copy-done | bytes 2097176
  78.3 0.7 convolution_convert_fusion
  79.0 2.4 %collective-permute-start = (bf16[1024,256]{1,0:T(8,128)(2,1)S(1)}, bf16[1024,256]{1,0:T(8,128)(2,1)S(1)}, u32[]{:S(2)}, u32[]{:S(2)}) collective-permute-start(bf16[1024,256]{1,0:T(8,128)(2,1)S(1)} %convolution_convert_fusion), channel_id=1, source_target_pairs={{0,1},{1,0},{2,3},{3,2},{4,5},{5,4},{6,7},{7,6},{8,9},{9,8},{10,11... | collective-permute-start | bytes 1572872 | tf_op jit(solution)/shard_map/ppermute | solution.py:23
  81.4 0.8 fusion.1
  82.2 0.3 fusion.13
  82.5 0.4 collective-permute-done
  82.9 0.7 fusion.9
  83.6 0.3 fusion.3
  84.0 0.9 pad_maximum_fusion
  84.9 11.4 %all-to-all-start.1 = ((bf16[32,40,256]{2,1,0:T(8,128)(2,1)}), bf16[32,40,256]{2,1,0:T(8,128)(2,1)S(1)}, u32[]{:S(2)}, u32[]{:S(2)}) async-start(bf16[32,40,256]{2,1,0:T(8,128)(2,1)} %pad_maximum_fusion), calls=%async_computation.1 | async-start | bytes 1310720 | tf_op jit(solution)/shard_map/all_to_all | solution.py:284
  96.3 3.8 %collective-permute-start.1 = (bf16[256,256]{1,0:T(8,128)(2,1)S(1)}, bf16[256,256]{1,0:T(8,128)(2,1)S(1)}, u32[]{:S(2)}, u32[]{:S(2)}) collective-permute-start(bf16[256,256]{1,0:T(8,128)(2,1)S(1)} %get-tuple-element.19), channel_id=1, source_target_pairs={{0,4},{1,5},{2,6},{3,7},{4,8},{5,9},{6,10},{7,11},{8,12},{9,13},{1... | collective-permute-start | bytes 393224 | tf_op jit(solution)/shard_map/ppermute | solution.py:38
  100.1 2.7 %collective-permute-start.3 = (bf16[256,256]{1,0:T(8,128)(2,1)S(1)}, bf16[256,256]{1,0:T(8,128)(2,1)S(1)}, u32[]{:S(2)}, u32[]{:S(2)}) collective-permute-start(bf16[256,256]{1,0:T(8,128)(2,1)S(1)} %get-tuple-element.20), channel_id=1, source_target_pairs={{0,12},{1,13},{2,14},{3,15},{4,0},{5,1},{6,2},{7,3},{8,4},{9,5},{1... | collective-permute-start | bytes 393224 | tf_op jit(solution)/shard_map/ppermute | solution.py:38
  102.9 3.3 %collective-permute-start.2 = (bf16[256,256]{1,0:T(8,128)(2,1)S(1)}, bf16[256,256]{1,0:T(8,128)(2,1)S(1)}, u32[]{:S(2)}, u32[]{:S(2)}) collective-permute-start(bf16[256,256]{1,0:T(8,128)(2,1)S(1)} %get-tuple-element.21), channel_id=1, source_target_pairs={{0,8},{1,9},{2,10},{3,11},{4,12},{5,13},{6,14},{7,15},{8,0},{9,1},... | collective-permute-start | bytes 393224 | tf_op jit(solution)/shard_map/ppermute | solution.py:38
  106.2 8.0 %all-to-all-done.1 = bf16[32,40,256]{2,1,0:T(8,128)(2,1)S(1)} async-done(((bf16[32,40,256]{2,1,0:T(8,128)(2,1)}), bf16[32,40,256]{2,1,0:T(8,128)(2,1)S(1)}, u32[]{:S(2)}, u32[]{:S(2)}) %all-to-all-start.1) | async-done | bytes 655392 | tf_op jit(solution)/shard_map/all_to_all | solution.py:284
  114.3 0.1 reduce
  114.4 0.6 broadcast_in_dim.14
  115.0 9.1 %all-to-all-start.2 = ((bf16[16,8,256]{2,1,0:T(8,128)(2,1)}), bf16[16,8,256]{2,1,0:T(8,128)(2,1)S(1)}, u32[]{:S(2)}, u32[]{:S(2)}) async-start(bf16[16,8,256]{2,1,0:T(8,128)(2,1)} %broadcast_in_dim.14), calls=%async_computation.2 | async-start | bytes 131072 | tf_op jit(solution)/shard_map/all_to_all | solution.py:19
  124.1 0.0 collective-permute-done.1
  124.1 0.0 collective-permute-done.3
  124.1 0.1 slice_add_fusion
  124.2 7.2 %collective-permute-start.4 = (bf16[128,256]{1,0:T(8,128)(2,1)S(1)}, bf16[128,256]{1,0:T(8,128)(2,1)S(1)}, u32[]{:S(2)}, u32[]{:S(2)}) collective-permute-start(bf16[128,256]{1,0:T(8,128)(2,1)S(1)} %slice.65), channel_id=1, source_target_pairs={{0,2},{1,3},{2,0},{3,1},{4,6},{5,7},{6,4},{7,5},{8,10},{9,11},{10,... | collective-permute-start | bytes 196616 | tf_op jit(solution)/shard_map/ppermute | solution.py:23
  131.4 2.4 %all-to-all-done.2 = bf16[16,8,256]{2,1,0:T(8,128)(2,1)S(1)} async-done(((bf16[16,8,256]{2,1,0:T(8,128)(2,1)}), bf16[16,8,256]{2,1,0:T(8,128)(2,1)S(1)}, u32[]{:S(2)}, u32[]{:S(2)}) %all-to-all-start.2) | async-done | bytes 65568 | tf_op jit(solution)/shard_map/all_to_all | solution.py:19
  133.9 0.7 broadcast_in_dim.15
  134.5 5.2 %all-to-all-start.3 = ((bf16[32,8,256]{2,1,0:T(8,128)(2,1)}), bf16[32,8,256]{2,1,0:T(8,128)(2,1)S(1)}, u32[]{:S(2)}, u32[]{:S(2)}) async-start(bf16[32,8,256]{2,1,0:T(8,128)(2,1)} %broadcast_in_dim.15), calls=%async_computation.3 | async-start | bytes 262144 | tf_op jit(solution)/shard_map/all_to_all | solution.py:19
  139.8 0.8 fusion.4
  140.6 0.8 fusion.5
  141.4 8.2 %all-to-all-done.3 = bf16[32,8,256]{2,1,0:T(8,128)(2,1)S(1)} async-done(((bf16[32,8,256]{2,1,0:T(8,128)(2,1)}), bf16[32,8,256]{2,1,0:T(8,128)(2,1)S(1)}, u32[]{:S(2)}, u32[]{:S(2)}) %all-to-all-start.3) | async-done | bytes 131104 | tf_op jit(solution)/shard_map/all_to_all | solution.py:19
  149.6 0.7 bitcast_convert_fusion
  (33 shorter events, 0.1 us)
Async XLA Ops:
  0.6 139.1 %copy-start = (bf16[256,256]{1,0:T(8,128)(2,1)S(1)}, bf16[256,256]{1,0:T(8,128)(2,1)}, u32[]{:S(2)}) copy-start(bf16[256,256]{1,0:T(8,128)(2,1)} %param.12) | copy-start | bytes 393220
  0.6 67.6 %copy-start.10 = (s32[1,128]{1,0:T(1,128)S(1)}, s32[1,128]{1,0:T(1,128)}, u32[]{:S(2)}) copy-start(s32[1,128]{1,0:T(1,128)} %param.16) | copy-start | bytes 1540
  0.7 67.7 %copy-start.2 = (s32[1,128]{1,0:T(1,128)S(1)}, s32[1,128]{1,0:T(1,128)}, u32[]{:S(2)}) copy-start(s32[1,128]{1,0:T(1,128)} %param.18) | copy-start | bytes 1540
  0.7 67.7 %copy-start.1 = (s32[1,128]{1,0:T(1,128)S(1)}, s32[1,128]{1,0:T(1,128)}, u32[]{:S(2)}) copy-start(s32[1,128]{1,0:T(1,128)} %param.17) | copy-start | bytes 1540
  2.7 14.4 %copy-start.8 = (bf16[256,256]{1,0:T(8,128)(2,1)S(1)}, bf16[256,256]{1,0:T(8,128)(2,1)}, u32[]{:S(2)}) copy-start(bf16[256,256]{1,0:T(8,128)(2,1)} %get-tuple-element.12.mine) | copy-start | bytes 393220
  2.7 74.0 %all-to-all-start = ((bf16[32,2,32,256]{3,2,1,0:T(8,128)(2,1)}), bf16[32,2,32,256]{3,2,1,0:T(8,128)(2,1)S(1)}, u32[]{:S(2)}, u32[]{:S(2)}) async-start(bf16[32,2,32,256]{3,2,1,0:T(8,128)(2,1)} %get-tuple-element.10), calls=%async_computation | async-start | bytes 2097152 | tf_op jit(solution)/shard_map/all_to_all | solution.py:246
  17.1 23.2 %collective-permute-start.5 = (bf16[256,256]{1,0:T(8,128)(2,1)S(1)}, bf16[256,256]{1,0:T(8,128)(2,1)S(1)}, u32[]{:S(2)}, u32[]{:S(2)}) collective-permute-start(bf16[256,256]{1,0:T(8,128)(2,1)S(1)} %copy-done.8), channel_id=1, source_target_pairs={{0,2},{1,3},{2,0},{3,1},{4,6},{5,7},{6,4},{7,5},{8,10},{9,11},{10,... | collective-permute-start | bytes 393224 | tf_op jit(solution)/shard_map/ppermute | solution.py:23
  40.3 0.7 copy-start.9
  42.6 10.6 %collective-permute-start.8 = (bf16[512,256]{1,0:T(8,128)(2,1)}, bf16[512,256]{1,0:T(8,128)(2,1)S(1)}, u32[]{:S(2)}, u32[]{:S(2)}) collective-permute-start(bf16[512,256]{1,0:T(8,128)(2,1)} %join.1.refs_0_), channel_id=1, source_target_pairs={{12,0},{13,1},{14,2},{15,3},{0,4},{1,5},{2,6},{3,7},{4,8},{5,9},{6... | collective-permute-start | bytes 786440 | tf_op jit(solution)/shard_map/ppermute | solution.py:33
  45.7 12.8 %collective-permute-start.7 = (bf16[512,256]{1,0:T(8,128)(2,1)}, bf16[512,256]{1,0:T(8,128)(2,1)S(1)}, u32[]{:S(2)}, u32[]{:S(2)}) collective-permute-start(bf16[512,256]{1,0:T(8,128)(2,1)} %join.1.refs_0_), channel_id=1, source_target_pairs={{8,0},{9,1},{10,2},{11,3},{12,4},{13,5},{14,6},{15,7},{0,8},{1,9},... | collective-permute-start | bytes 786440 | tf_op jit(solution)/shard_map/ppermute | solution.py:33
  50.1 10.4 %collective-permute-start.6 = (bf16[512,256]{1,0:T(8,128)(2,1)}, bf16[512,256]{1,0:T(8,128)(2,1)S(1)}, u32[]{:S(2)}, u32[]{:S(2)}) collective-permute-start(bf16[512,256]{1,0:T(8,128)(2,1)} %join.1.refs_0_), channel_id=1, source_target_pairs={{4,0},{5,1},{6,2},{7,3},{8,4},{9,5},{10,6},{11,7},{12,8},{13,9},{1... | collective-permute-start | bytes 786440 | tf_op jit(solution)/shard_map/ppermute | solution.py:33
  53.2 7.3 %copy-start.5 = (bf16[512,256]{1,0:T(8,128)(2,1)}, bf16[512,256]{1,0:T(8,128)(2,1)S(1)}, u32[]{:S(2)}) copy-start(bf16[512,256]{1,0:T(8,128)(2,1)S(1)} %collective-permute-done.8.refs_3_) | copy-start | bytes 786436
  58.6 2.0 %copy-start.6 = (bf16[512,256]{1,0:T(8,128)(2,1)}, bf16[512,256]{1,0:T(8,128)(2,1)S(1)}, u32[]{:S(2)}) copy-start(bf16[512,256]{1,0:T(8,128)(2,1)S(1)} %collective-permute-done.7.refs_2_) | copy-start | bytes 786436
  60.5 0.7 copy-start.7
  63.5 9.8 %collective-permute-start.9 = (bf16[1024,256]{1,0:T(8,128)(2,1)}, bf16[1024,256]{1,0:T(8,128)(2,1)S(1)}, u32[]{:S(2)}, u32[]{:S(2)}) collective-permute-start(bf16[1024,256]{1,0:T(8,128)(2,1)} %get-tuple-element.13), channel_id=1, source_target_pairs={{0,1},{1,0},{2,3},{3,2},{4,5},{5,4},{6,7},{7,6},{8,9},{9,8},{10,11... | collective-permute-start | bytes 1572872 | tf_op jit(solution)/shard_map/ppermute | solution.py:23
  76.7 1.6 %copy-start.11 = (bf16[1024,1024]{1,0:T(8,128)(2,1)S(1)}, bf16[1024,1024]{1,0:T(8,128)(2,1)}, u32[]{:S(2)}) copy-start(bf16[1024,1024]{1,0:T(8,128)(2,1)} %get-tuple-element.11) | copy-start | bytes 6291460
  78.3 3.1 %copy-start.3 = (bf16[1024,1024]{1,0:T(8,128)(2,1)S(1)}, bf16[1024,1024]{1,0:T(8,128)(2,1)}, u32[]{:S(2)}) copy-start(bf16[1024,1024]{1,0:T(8,128)(2,1)} %get-tuple-element.9) | copy-start | bytes 6291460
  78.3 3.1 %copy-start.12 = (bf16[1024,256]{1,0:T(8,128)(2,1)S(1)}, bf16[1024,256]{1,0:T(8,128)(2,1)}, u32[]{:S(2)}) copy-start(bf16[1024,256]{1,0:T(8,128)(2,1)} %get-tuple-element.13) | copy-start | bytes 1572868
  78.3 3.2 %copy-start.13 = (f32[1024,256]{1,0:T(8,128)S(1)}, f32[1024,256]{1,0:T(8,128)}, u32[]{:S(2)}) copy-start(f32[1024,256]{1,0:T(8,128)} %fusion.12) | copy-start | bytes 3145732
  79.0 3.9 %collective-permute-start = (bf16[1024,256]{1,0:T(8,128)(2,1)S(1)}, bf16[1024,256]{1,0:T(8,128)(2,1)S(1)}, u32[]{:S(2)}, u32[]{:S(2)}) collective-permute-start(bf16[1024,256]{1,0:T(8,128)(2,1)S(1)} %convolution_convert_fusion), channel_id=1, source_target_pairs={{0,1},{1,0},{2,3},{3,2},{4,5},{5,4},{6,7},{7,6},{8,9},{9,8},{10,11... | collective-permute-start | bytes 1572872 | tf_op jit(solution)/shard_map/ppermute | solution.py:23
  82.5 1.1 copy-start.4
  84.9 29.4 %all-to-all-start.1 = ((bf16[32,40,256]{2,1,0:T(8,128)(2,1)}), bf16[32,40,256]{2,1,0:T(8,128)(2,1)S(1)}, u32[]{:S(2)}, u32[]{:S(2)}) async-start(bf16[32,40,256]{2,1,0:T(8,128)(2,1)} %pad_maximum_fusion), calls=%async_computation.1 | async-start | bytes 1310720 | tf_op jit(solution)/shard_map/all_to_all | solution.py:284
  96.3 27.8 %collective-permute-start.1 = (bf16[256,256]{1,0:T(8,128)(2,1)S(1)}, bf16[256,256]{1,0:T(8,128)(2,1)S(1)}, u32[]{:S(2)}, u32[]{:S(2)}) collective-permute-start(bf16[256,256]{1,0:T(8,128)(2,1)S(1)} %get-tuple-element.19), channel_id=1, source_target_pairs={{0,4},{1,5},{2,6},{3,7},{4,8},{5,9},{6,10},{7,11},{8,12},{9,13},{1... | collective-permute-start | bytes 393224 | tf_op jit(solution)/shard_map/ppermute | solution.py:38
  100.1 24.0 %collective-permute-start.3 = (bf16[256,256]{1,0:T(8,128)(2,1)S(1)}, bf16[256,256]{1,0:T(8,128)(2,1)S(1)}, u32[]{:S(2)}, u32[]{:S(2)}) collective-permute-start(bf16[256,256]{1,0:T(8,128)(2,1)S(1)} %get-tuple-element.20), channel_id=1, source_target_pairs={{0,12},{1,13},{2,14},{3,15},{4,0},{5,1},{6,2},{7,3},{8,4},{9,5},{1... | collective-permute-start | bytes 393224 | tf_op jit(solution)/shard_map/ppermute | solution.py:38
  102.9 21.2 %collective-permute-start.2 = (bf16[256,256]{1,0:T(8,128)(2,1)S(1)}, bf16[256,256]{1,0:T(8,128)(2,1)S(1)}, u32[]{:S(2)}, u32[]{:S(2)}) collective-permute-start(bf16[256,256]{1,0:T(8,128)(2,1)S(1)} %get-tuple-element.21), channel_id=1, source_target_pairs={{0,8},{1,9},{2,10},{3,11},{4,12},{5,13},{6,14},{7,15},{8,0},{9,1},... | collective-permute-start | bytes 393224 | tf_op jit(solution)/shard_map/ppermute | solution.py:38
  115.0 18.8 %all-to-all-start.2 = ((bf16[16,8,256]{2,1,0:T(8,128)(2,1)}), bf16[16,8,256]{2,1,0:T(8,128)(2,1)S(1)}, u32[]{:S(2)}, u32[]{:S(2)}) async-start(bf16[16,8,256]{2,1,0:T(8,128)(2,1)} %broadcast_in_dim.14), calls=%async_computation.2 | async-start | bytes 131072 | tf_op jit(solution)/shard_map/all_to_all | solution.py:19
  124.2 15.5 %collective-permute-start.4 = (bf16[128,256]{1,0:T(8,128)(2,1)S(1)}, bf16[128,256]{1,0:T(8,128)(2,1)S(1)}, u32[]{:S(2)}, u32[]{:S(2)}) collective-permute-start(bf16[128,256]{1,0:T(8,128)(2,1)S(1)} %slice.65), channel_id=1, source_target_pairs={{0,2},{1,3},{2,0},{3,1},{4,6},{5,7},{6,4},{7,5},{8,10},{9,11},{10,... | collective-permute-start | bytes 196616 | tf_op jit(solution)/shard_map/ppermute | solution.py:23
  134.5 15.1 %all-to-all-start.3 = ((bf16[32,8,256]{2,1,0:T(8,128)(2,1)}), bf16[32,8,256]{2,1,0:T(8,128)(2,1)S(1)}, u32[]{:S(2)}, u32[]{:S(2)}) async-start(bf16[32,8,256]{2,1,0:T(8,128)(2,1)} %broadcast_in_dim.15), calls=%async_computation.3 | async-start | bytes 262144 | tf_op jit(solution)/shard_map/all_to_all | solution.py:19

commit v5 on v4

--- a/solution.py
+++ b/solution.py
@@ -249,6 +249,7 @@
         parts.append(from_ahead(pair, distance))
     near, near_emb = assemble(parts)
     far = partner(near, core_bit)
+    far_emb = partner(near_emb, core_bit)
 
     items = item_pieces[:, 0].reshape(item_rows, width)
     item_table = item_pieces[:, 1].reshape(item_rows, width)
@@ -264,13 +265,13 @@
     )
     user_far = product("ui,id->ud", dense_far, items).astype(low)
     user_near = product("ui,id->ud", dense_near, items).astype(low)
-    user_sum = wide(user_near) + wide(partner(user_far, core_bit))
-    user_sent = user_sum.astype(low)
-
+    user_far, user_near = lax.optimization_barrier((user_far, user_near))
     item_part = product("ui,ud->id", dense_near, near) + product("ui,ud->id", dense_far, far)
     item_part = item_part.astype(low)
-    weight_part = product("rd,re->de", near_emb, user_sent) + product(
-        "rd,re->de", item_table, item_part
+    weight_part = (
+        product("rd,re->de", near_emb, user_near)
+        + product("rd,re->de", far_emb, user_far)
+        + product("rd,re->de", item_table, item_part)
     )
 
     peers = lax.axis_size("au")
@@ -281,7 +282,8 @@
         ],
         axis=1,
     )
-    arrived = summed(lax.all_to_all(pieces, "au", split_axis=0, concat_axis=0, tiled=True))
+    arrived = lax.all_to_all(pieces, "au", split_axis=0, concat_axis=0, tiled=True)
+    arrived = summed(arrived)
     q_item = arrived[: item_rows // peers]
     strip = summed(from_everyone(arrived[item_rows // peers :].astype(low), "ia"))
     user_count = user_rows * lax.axis_size("au")
@@ -289,8 +291,9 @@
     strip = strip / math.sqrt(user_count + item_count)
     grad_weight = wide(from_everyone(strip.astype(low), "au")).reshape(width, width)
 
-    along = user_sum.reshape(ring, user_rows // (2 * ring), width)
-    sent = user_sent.reshape(along.shape)
+    across = partner(user_far, core_bit)
+    along = (wide(user_near) + wide(across)).reshape(ring, user_rows // (2 * ring), width)
+    sent = along.astype(low)
     both = along[0] + sum(wide(send_ahead(sent[d], d)) for d in range(1, ring))
     q_user = both[:own_rows] + wide(partner(both[own_rows:].astype(low), side_bit))
 

time: 151 us -> 151 us (level)
  starting transfers between devices: 79 us -> 75.4 us
  waiting for transfers between devices: 44.8 us -> 47.5 us
    ppermute x3, waiting for transfers between devices: 7.34 us -> 11.6 us  [from_ahead(): lax.ppermute(value, 'ia', [(ahead(i, distance), i) for i in range(size)])]
    all_to_all x1, waiting for transfers between devices: 8.02 us -> 5.27 us  [device_step(): lax.all_to_all(pieces, 'au', split_axis=0, concat_axis=0, tiled=True)]
    all_to_all x2, starting transfers between devices: 14.3 us -> 12.1 us  [from_everyone(): return lax.all_to_all(copies, axis, split_axis=0, concat_axis=0, tiled=True)]
    ppermute x4 -> x5, starting transfers between devices: 18.5 us -> 20 us  [partner(): lax.ppermute(value, 'ia', [(i, i ^ bit) for i in range(lax.axis_size('ia'...]
    ppermute x4 -> x5, waiting for transfers between devices: 18.8 us -> 19.9 us  [partner(): lax.ppermute(value, 'ia', [(i, i ^ bit) for i in range(lax.axis_size('ia'...]
    dot_general x8 -> x9, matrix products: 7.82 us -> 7.3 us  [product(): return jnp.einsum(spec, left, right, preferred_element_type=jnp.float32)]
  transfers between devices with their start and end apart: 14 -> 15, of which waited for: 7 -> 7; matrix products, arithmetic and copies ran while one was open for 5% -> 6% of each run, Pallas kernels for 6% -> 6%
where the time goes in v5:
time: 151 us; the launch traced here: 150 us
  starting transfers between devices  75.4 us (50%)
  waiting for transfers between devices  47.5 us (31%)
  Pallas kernels  10.9 us (7%)
  matrix products  7.3 us (5%)
  local copies, waits for them, and re-layouts  5.21 us (3%)
  other arithmetic  1.91 us (1%)
  between operations  1.71 us (1%)
    ppermute x5, starting transfers between devices, partner(): lax.ppermute(value, 'ia', [(i, i ^ bit) for i in range(lax.axis_size('ia'...  20 us
    ppermute x5, waiting for transfers between devices, partner(): lax.ppermute(value, 'ia', [(i, i ^ bit) for i in range(lax.axis_size('ia'...  19.9 us
    all_to_all x1, starting transfers between devices, device_step(): lax.all_to_all(item_sent, 'au', split_axis=0, concat_axis=0, tiled=True)  14.4 us
    all_to_all x2, starting transfers between devices, from_everyone(): return lax.all_to_all(copies, axis, split_axis=0, concat_axis=0, tiled=True)  12.1 us
    ppermute x3, waiting for transfers between devices, from_ahead(): lax.ppermute(value, 'ia', [(ahead(i, distance), i) for i in range(size)])  11.6 us
    all_to_all x1, starting transfers between devices, device_step(): lax.all_to_all(pieces, 'au', split_axis=0, concat_axis=0, tiled=True)  11.2 us
    all_to_all x2, waiting for transfers between devices, from_everyone(): return lax.all_to_all(copies, axis, split_axis=0, concat_axis=0, tiled=True)  10.7 us
    ppermute x3, starting transfers between devices, from_ahead(): lax.ppermute(value, 'ia', [(ahead(i, distance), i) for i in range(size)])  9.32 us
  transfers between devices with their start and end apart: 15, of which 7 were waited for; matrix products, arithmetic and copies ran while one was open for 6% of the time, Pallas kernels for 6%

profile of v5, /device:TPU:1, one launch (start us, length us, event | category | flops | bytes accessed | tf_op | source)
XLA Modules:
  0.0 149.9 jit_solution(5388660266859787469)
XLA Ops:
  0.6 0.0 copy-start
  0.7 2.0 %lay_out.1 = (bf16[256,256]{1,0:T(8,128)(2,1)}, bf16[32,2,32,256]{3,2,1,0:T(8,128)(2,1)}) custom-call(bf16[128,256]{1,0:T(8,128)(2,1)} %bitcast.46, bf16[128,256]{1,0:T(8,128)(2,1)} %bitcast.47, bf16[32,256]{1,0:T(8,128)(2,1)} %bitcast.48, bf16[32,256]{1,0:T(8,128)(2,1)} %bitcast.49), custom_call_target="tpu_custom_call" | custom-call | tf_op jit(solution)/shard_map/lay_out/pallas_call | solution.py:206
  2.7 14.4 %all-to-all-start = ((bf16[32,2,32,256]{3,2,1,0:T(8,128)(2,1)}), bf16[32,2,32,256]{3,2,1,0:T(8,128)(2,1)S(1)}, u32[]{:S(2)}, u32[]{:S(2)}) async-start(bf16[32,2,32,256]{3,2,1,0:T(8,128)(2,1)} %get-tuple-element.12), calls=%async_computation | async-start | bytes 2097152 | tf_op jit(solution)/shard_map/all_to_all | solution.py:246
  17.1 4.8 %collective-permute-start.5 = (bf16[256,256]{1,0:T(8,128)(2,1)S(1)}, bf16[256,256]{1,0:T(8,128)(2,1)S(1)}, u32[]{:S(2)}, u32[]{:S(2)}) collective-permute-start(bf16[256,256]{1,0:T(8,128)(2,1)S(1)} %copy-done.7), channel_id=1, source_target_pairs={{0,2},{1,3},{2,0},{3,1},{4,6},{5,7},{6,4},{7,5},{8,10},{9,11},{10,... | collective-permute-start | bytes 393224 | tf_op jit(solution)/shard_map/ppermute | solution.py:23
  21.9 18.4 %collective-permute-done.5.beside = bf16[256,256]{1,0:T(8,128)(2,1)S(1)} collective-permute-done((bf16[256,256]{1,0:T(8,128)(2,1)S(1)}, bf16[256,256]{1,0:T(8,128)(2,1)S(1)}, u32[]{:S(2)}, u32[]{:S(2)}) %collective-permute-start.5) | collective-permute-done | bytes 131104 | tf_op jit(solution)/shard_map/ppermute | solution.py:23
  40.3 0.6 copy-done.8
  40.9 1.7 %join.1.refs_0_ = bf16[512,256]{1,0:T(8,128)(2,1)} custom-call(bf16[256,256]{1,0:T(8,128)(2,1)} %get-tuple-element.16.mine, bf16[256,256]{1,0:T(8,128)(2,1)} %copy-done.8), custom_call_target="tpu_custom_call" | custom-call | tf_op jit(solution)/shard_map/join/pallas_call | solution.py:174
  42.6 4.4 %collective-permute-start.6 = (bf16[512,256]{1,0:T(8,128)(2,1)}, bf16[512,256]{1,0:T(8,128)(2,1)S(1)}, u32[]{:S(2)}, u32[]{:S(2)}) collective-permute-start(bf16[512,256]{1,0:T(8,128)(2,1)} %join.1.refs_0_), channel_id=1, source_target_pairs={{4,0},{5,1},{6,2},{7,3},{8,4},{9,5},{10,6},{11,7},{12,8},{13,9},{1... | collective-permute-start | bytes 786440 | tf_op jit(solution)/shard_map/ppermute | solution.py:33
  47.0 2.4 %collective-permute-start.7 = (bf16[512,256]{1,0:T(8,128)(2,1)}, bf16[512,256]{1,0:T(8,128)(2,1)S(1)}, u32[]{:S(2)}, u32[]{:S(2)}) collective-permute-start(bf16[512,256]{1,0:T(8,128)(2,1)} %join.1.refs_0_), channel_id=1, source_target_pairs={{8,0},{9,1},{10,2},{11,3},{12,4},{13,5},{14,6},{15,7},{0,8},{1,9},... | collective-permute-start | bytes 786440 | tf_op jit(solution)/shard_map/ppermute | solution.py:33
  49.5 2.5 %collective-permute-start.8 = (bf16[512,256]{1,0:T(8,128)(2,1)}, bf16[512,256]{1,0:T(8,128)(2,1)S(1)}, u32[]{:S(2)}, u32[]{:S(2)}) collective-permute-start(bf16[512,256]{1,0:T(8,128)(2,1)} %join.1.refs_0_), channel_id=1, source_target_pairs={{12,0},{13,1},{14,2},{15,3},{0,4},{1,5},{2,6},{3,7},{4,8},{5,9},{6... | collective-permute-start | bytes 786440 | tf_op jit(solution)/shard_map/ppermute | solution.py:33
  52.0 4.4 %collective-permute-done.7.refs_2_ = bf16[512,256]{1,0:T(8,128)(2,1)S(1)} collective-permute-done((bf16[512,256]{1,0:T(8,128)(2,1)}, bf16[512,256]{1,0:T(8,128)(2,1)S(1)}, u32[]{:S(2)}, u32[]{:S(2)}) %collective-permute-start.7) | collective-permute-done | bytes 262176 | tf_op jit(solution)/shard_map/ppermute | solution.py:33
  56.4 7.2 %collective-permute-done.8.refs_3_ = bf16[512,256]{1,0:T(8,128)(2,1)S(1)} collective-permute-done((bf16[512,256]{1,0:T(8,128)(2,1)}, bf16[512,256]{1,0:T(8,128)(2,1)S(1)}, u32[]{:S(2)}, u32[]{:S(2)}) %collective-permute-start.8) | collective-permute-done | bytes 262176 | tf_op jit(solution)/shard_map/ppermute | solution.py:33
  63.6 0.7 copy-done.6
  64.3 2.3 %assemble.1 = (bf16[1024,256]{1,0:T(8,128)(2,1)}, bf16[1024,256]{1,0:T(8,128)(2,1)}) custom-call(bf16[512,256]{1,0:T(8,128)(2,1)} %join.1.refs_0_, bf16[512,256]{1,0:T(8,128)(2,1)} %copy-done.4, bf16[512,256]{1,0:T(8,128)(2,1)} %copy-done.5, bf16[512,256]{1,0:T(8,128)(2,1)} %copy-done.6), custom_call_target="tpu_custom_call" | custom-call | tf_op jit(solution)/shard_map/assemble/pallas_call | solution.py:192
  66.6 3.3 %collective-permute-start.9 = (bf16[1024,256]{1,0:T(8,128)(2,1)}, bf16[1024,256]{1,0:T(8,128)(2,1)S(1)}, u32[]{:S(2)}, u32[]{:S(2)}) collective-permute-start(bf16[1024,256]{1,0:T(8,128)(2,1)} %get-tuple-element.17), channel_id=1, source_target_pairs={{0,1},{1,0},{2,3},{3,2},{4,5},{5,4},{6,7},{7,6},{8,9},{9,8},{10,11... | collective-permute-start | bytes 1572872 | tf_op jit(solution)/shard_map/ppermute | solution.py:23
  70.5 5.0 %dense_block.1 = (bf16[1024,1024]{1,0:T(8,128)(2,1)}, bf16[1024,1024]{1,0:T(8,128)(2,1)}) custom-call(s32[128]{0:T(128)S(1)} %add_bitcast_fusion.rows, s32[128]{0:T(128)S(1)} %bitcast.39, s32[128]{0:T(128)S(1)} %bitcast.40, s32[1]{0:T(128)} %bitcast.38.count, bf16[128,128,128]{2,1,0:T(8,128)(2,1)} %bitcast.41), custom_call_target="tpu_custom_call" | custom-call | flops 8388608 | bytes 8388608 | tf_op jit(solution)/shard_map/dense_block/pallas_call | solution.py:140
  75.5 2.3 %collective-permute-start.10 = (bf16[1024,256]{1,0:T(8,128)(2,1)S(1)}, bf16[1024,256]{1,0:T(8,128)(2,1)S(1)}, u32[]{:S(2)}, u32[]{:S(2)}) collective-permute-start(bf16[1024,256]{1,0:T(8,128)(2,1)S(1)} %copy-done.3), channel_id=1, source_target_pairs={{0,1},{1,0},{2,3},{3,2},{4,5},{5,4},{6,7},{7,6},{8,9},{9,8},{10,11... | collective-permute-start | bytes 1572872 | tf_op jit(solution)/shard_map/ppermute | solution.py:23
  77.9 2.5 %fusion.12 = f32[1024,256]{1,0:T(8,128)S(1)} fusion(bf16[1024,1024]{1,0:T(8,128)(2,1)} %get-tuple-element.11, bf16[1024,256]{1,0:T(8,128)(2,1)S(1)} %collective-permute-done.9), kind=kOutput, calls=%fused_computation.26 | convolution fusion | flops 536870912 | bytes 3670016 | tf_op jit(solution)/shard_map/ui,ud->id/dot_general | solution.py:217
  80.4 0.8 fusion
  81.2 0.1 fusion.10
  81.2 1.5 %copy-done.12 = bf16[1024,1024]{1,0:T(8,128)(2,1)S(1)} copy-done((bf16[1024,1024]{1,0:T(8,128)(2,1)S(1)}, bf16[1024,1024]{1,0:T(8,128)(2,1)}, u32[]{:S(2)}) %copy-start.12) | copy-done | bytes 2097176
  82.8 0.7 convolution_convert_fusion
  83.5 0.9 copy-done.10
  84.3 0.7 convolution_convert_fusion.1
  85.1 0.3 fusion.14
  85.4 0.3 fusion.13
  85.7 0.3 fusion.3
  86.1 0.9 pad_maximum_fusion
  87.0 11.2 %all-to-all-start.1 = ((bf16[32,40,256]{2,1,0:T(8,128)(2,1)}), bf16[32,40,256]{2,1,0:T(8,128)(2,1)S(1)}, u32[]{:S(2)}, u32[]{:S(2)}) async-start(bf16[32,40,256]{2,1,0:T(8,128)(2,1)} %pad_maximum_fusion), calls=%async_computation.1 | async-start | bytes 1310720 | tf_op jit(solution)/shard_map/all_to_all | solution.py:285
  98.1 2.5 %collective-permute-start = (bf16[1024,256]{1,0:T(8,128)(2,1)S(1)}, bf16[1024,256]{1,0:T(8,128)(2,1)S(1)}, u32[]{:S(2)}, u32[]{:S(2)}) collective-permute-start(bf16[1024,256]{1,0:T(8,128)(2,1)S(1)} %convolution_convert_fusion.1), channel_id=1, source_target_pairs={{0,1},{1,0},{2,3},{3,2},{4,5},{5,4},{6,7},{7,6},{8,9},{9,8},{10,11... | collective-permute-start | bytes 1572872 | tf_op jit(solution)/shard_map/ppermute | solution.py:23
  100.7 1.5 %collective-permute-done = bf16[1024,256]{1,0:T(8,128)(2,1)S(1)} collective-permute-done((bf16[1024,256]{1,0:T(8,128)(2,1)S(1)}, bf16[1024,256]{1,0:T(8,128)(2,1)S(1)}, u32[]{:S(2)}, u32[]{:S(2)}) %collective-permute-start) | collective-permute-done | bytes 524320 | tf_op jit(solution)/shard_map/ppermute | solution.py:23
  102.2 0.1 fusion.9
  102.3 1.9 %collective-permute-start.1 = (bf16[256,256]{1,0:T(8,128)(2,1)S(1)}, bf16[256,256]{1,0:T(8,128)(2,1)S(1)}, u32[]{:S(2)}, u32[]{:S(2)}) collective-permute-start(bf16[256,256]{1,0:T(8,128)(2,1)S(1)} %get-tuple-element.23), channel_id=1, source_target_pairs={{0,4},{1,5},{2,6},{3,7},{4,8},{5,9},{6,10},{7,11},{8,12},{9,13},{1... | collective-permute-start | bytes 393224 | tf_op jit(solution)/shard_map/ppermute | solution.py:38
  104.3 3.7 %collective-permute-start.2 = (bf16[256,256]{1,0:T(8,128)(2,1)S(1)}, bf16[256,256]{1,0:T(8,128)(2,1)S(1)}, u32[]{:S(2)}, u32[]{:S(2)}) collective-permute-start(bf16[256,256]{1,0:T(8,128)(2,1)S(1)} %get-tuple-element.25), channel_id=1, source_target_pairs={{0,8},{1,9},{2,10},{3,11},{4,12},{5,13},{6,14},{7,15},{8,0},{9,1},... | collective-permute-start | bytes 393224 | tf_op jit(solution)/shard_map/ppermute | solution.py:38
  108.0 2.8 %collective-permute-start.3 = (bf16[256,256]{1,0:T(8,128)(2,1)S(1)}, bf16[256,256]{1,0:T(8,128)(2,1)S(1)}, u32[]{:S(2)}, u32[]{:S(2)}) collective-permute-start(bf16[256,256]{1,0:T(8,128)(2,1)S(1)} %get-tuple-element.24), channel_id=1, source_target_pairs={{0,12},{1,13},{2,14},{3,15},{4,0},{5,1},{6,2},{7,3},{8,4},{9,5},{1... | collective-permute-start | bytes 393224 | tf_op jit(solution)/shard_map/ppermute | solution.py:38
  110.8 5.3 %all-to-all-done.1 = bf16[32,40,256]{2,1,0:T(8,128)(2,1)S(1)} async-done(((bf16[32,40,256]{2,1,0:T(8,128)(2,1)}), bf16[32,40,256]{2,1,0:T(8,128)(2,1)S(1)}, u32[]{:S(2)}, u32[]{:S(2)}) %all-to-all-start.1) | async-done | bytes 655392 | tf_op jit(solution)/shard_map/all_to_all | solution.py:285
  116.0 0.1 reduce
  116.2 0.6 broadcast_in_dim.14
  116.8 7.0 %all-to-all-start.2 = ((bf16[16,8,256]{2,1,0:T(8,128)(2,1)}), bf16[16,8,256]{2,1,0:T(8,128)(2,1)S(1)}, u32[]{:S(2)}, u32[]{:S(2)}) async-start(bf16[16,8,256]{2,1,0:T(8,128)(2,1)} %broadcast_in_dim.14), calls=%async_computation.2 | async-start | bytes 131072 | tf_op jit(solution)/shard_map/all_to_all | solution.py:19
  123.9 0.1 slice_add_fusion
  123.9 7.2 %collective-permute-start.4 = (bf16[128,256]{1,0:T(8,128)(2,1)S(1)}, bf16[128,256]{1,0:T(8,128)(2,1)S(1)}, u32[]{:S(2)}, u32[]{:S(2)}) collective-permute-start(bf16[128,256]{1,0:T(8,128)(2,1)S(1)} %slice.65), channel_id=1, source_target_pairs={{0,2},{1,3},{2,0},{3,1},{4,6},{5,7},{6,4},{7,5},{8,10},{9,11},{10,... | collective-permute-start | bytes 196616 | tf_op jit(solution)/shard_map/ppermute | solution.py:23
  131.1 2.4 %all-to-all-done.2 = bf16[16,8,256]{2,1,0:T(8,128)(2,1)S(1)} async-done(((bf16[16,8,256]{2,1,0:T(8,128)(2,1)}), bf16[16,8,256]{2,1,0:T(8,128)(2,1)S(1)}, u32[]{:S(2)}, u32[]{:S(2)}) %all-to-all-start.2) | async-done | bytes 65568 | tf_op jit(solution)/shard_map/all_to_all | solution.py:19
  133.6 0.7 broadcast_in_dim.15
  134.3 5.1 %all-to-all-start.3 = ((bf16[32,8,256]{2,1,0:T(8,128)(2,1)}), bf16[32,8,256]{2,1,0:T(8,128)(2,1)S(1)}, u32[]{:S(2)}, u32[]{:S(2)}) async-start(bf16[32,8,256]{2,1,0:T(8,128)(2,1)} %broadcast_in_dim.15), calls=%async_computation.3 | async-start | bytes 262144 | tf_op jit(solution)/shard_map/all_to_all | solution.py:19
  139.3 0.8 fusion.4
  140.2 0.8 fusion.5
  141.0 8.2 %all-to-all-done.3 = bf16[32,8,256]{2,1,0:T(8,128)(2,1)S(1)} async-done(((bf16[32,8,256]{2,1,0:T(8,128)(2,1)}), bf16[32,8,256]{2,1,0:T(8,128)(2,1)S(1)}, u32[]{:S(2)}, u32[]{:S(2)}) %all-to-all-start.3) | async-done | bytes 131104 | tf_op jit(solution)/shard_map/all_to_all | solution.py:19
  149.2 0.7 bitcast_convert_fusion
  (37 shorter events, 0.1 us)
Async XLA Ops:
  0.6 138.7 %copy-start = (bf16[256,256]{1,0:T(8,128)(2,1)S(1)}, bf16[256,256]{1,0:T(8,128)(2,1)}, u32[]{:S(2)}) copy-start(bf16[256,256]{1,0:T(8,128)(2,1)} %param.12) | copy-start | bytes 393220
  0.6 69.8 %copy-start.9 = (s32[1,128]{1,0:T(1,128)S(1)}, s32[1,128]{1,0:T(1,128)}, u32[]{:S(2)}) copy-start(s32[1,128]{1,0:T(1,128)} %param.16) | copy-start | bytes 1540
  0.7 69.9 %copy-start.1 = (s32[1,128]{1,0:T(1,128)S(1)}, s32[1,128]{1,0:T(1,128)}, u32[]{:S(2)}) copy-start(s32[1,128]{1,0:T(1,128)} %param.17) | copy-start | bytes 1540
  0.7 69.9 %copy-start.2 = (s32[1,128]{1,0:T(1,128)S(1)}, s32[1,128]{1,0:T(1,128)}, u32[]{:S(2)}) copy-start(s32[1,128]{1,0:T(1,128)} %param.18) | copy-start | bytes 1540
  2.7 14.4 %copy-start.7 = (bf16[256,256]{1,0:T(8,128)(2,1)S(1)}, bf16[256,256]{1,0:T(8,128)(2,1)}, u32[]{:S(2)}) copy-start(bf16[256,256]{1,0:T(8,128)(2,1)} %get-tuple-element.16.mine) | copy-start | bytes 393220
  2.7 78.4 %all-to-all-start = ((bf16[32,2,32,256]{3,2,1,0:T(8,128)(2,1)}), bf16[32,2,32,256]{3,2,1,0:T(8,128)(2,1)S(1)}, u32[]{:S(2)}, u32[]{:S(2)}) async-start(bf16[32,2,32,256]{3,2,1,0:T(8,128)(2,1)} %get-tuple-element.12), calls=%async_computation | async-start | bytes 2097152 | tf_op jit(solution)/shard_map/all_to_all | solution.py:246
  17.1 23.2 %collective-permute-start.5 = (bf16[256,256]{1,0:T(8,128)(2,1)S(1)}, bf16[256,256]{1,0:T(8,128)(2,1)S(1)}, u32[]{:S(2)}, u32[]{:S(2)}) collective-permute-start(bf16[256,256]{1,0:T(8,128)(2,1)S(1)} %copy-done.7), channel_id=1, source_target_pairs={{0,2},{1,3},{2,0},{3,1},{4,6},{5,7},{6,4},{7,5},{8,10},{9,11},{10,... | collective-permute-start | bytes 393224 | tf_op jit(solution)/shard_map/ppermute | solution.py:23
  40.3 0.6 copy-start.8
  42.6 9.3 %collective-permute-start.6 = (bf16[512,256]{1,0:T(8,128)(2,1)}, bf16[512,256]{1,0:T(8,128)(2,1)S(1)}, u32[]{:S(2)}, u32[]{:S(2)}) collective-permute-start(bf16[512,256]{1,0:T(8,128)(2,1)} %join.1.refs_0_), channel_id=1, source_target_pairs={{4,0},{5,1},{6,2},{7,3},{8,4},{9,5},{10,6},{11,7},{12,8},{13,9},{1... | collective-permute-start | bytes 786440 | tf_op jit(solution)/shard_map/ppermute | solution.py:33
  47.0 9.4 %collective-permute-start.7 = (bf16[512,256]{1,0:T(8,128)(2,1)}, bf16[512,256]{1,0:T(8,128)(2,1)S(1)}, u32[]{:S(2)}, u32[]{:S(2)}) collective-permute-start(bf16[512,256]{1,0:T(8,128)(2,1)} %join.1.refs_0_), channel_id=1, source_target_pairs={{8,0},{9,1},{10,2},{11,3},{12,4},{13,5},{14,6},{15,7},{0,8},{1,9},... | collective-permute-start | bytes 786440 | tf_op jit(solution)/shard_map/ppermute | solution.py:33
  49.5 14.2 %collective-permute-start.8 = (bf16[512,256]{1,0:T(8,128)(2,1)}, bf16[512,256]{1,0:T(8,128)(2,1)S(1)}, u32[]{:S(2)}, u32[]{:S(2)}) collective-permute-start(bf16[512,256]{1,0:T(8,128)(2,1)} %join.1.refs_0_), channel_id=1, source_target_pairs={{12,0},{13,1},{14,2},{15,3},{0,4},{1,5},{2,6},{3,7},{4,8},{5,9},{6... | collective-permute-start | bytes 786440 | tf_op jit(solution)/shard_map/ppermute | solution.py:33
  52.0 11.6 %copy-start.4 = (bf16[512,256]{1,0:T(8,128)(2,1)}, bf16[512,256]{1,0:T(8,128)(2,1)S(1)}, u32[]{:S(2)}) copy-start(bf16[512,256]{1,0:T(8,128)(2,1)S(1)} %collective-permute-done.6.refs_1_) | copy-start | bytes 786436
  56.4 7.2 %copy-start.5 = (bf16[512,256]{1,0:T(8,128)(2,1)}, bf16[512,256]{1,0:T(8,128)(2,1)S(1)}, u32[]{:S(2)}) copy-start(bf16[512,256]{1,0:T(8,128)(2,1)S(1)} %collective-permute-done.7.refs_2_) | copy-start | bytes 786436
  63.6 0.7 copy-start.6
  66.6 11.3 %collective-permute-start.9 = (bf16[1024,256]{1,0:T(8,128)(2,1)}, bf16[1024,256]{1,0:T(8,128)(2,1)S(1)}, u32[]{:S(2)}, u32[]{:S(2)}) collective-permute-start(bf16[1024,256]{1,0:T(8,128)(2,1)} %get-tuple-element.17), channel_id=1, source_target_pairs={{0,1},{1,0},{2,3},{3,2},{4,5},{5,4},{6,7},{7,6},{8,9},{9,8},{10,11... | collective-permute-start | bytes 1572872 | tf_op jit(solution)/shard_map/ppermute | solution.py:23
  70.5 5.0 %copy-start.3 = (bf16[1024,256]{1,0:T(8,128)(2,1)S(1)}, bf16[1024,256]{1,0:T(8,128)(2,1)}, u32[]{:S(2)}) copy-start(bf16[1024,256]{1,0:T(8,128)(2,1)} %get-tuple-element.18) | copy-start | bytes 1572868
  75.5 9.8 %collective-permute-start.10 = (bf16[1024,256]{1,0:T(8,128)(2,1)S(1)}, bf16[1024,256]{1,0:T(8,128)(2,1)S(1)}, u32[]{:S(2)}, u32[]{:S(2)}) collective-permute-start(bf16[1024,256]{1,0:T(8,128)(2,1)S(1)} %copy-done.3), channel_id=1, source_target_pairs={{0,1},{1,0},{2,3},{3,2},{4,5},{5,4},{6,7},{7,6},{8,9},{9,8},{10,11... | collective-permute-start | bytes 1572872 | tf_op jit(solution)/shard_map/ppermute | solution.py:23
  77.8 2.5 %copy-start.11 = (bf16[1024,1024]{1,0:T(8,128)(2,1)S(1)}, bf16[1024,1024]{1,0:T(8,128)(2,1)}, u32[]{:S(2)}) copy-start(bf16[1024,1024]{1,0:T(8,128)(2,1)} %get-tuple-element.13) | copy-start | bytes 6291460
  77.9 2.5 %copy-start.13 = (bf16[1024,256]{1,0:T(8,128)(2,1)S(1)}, bf16[1024,256]{1,0:T(8,128)(2,1)}, u32[]{:S(2)}) copy-start(bf16[1024,256]{1,0:T(8,128)(2,1)} %get-tuple-element.17) | copy-start | bytes 1572868
  81.2 1.6 %copy-start.12 = (bf16[1024,1024]{1,0:T(8,128)(2,1)S(1)}, bf16[1024,1024]{1,0:T(8,128)(2,1)}, u32[]{:S(2)}) copy-start(bf16[1024,1024]{1,0:T(8,128)(2,1)} %get-tuple-element.13) | copy-start | bytes 6291460
  82.8 1.6 %copy-start.10 = (bf16[1024,1024]{1,0:T(8,128)(2,1)S(1)}, bf16[1024,1024]{1,0:T(8,128)(2,1)}, u32[]{:S(2)}) copy-start(bf16[1024,1024]{1,0:T(8,128)(2,1)} %get-tuple-element.11) | copy-start | bytes 6291460
  87.0 29.1 %all-to-all-start.1 = ((bf16[32,40,256]{2,1,0:T(8,128)(2,1)}), bf16[32,40,256]{2,1,0:T(8,128)(2,1)S(1)}, u32[]{:S(2)}, u32[]{:S(2)}) async-start(bf16[32,40,256]{2,1,0:T(8,128)(2,1)} %pad_maximum_fusion), calls=%async_computation.1 | async-start | bytes 1310720 | tf_op jit(solution)/shard_map/all_to_all | solution.py:285
  98.1 4.0 %collective-permute-start = (bf16[1024,256]{1,0:T(8,128)(2,1)S(1)}, bf16[1024,256]{1,0:T(8,128)(2,1)S(1)}, u32[]{:S(2)}, u32[]{:S(2)}) collective-permute-start(bf16[1024,256]{1,0:T(8,128)(2,1)S(1)} %convolution_convert_fusion.1), channel_id=1, source_target_pairs={{0,1},{1,0},{2,3},{3,2},{4,5},{5,4},{6,7},{7,6},{8,9},{9,8},{10,11... | collective-permute-start | bytes 1572872 | tf_op jit(solution)/shard_map/ppermute | solution.py:23
  102.3 21.5 %collective-permute-start.1 = (bf16[256,256]{1,0:T(8,128)(2,1)S(1)}, bf16[256,256]{1,0:T(8,128)(2,1)S(1)}, u32[]{:S(2)}, u32[]{:S(2)}) collective-permute-start(bf16[256,256]{1,0:T(8,128)(2,1)S(1)} %get-tuple-element.23), channel_id=1, source_target_pairs={{0,4},{1,5},{2,6},{3,7},{4,8},{5,9},{6,10},{7,11},{8,12},{9,13},{1... | collective-permute-start | bytes 393224 | tf_op jit(solution)/shard_map/ppermute | solution.py:38
  104.3 19.6 %collective-permute-start.2 = (bf16[256,256]{1,0:T(8,128)(2,1)S(1)}, bf16[256,256]{1,0:T(8,128)(2,1)S(1)}, u32[]{:S(2)}, u32[]{:S(2)}) collective-permute-start(bf16[256,256]{1,0:T(8,128)(2,1)S(1)} %get-tuple-element.25), channel_id=1, source_target_pairs={{0,8},{1,9},{2,10},{3,11},{4,12},{5,13},{6,14},{7,15},{8,0},{9,1},... | collective-permute-start | bytes 393224 | tf_op jit(solution)/shard_map/ppermute | solution.py:38
  108.0 15.9 %collective-permute-start.3 = (bf16[256,256]{1,0:T(8,128)(2,1)S(1)}, bf16[256,256]{1,0:T(8,128)(2,1)S(1)}, u32[]{:S(2)}, u32[]{:S(2)}) collective-permute-start(bf16[256,256]{1,0:T(8,128)(2,1)S(1)} %get-tuple-element.24), channel_id=1, source_target_pairs={{0,12},{1,13},{2,14},{3,15},{4,0},{5,1},{6,2},{7,3},{8,4},{9,5},{1... | collective-permute-start | bytes 393224 | tf_op jit(solution)/shard_map/ppermute | solution.py:38
  116.8 16.8 %all-to-all-start.2 = ((bf16[16,8,256]{2,1,0:T(8,128)(2,1)}), bf16[16,8,256]{2,1,0:T(8,128)(2,1)S(1)}, u32[]{:S(2)}, u32[]{:S(2)}) async-start(bf16[16,8,256]{2,1,0:T(8,128)(2,1)} %broadcast_in_dim.14), calls=%async_computation.2 | async-start | bytes 131072 | tf_op jit(solution)/shard_map/all_to_all | solution.py:19
  123.9 15.4 %collective-permute-start.4 = (bf16[128,256]{1,0:T(8,128)(2,1)S(1)}, bf16[128,256]{1,0:T(8,128)(2,1)S(1)}, u32[]{:S(2)}, u32[]{:S(2)}) collective-permute-start(bf16[128,256]{1,0:T(8,128)(2,1)S(1)} %slice.65), channel_id=1, source_target_pairs={{0,2},{1,3},{2,0},{3,1},{4,6},{5,7},{6,4},{7,5},{8,10},{9,11},{10,... | collective-permute-start | bytes 196616 | tf_op jit(solution)/shard_map/ppermute | solution.py:23
  134.3 14.9 %all-to-all-start.3 = ((bf16[32,8,256]{2,1,0:T(8,128)(2,1)}), bf16[32,8,256]{2,1,0:T(8,128)(2,1)S(1)}, u32[]{:S(2)}, u32[]{:S(2)}) async-start(bf16[32,8,256]{2,1,0:T(8,128)(2,1)} %broadcast_in_dim.15), calls=%async_computation.3 | async-start | bytes 262144 | tf_op jit(solution)/shard_map/all_to_all | solution.py:19

commit v6 on v5

--- a/solution.py
+++ b/solution.py
@@ -163,54 +163,146 @@
     )(row_ids, col_ids, norm_ids, count, in_main(tile_block))
 
 
-def join_kernel(mine, beside, pair):
-    rows = mine.shape[0]
-    pair[:rows] = mine[...]
-    pair[rows:] = beside[...]
-
-
-def join(mine, beside):
-    rows, width = mine.shape
-    return pl.pallas_call(
-        join_kernel, out_shape=jax.ShapeDtypeStruct((2 * rows, width), mine.dtype), name="join"
-    )(in_main(mine), in_main(beside))
-
-
 def assemble_kernel(*refs):
-    *parts, near, near_emb = refs
+    *parts, near = refs
     rows = parts[0].shape[0] // 4
+    table = near.shape[0] // 2
     for index, part in enumerate(parts):
         for side in range(2):
-            out = pl.ds((2 * index + side) * rows, rows)
-            near[out] = part[pl.ds(2 * side * rows, rows)]
-            near_emb[out] = part[pl.ds((2 * side + 1) * rows, rows)]
+            place = (2 * index + side) * rows
+            near[pl.ds(place, rows)] = part[pl.ds(2 * side * rows, rows)]
+            near[pl.ds(table + place, rows)] = part[pl.ds((2 * side + 1) * rows, rows)]
 
 
 def assemble(parts):
     rows, width = parts[0].shape
-    shape = jax.ShapeDtypeStruct((len(parts) * rows // 2, width), parts[0].dtype)
-    return pl.pallas_call(assemble_kernel, out_shape=[shape] * 2, name="assemble")(*map(in_main, parts))
-
-
-def lay_out_kernel(grad_user, user_emb, grad_item, item_emb, mine, pieces):
+    shape = jax.ShapeDtypeStruct((len(parts) * rows, width), parts[0].dtype)
+    return pl.pallas_call(assemble_kernel, out_shape=shape, name="assemble")(*map(in_main, parts))
+
+
+def lay_out_kernel(grad_user, user_emb, grad_item, item_emb, mine, pair, pieces):
     rows = grad_user.shape[0]
     mine[:rows] = grad_user[...]
     mine[rows:] = user_emb[...]
+    pair[:rows] = grad_user[...]
+    pair[rows : 2 * rows] = user_emb[...]
+    pair[2 * rows :] = jnp.zeros((2 * rows, pair.shape[1]), pair.dtype)
+    item_rows = grad_item.shape[0]
     for peer in range(pieces.shape[0]):
-        pieces[peer, 0] = grad_item[...]
-        pieces[peer, 1] = item_emb[...]
+        pieces[peer, :item_rows] = grad_item[...]
+        pieces[peer, item_rows:] = item_emb[...]
 
 
 def lay_out(grad_user, user_emb, grad_item, item_emb):
     peers = lax.axis_size("au")
+    rows, width = grad_user.shape
     return pl.pallas_call(
         lay_out_kernel,
         out_shape=[
-            jax.ShapeDtypeStruct((2 * grad_user.shape[0], grad_user.shape[1]), grad_user.dtype),
-            jax.ShapeDtypeStruct((peers, 2, *grad_item.shape), grad_item.dtype),
+            jax.ShapeDtypeStruct((2 * rows, width), grad_user.dtype),
+            jax.ShapeDtypeStruct((4 * rows, width), grad_user.dtype),
+            jax.ShapeDtypeStruct((peers, 2 * grad_item.shape[0], width), grad_item.dtype),
         ],
         name="lay_out",
     )(grad_user, user_emb, grad_item, item_emb)
+
+
+def transposed_product(left, right):
+    return lax.dot_general(
+        left, right, (((0,), (0,)), ((), ())), preferred_element_type=jnp.float32
+    )
+
+
+def finish_kernel(
+    dense_near,
+    dense_far,
+    item_in,
+    near_in,
+    far_in,
+    user_near,
+    user_far,
+    pieces,
+    dense,
+    item_rows,
+    sources,
+    q_turned,
+    sems,
+):
+    low = jnp.bfloat16
+    peers, both_rows, width = item_rows.shape
+    piece_rows = both_rows // 2
+    half_rows, all_items = dense.shape[1:]
+    step = 256
+    item_copy = pltpu.make_async_copy(item_in, item_rows, sems.at[0])
+    dense_copies = [
+        pltpu.make_async_copy(ref, dense.at[half], sems.at[1 + half])
+        for half, ref in enumerate((dense_near, dense_far))
+    ]
+    source_copies = [
+        pltpu.make_async_copy(ref, sources.at[half], sems.at[3 + half])
+        for half, ref in enumerate((near_in, far_in))
+    ]
+    item_copy.start()
+    for half in range(2):
+        dense_copies[half].start()
+        source_copies[half].start()
+    item_copy.wait()
+    items = item_rows[:, :piece_rows].reshape(all_items, width)
+    weight_term = jnp.zeros((width, width), jnp.float32)
+    for half, user in enumerate((user_near, user_far)):
+        dense_copies[half].wait()
+        for start in range(0, half_rows, step):
+            rows = dense[half, start : start + step]
+            user[start : start + step] = jnp.dot(
+                rows, items, preferred_element_type=jnp.float32
+            ).astype(low)
+        source_copies[half].wait()
+        weight_term += transposed_product(sources[half, half_rows:], user[...])
+        turned = sources[half, :half_rows].T
+        for start in range(0, all_items, step):
+            part = jnp.dot(
+                turned, dense[half, :, start : start + step], preferred_element_type=jnp.float32
+            )
+            if half == 0:
+                q_turned[:, start : start + step] = part
+            else:
+                q_turned[:, start : start + step] += part
+    q_low = q_turned[...].astype(low)
+    table = item_rows[:, piece_rows:].reshape(all_items, width)
+    weight_term += jnp.dot(q_low, table, preferred_element_type=jnp.float32).T
+    pieces[:, :piece_rows] = q_turned[...].T.astype(low).reshape(peers, piece_rows, width)
+    pieces[:, piece_rows:] = weight_term.reshape(peers, width // peers, width).astype(low)
+
+
+def finish(dense_near, dense_far, item_pieces, near, far):
+    half_rows, all_items = dense_near.shape
+    peers, both_rows, width = item_pieces.shape
+    low = jnp.bfloat16
+    strip = both_rows // 2 + width // peers
+    in_place = pl.BlockSpec(memory_space=pltpu.HBM)
+    return pl.pallas_call(
+        finish_kernel,
+        in_specs=[in_place] * 5,
+        out_shape=[
+            jax.ShapeDtypeStruct((half_rows, width), low),
+            jax.ShapeDtypeStruct((half_rows, width), low),
+            jax.ShapeDtypeStruct((peers, strip, width), low),
+        ],
+        scratch_shapes=[
+            pltpu.VMEM((2, half_rows, all_items), low),
+            pltpu.VMEM((peers, both_rows, width), low),
+            pltpu.VMEM((2, 2 * half_rows, width), low),
+            pltpu.VMEM((width, all_items), jnp.float32),
+            pltpu.SemaphoreType.DMA((5,)),
+        ],
+        compiler_params=pltpu.CompilerParams(vmem_limit_bytes=32 << 20),
+        cost_estimate=pl.CostEstimate(
+            flops=8 * half_rows * all_items * width,
+            bytes_accessed=4 * half_rows * all_items + 8 * half_rows * width,
+            transcendentals=0,
+        ),
+        name="finish",
+    )(*map(in_main, (dense_near, dense_far, item_pieces, near, far)))
 
 
 def product(spec, left, right):
@@ -239,20 +331,16 @@
     low = jnp.bfloat16
     ring = lax.axis_size("ia") // ring_step
 
-    mine, item_sent = lay_out(grad_user[0], user_emb[0], grad_item[0], item_emb[0])
+    mine, pair, item_sent = lay_out(grad_user[0], user_emb[0], grad_item[0], item_emb[0])
     beside = partner(mine, side_bit)
-    pair = join(mine, beside)
+    pair = lax.dynamic_update_slice(pair, beside, (mine.shape[0], 0))
     own_rows = user_emb.shape[1]
     item_pieces = lax.all_to_all(item_sent, "au", split_axis=0, concat_axis=0, tiled=True)
     parts = [pair]
     for distance in range(1, ring):
         parts.append(from_ahead(pair, distance))
-    near, near_emb = assemble(parts)
+    near = assemble(parts)
     far = partner(near, core_bit)
-    far_emb = partner(near_emb, core_bit)
-
-    items = item_pieces[:, 0].reshape(item_rows, width)
-    item_table = item_pieces[:, 1].reshape(item_rows, width)
 
     dense_near, dense_far = dense_block(
         tile_values[0],
@@ -263,25 +351,8 @@
         user_rows,
         item_rows,
     )
-    user_far = product("ui,id->ud", dense_far, items).astype(low)
-    user_near = product("ui,id->ud", dense_near, items).astype(low)
-    user_far, user_near = lax.optimization_barrier((user_far, user_near))
-    item_part = product("ui,ud->id", dense_near, near) + product("ui,ud->id", dense_far, far)
-    item_part = item_part.astype(low)
-    weight_part = (
-        product("rd,re->de", near_emb, user_near)
-        + product("rd,re->de", far_emb, user_far)
-        + product("rd,re->de", item_table, item_part)
-    )
-
+    user_near, user_far, pieces = finish(dense_near, dense_far, item_pieces, near, far)
     peers = lax.axis_size("au")
-    pieces = jnp.concatenate(
-        [
-            item_part.reshape(peers, item_rows // peers, width),
-            weight_part.astype(low).reshape(peers, width // peers, width),
-        ],
-        axis=1,
-    )
     arrived = lax.all_to_all(pieces, "au", split_axis=0, concat_axis=0, tiled=True)
     arrived = summed(arrived)
     q_item = arrived[: item_rows // peers]

time: 151 us -> 145 us (0.960)
  waiting for transfers between devices: 47.5 us -> 41.5 us
  matrix products: 7.3 us -> 1.62 us
  Pallas kernels: 10.9 us -> 15.9 us
  starting transfers between devices: 75.4 us -> 79.1 us
  local copies, waits for them, and re-layouts: 5.21 us -> 3.39 us
    dot_general x9 -> x2, matrix products: 7.3 us -> 1.62 us  [product(): return jnp.einsum(spec, left, right, preferred_element_type=jnp.float32)]
    pallas_call x3, Pallas kernels: 5.96 us -> 11 us  [the longest x1 6.66 us: finish(): pl.pallas_call(finish_kernel, in_specs=[in_place] * 5, out_shape=[jax.Sha...]
    ppermute x3, waiting for transfers between devices: 11.6 us -> 7.13 us  [from_ahead(): lax.ppermute(value, 'ia', [(ahead(i, distance), i) for i in range(size)])]
    all_to_all x2, starting transfers between devices: 12.1 us -> 14.3 us  [from_everyone(): return lax.all_to_all(copies, axis, split_axis=0, concat_axis=0, tiled=True)]
    unnamed x28 -> x24, local copies, waits for them, and re-layouts: 3.79 us -> 2.04 us
    ppermute x3, starting transfers between devices: 8.41 us -> 10.1 us  [send_ahead(): lax.ppermute(value, 'ia', [(i, ahead(i, distance)) for i in range(size)])]
    ppermute x5 -> x4, starting transfers between devices: 20 us -> 18.4 us  [partner(): lax.ppermute(value, 'ia', [(i, i ^ bit) for i in range(lax.axis_size('ia'...]
    ppermute x5 -> x4, waiting for transfers between devices: 19.9 us -> 19.9 us  [partner(): lax.ppermute(value, 'ia', [(i, i ^ bit) for i in range(lax.axis_size('ia'...]
  transfers between devices with their start and end apart: 15 -> 14, of which waited for: 7 -> 7; matrix products, arithmetic and copies ran while one was open for 6% -> 2% of each run, Pallas kernels for 6% -> 5%
where the time goes in v6:
time: 145 us; the launch traced here: 144 us
  starting transfers between devices  79.1 us (55%)
  waiting for transfers between devices  41.5 us (29%)
  Pallas kernels  15.9 us (11%)
  local copies, waits for them, and re-layouts  3.39 us (2%)
  between operations  1.63 us (1%)
  matrix products  1.62 us (1%)
    ppermute x4, waiting for transfers between devices, partner(): lax.ppermute(value, 'ia', [(i, i ^ bit) for i in range(lax.axis_size('ia'...  19.9 us
    ppermute x4, starting transfers between devices, partner(): lax.ppermute(value, 'ia', [(i, i ^ bit) for i in range(lax.axis_size('ia'...  18.4 us
    all_to_all x1, starting transfers between devices, device_step(): lax.all_to_all(item_sent, 'au', split_axis=0, concat_axis=0, tiled=True)  14.4 us
    all_to_all x2, starting transfers between devices, from_everyone(): return lax.all_to_all(copies, axis, split_axis=0, concat_axis=0, tiled=True)  14.3 us
    all_to_all x1, starting transfers between devices, device_step(): lax.all_to_all(pieces, 'au', split_axis=0, concat_axis=0, tiled=True)  11.4 us
    all_to_all x2, waiting for transfers between devices, from_everyone(): return lax.all_to_all(copies, axis, split_axis=0, concat_axis=0, tiled=True)  10.7 us
    ppermute x3, starting transfers between devices, from_ahead(): lax.ppermute(value, 'ia', [(ahead(i, distance), i) for i in range(size)])  10.5 us
    ppermute x3, starting transfers between devices, send_ahead(): lax.ppermute(value, 'ia', [(i, ahead(i, distance)) for i in range(size)])  10.1 us
  transfers between devices with their start and end apart: 14, of which 7 were waited for; matrix products, arithmetic and copies ran while one was open for 2% of the time, Pallas kernels for 5%

profile of v6, /device:TPU:1, one launch (start us, length us, event | category | flops | bytes accessed | tf_op | source)
XLA Modules:
  0.0 144.3 jit_solution(6944235523284068651)
XLA Ops:
  0.6 0.0 copy-start
  0.6 2.1 %lay_out.1 = (bf16[256,256]{1,0:T(8,128)(2,1)}, bf16[512,256]{1,0:T(8,128)(2,1)}, bf16[32,64,256]{2,1,0:T(8,128)(2,1)}) custom-call(bf16[128,256]{1,0:T(8,128)(2,1)} %bitcast.23, bf16[128,256]{1,0:T(8,128)(2,1)} %bitcast.24, bf16[32,256]{1,0:T(8,128)(2,1)} %bitcast.25, bf16[32,256]{1,0:T(8,128)(2,1)} %bitcast.26), custom_call_target="tpu_custom_call" | custom-call | tf_op jit(solution)/shard_map/lay_out/pallas_call | solution.py:199
  2.7 0.0 copy-start.1
  2.7 0.0 copy-start.2
  2.8 14.4 %all-to-all-start = ((bf16[32,64,256]{2,1,0:T(8,128)(2,1)}), bf16[32,64,256]{2,1,0:T(8,128)(2,1)S(1)}, u32[]{:S(2)}, u32[]{:S(2)}) async-start(bf16[32,64,256]{2,1,0:T(8,128)(2,1)} %get-tuple-element.13), calls=%async_computation | async-start | bytes 2097152 | tf_op jit(solution)/shard_map/all_to_all | solution.py:338
  17.2 4.8 %collective-permute-start = (bf16[256,256]{1,0:T(8,128)(2,1)S(1)}, bf16[256,256]{1,0:T(8,128)(2,1)S(1)}, u32[]{:S(2)}, u32[]{:S(2)}) collective-permute-start(bf16[256,256]{1,0:T(8,128)(2,1)S(1)} %copy-done.11), channel_id=1, source_target_pairs={{0,2},{1,3},{2,0},{3,1},{4,6},{5,7},{6,4},{7,5},{8,10},{9,11},{10,... | collective-permute-start | bytes 393224 | tf_op jit(solution)/shard_map/ppermute | solution.py:23
  22.0 18.4 %collective-permute-done = bf16[256,256]{1,0:T(8,128)(2,1)S(1)} collective-permute-done((bf16[256,256]{1,0:T(8,128)(2,1)S(1)}, bf16[256,256]{1,0:T(8,128)(2,1)S(1)}, u32[]{:S(2)}, u32[]{:S(2)}) %collective-permute-start) | collective-permute-done | bytes 131104 | tf_op jit(solution)/shard_map/ppermute | solution.py:23
  40.4 0.0 copy-done.5
  40.4 0.0 copy-start.6
  40.4 3.1 %collective-permute-start.3 = (bf16[512,256]{1,0:T(8,128)(2,1)S(1)}, bf16[512,256]{1,0:T(8,128)(2,1)S(1)}, u32[]{:S(2)}, u32[]{:S(2)}) collective-permute-start(bf16[512,256]{1,0:T(8,128)(2,1)S(1)} %constant_dynamic-update-slice_fusion.refs_0_), channel_id=1, source_target_pairs={{12,0},{13,1},{14,2},{15,3},{0,4},{1,5},{2,6},{3,7},{4,8},{5,9},{6... | collective-permute-start | bytes 786440 | tf_op jit(solution)/shard_map/ppermute | solution.py:33
  43.5 4.4 %collective-permute-start.2 = (bf16[512,256]{1,0:T(8,128)(2,1)S(1)}, bf16[512,256]{1,0:T(8,128)(2,1)S(1)}, u32[]{:S(2)}, u32[]{:S(2)}) collective-permute-start(bf16[512,256]{1,0:T(8,128)(2,1)S(1)} %constant_dynamic-update-slice_fusion.refs_0_), channel_id=1, source_target_pairs={{8,0},{9,1},{10,2},{11,3},{12,4},{13,5},{14,6},{15,7},{0,8},{1,9},... | collective-permute-start | bytes 786440 | tf_op jit(solution)/shard_map/ppermute | solution.py:33
  47.9 3.1 %collective-permute-start.1 = (bf16[512,256]{1,0:T(8,128)(2,1)S(1)}, bf16[512,256]{1,0:T(8,128)(2,1)S(1)}, u32[]{:S(2)}, u32[]{:S(2)}) collective-permute-start(bf16[512,256]{1,0:T(8,128)(2,1)S(1)} %constant_dynamic-update-slice_fusion.refs_0_), channel_id=1, source_target_pairs={{4,0},{5,1},{6,2},{7,3},{8,4},{9,5},{10,6},{11,7},{12,8},{13,9},{1... | collective-permute-start | bytes 786440 | tf_op jit(solution)/shard_map/ppermute | solution.py:33
  51.0 0.0 collective-permute-done.3.refs_3_
  51.0 5.2 %collective-permute-done.2.refs_2_ = bf16[512,256]{1,0:T(8,128)(2,1)S(1)} collective-permute-done((bf16[512,256]{1,0:T(8,128)(2,1)S(1)}, bf16[512,256]{1,0:T(8,128)(2,1)S(1)}, u32[]{:S(2)}, u32[]{:S(2)}) %collective-permute-start.2) | collective-permute-done | bytes 262176 | tf_op jit(solution)/shard_map/ppermute | solution.py:33
  56.1 2.0 %collective-permute-done.1.refs_1_ = bf16[512,256]{1,0:T(8,128)(2,1)S(1)} collective-permute-done((bf16[512,256]{1,0:T(8,128)(2,1)S(1)}, bf16[512,256]{1,0:T(8,128)(2,1)S(1)}, u32[]{:S(2)}, u32[]{:S(2)}) %collective-permute-start.1) | collective-permute-done | bytes 262176 | tf_op jit(solution)/shard_map/ppermute | solution.py:33
  58.1 0.7 copy-done.8
  58.8 2.2 %assemble.1.near_in = bf16[2048,256]{1,0:T(8,128)(2,1)} custom-call(bf16[512,256]{1,0:T(8,128)(2,1)} %copy-done.6, bf16[512,256]{1,0:T(8,128)(2,1)} %copy-done.8, bf16[512,256]{1,0:T(8,128)(2,1)} %copy-done.7, bf16[512,256]{1,0:T(8,128)(2,1)} %copy-done.4), custom_call_target="tpu_custom_call" | custom-call | tf_op jit(solution)/shard_map/assemble/pallas_call | solution.py:180
  61.1 4.1 %collective-permute-start.4 = (bf16[2048,256]{1,0:T(8,128)(2,1)}, bf16[2048,256]{1,0:T(8,128)(2,1)S(1)}, u32[]{:S(2)}, u32[]{:S(2)}) collective-permute-start(bf16[2048,256]{1,0:T(8,128)(2,1)} %assemble.1.near_in), channel_id=1, source_target_pairs={{0,1},{1,0},{2,3},{3,2},{4,5},{5,4},{6,7},{7,6},{8,9},{9,8},{10,11... | collective-permute-start | bytes 3145736 | tf_op jit(solution)/shard_map/ppermute | solution.py:23
  65.9 4.9 %dense_block.1 = (bf16[1024,1024]{1,0:T(8,128)(2,1)}, bf16[1024,1024]{1,0:T(8,128)(2,1)}) custom-call(s32[128]{0:T(128)S(1)} %add_bitcast_fusion.rows, s32[128]{0:T(128)S(1)} %bitcast.20, s32[128]{0:T(128)S(1)} %bitcast.21, s32[1]{0:T(128)} %bitcast.19.count, bf16[128,128,128]{2,1,0:T(8,128)(2,1)} %bitcast.22), custom_call_target="tpu_custom_call" | custom-call | flops 8388608 | bytes 8388608 | tf_op jit(solution)/shard_map/dense_block/pallas_call | solution.py:140
  70.8 0.0 collective-permute-done.4.far_in
  70.9 0.0 all-to-all-done.item_in
  70.9 0.9 copy-done.10
  71.8 0.4 copy-done.3
  72.2 6.7 %finish.1 = (bf16[1024,256]{1,0:T(8,128)(2,1)S(1)}, bf16[1024,256]{1,0:T(8,128)(2,1)S(1)}, bf16[32,40,256]{2,1,0:T(8,128)(2,1)}) custom-call(bf16[1024,1024]{1,0:T(8,128)(2,1)} %get-tuple-element.11.dense_near, bf16[1024,1024]{1,0:T(8,128)(2,1)} %get-tuple-element.12.dense_far, bf16[32,64,256]{2,1,0:T(8,128)(2,1)} %copy-done.3, ...), custom_call_target="tpu_custom_call" | custom-call | flops 2147483648 | bytes 6291456 | tf_op jit(solution)/shard_map/finish/pallas_call | solution.py:283
  78.8 11.4 %all-to-all-start.1 = ((bf16[32,40,256]{2,1,0:T(8,128)(2,1)}), bf16[32,40,256]{2,1,0:T(8,128)(2,1)S(1)}, u32[]{:S(2)}, u32[]{:S(2)}) async-start(bf16[32,40,256]{2,1,0:T(8,128)(2,1)} %get-tuple-element.18), calls=%async_computation.1 | async-start | bytes 1310720 | tf_op jit(solution)/shard_map/all_to_all | solution.py:356
  90.2 2.4 %collective-permute-start.5 = (bf16[1024,256]{1,0:T(8,128)(2,1)S(1)}, bf16[1024,256]{1,0:T(8,128)(2,1)S(1)}, u32[]{:S(2)}, u32[]{:S(2)}) collective-permute-start(bf16[1024,256]{1,0:T(8,128)(2,1)S(1)} %get-tuple-element.17), channel_id=1, source_target_pairs={{0,1},{1,0},{2,3},{3,2},{4,5},{5,4},{6,7},{7,6},{8,9},{9,8},{10,11... | collective-permute-start | bytes 1572872 | tf_op jit(solution)/shard_map/ppermute | solution.py:23
  92.6 1.5 %collective-permute-done.5 = bf16[1024,256]{1,0:T(8,128)(2,1)S(1)} collective-permute-done((bf16[1024,256]{1,0:T(8,128)(2,1)S(1)}, bf16[1024,256]{1,0:T(8,128)(2,1)S(1)}, u32[]{:S(2)}, u32[]{:S(2)}) %collective-permute-start.5) | collective-permute-done | bytes 524320 | tf_op jit(solution)/shard_map/ppermute | solution.py:23
  94.1 0.1 fusion.5
  94.3 3.8 %collective-permute-start.6 = (bf16[256,256]{1,0:T(8,128)(2,1)S(1)}, bf16[256,256]{1,0:T(8,128)(2,1)S(1)}, u32[]{:S(2)}, u32[]{:S(2)}) collective-permute-start(bf16[256,256]{1,0:T(8,128)(2,1)S(1)} %get-tuple-element.21), channel_id=1, source_target_pairs={{0,4},{1,5},{2,6},{3,7},{4,8},{5,9},{6,10},{7,11},{8,12},{9,13},{1... | collective-permute-start | bytes 393224 | tf_op jit(solution)/shard_map/ppermute | solution.py:38
  98.1 2.7 %collective-permute-start.8 = (bf16[256,256]{1,0:T(8,128)(2,1)S(1)}, bf16[256,256]{1,0:T(8,128)(2,1)S(1)}, u32[]{:S(2)}, u32[]{:S(2)}) collective-permute-start(bf16[256,256]{1,0:T(8,128)(2,1)S(1)} %get-tuple-element.22), channel_id=1, source_target_pairs={{0,12},{1,13},{2,14},{3,15},{4,0},{5,1},{6,2},{7,3},{8,4},{9,5},{1... | collective-permute-start | bytes 393224 | tf_op jit(solution)/shard_map/ppermute | solution.py:38
  100.8 3.6 %collective-permute-start.7 = (bf16[256,256]{1,0:T(8,128)(2,1)S(1)}, bf16[256,256]{1,0:T(8,128)(2,1)S(1)}, u32[]{:S(2)}, u32[]{:S(2)}) collective-permute-start(bf16[256,256]{1,0:T(8,128)(2,1)S(1)} %get-tuple-element.23), channel_id=1, source_target_pairs={{0,8},{1,9},{2,10},{3,11},{4,12},{5,13},{6,14},{7,15},{8,0},{9,1},... | collective-permute-start | bytes 393224 | tf_op jit(solution)/shard_map/ppermute | solution.py:38
  104.4 3.8 %all-to-all-done.1 = bf16[32,40,256]{2,1,0:T(8,128)(2,1)S(1)} async-done(((bf16[32,40,256]{2,1,0:T(8,128)(2,1)}), bf16[32,40,256]{2,1,0:T(8,128)(2,1)S(1)}, u32[]{:S(2)}, u32[]{:S(2)}) %all-to-all-start.1) | async-done | bytes 655392 | tf_op jit(solution)/shard_map/all_to_all | solution.py:356
  108.2 0.1 reduce
  108.3 0.6 broadcast_in_dim.14
  109.0 8.9 %all-to-all-start.2 = ((bf16[16,8,256]{2,1,0:T(8,128)(2,1)}), bf16[16,8,256]{2,1,0:T(8,128)(2,1)S(1)}, u32[]{:S(2)}, u32[]{:S(2)}) async-start(bf16[16,8,256]{2,1,0:T(8,128)(2,1)} %broadcast_in_dim.14), calls=%async_computation.2 | async-start | bytes 131072 | tf_op jit(solution)/shard_map/all_to_all | solution.py:19
  117.8 0.0 collective-permute-done.6
  117.8 0.0 collective-permute-done.8
  117.8 0.0 collective-permute-done.7
  117.9 0.1 slice_add_fusion
  117.9 7.2 %collective-permute-start.9 = (bf16[128,256]{1,0:T(8,128)(2,1)S(1)}, bf16[128,256]{1,0:T(8,128)(2,1)S(1)}, u32[]{:S(2)}, u32[]{:S(2)}) collective-permute-start(bf16[128,256]{1,0:T(8,128)(2,1)S(1)} %slice.55), channel_id=1, source_target_pairs={{0,2},{1,3},{2,0},{3,1},{4,6},{5,7},{6,4},{7,5},{8,10},{9,11},{10,... | collective-permute-start | bytes 196616 | tf_op jit(solution)/shard_map/ppermute | solution.py:23
  125.1 2.4 %all-to-all-done.2 = bf16[16,8,256]{2,1,0:T(8,128)(2,1)S(1)} async-done(((bf16[16,8,256]{2,1,0:T(8,128)(2,1)}), bf16[16,8,256]{2,1,0:T(8,128)(2,1)S(1)}, u32[]{:S(2)}, u32[]{:S(2)}) %all-to-all-start.2) | async-done | bytes 65568 | tf_op jit(solution)/shard_map/all_to_all | solution.py:19
  127.6 0.7 broadcast_in_dim.15
  128.3 5.4 %all-to-all-start.3 = ((bf16[32,8,256]{2,1,0:T(8,128)(2,1)}), bf16[32,8,256]{2,1,0:T(8,128)(2,1)S(1)}, u32[]{:S(2)}, u32[]{:S(2)}) async-start(bf16[32,8,256]{2,1,0:T(8,128)(2,1)} %broadcast_in_dim.15), calls=%async_computation.3 | async-start | bytes 262144 | tf_op jit(solution)/shard_map/all_to_all | solution.py:19
  133.7 0.0 collective-permute-done.9
  133.7 0.8 fusion
  134.5 0.8 fusion.1
  135.3 8.2 %all-to-all-done.3 = bf16[32,8,256]{2,1,0:T(8,128)(2,1)S(1)} async-done(((bf16[32,8,256]{2,1,0:T(8,128)(2,1)}), bf16[32,8,256]{2,1,0:T(8,128)(2,1)S(1)}, u32[]{:S(2)}, u32[]{:S(2)}) %all-to-all-start.3) | async-done | bytes 131104 | tf_op jit(solution)/shard_map/all_to_all | solution.py:19
  143.5 0.7 bitcast_convert_fusion
  (23 shorter events, 0.1 us)
Async XLA Ops:
  0.6 133.1 %copy-start = (bf16[256,256]{1,0:T(8,128)(2,1)S(1)}, bf16[256,256]{1,0:T(8,128)(2,1)}, u32[]{:S(2)}) copy-start(bf16[256,256]{1,0:T(8,128)(2,1)} %param.12) | copy-start | bytes 393220
  2.7 14.5 %copy-start.11 = (bf16[256,256]{1,0:T(8,128)(2,1)S(1)}, bf16[256,256]{1,0:T(8,128)(2,1)}, u32[]{:S(2)}) copy-start(bf16[256,256]{1,0:T(8,128)(2,1)} %get-tuple-element.15) | copy-start | bytes 393220
  2.7 37.6 %copy-start.5 = (bf16[512,256]{1,0:T(8,128)(2,1)S(1)}, bf16[512,256]{1,0:T(8,128)(2,1)}, u32[]{:S(2)}) copy-start(bf16[512,256]{1,0:T(8,128)(2,1)} %get-tuple-element.14) | copy-start | bytes 786436
  2.7 63.1 %copy-start.9 = (s32[1,128]{1,0:T(1,128)S(1)}, s32[1,128]{1,0:T(1,128)}, u32[]{:S(2)}) copy-start(s32[1,128]{1,0:T(1,128)} %param.16) | copy-start | bytes 1540
  2.7 63.1 %copy-start.1 = (s32[1,128]{1,0:T(1,128)S(1)}, s32[1,128]{1,0:T(1,128)}, u32[]{:S(2)}) copy-start(s32[1,128]{1,0:T(1,128)} %param.17) | copy-start | bytes 1540
  2.7 63.1 %copy-start.2 = (s32[1,128]{1,0:T(1,128)S(1)}, s32[1,128]{1,0:T(1,128)}, u32[]{:S(2)}) copy-start(s32[1,128]{1,0:T(1,128)} %param.18) | copy-start | bytes 1540
  2.8 68.1 %all-to-all-start = ((bf16[32,64,256]{2,1,0:T(8,128)(2,1)}), bf16[32,64,256]{2,1,0:T(8,128)(2,1)S(1)}, u32[]{:S(2)}, u32[]{:S(2)}) async-start(bf16[32,64,256]{2,1,0:T(8,128)(2,1)} %get-tuple-element.13), calls=%async_computation | async-start | bytes 2097152 | tf_op jit(solution)/shard_map/all_to_all | solution.py:338
  17.2 23.2 %collective-permute-start = (bf16[256,256]{1,0:T(8,128)(2,1)S(1)}, bf16[256,256]{1,0:T(8,128)(2,1)S(1)}, u32[]{:S(2)}, u32[]{:S(2)}) collective-permute-start(bf16[256,256]{1,0:T(8,128)(2,1)S(1)} %copy-done.11), channel_id=1, source_target_pairs={{0,2},{1,3},{2,0},{3,1},{4,6},{5,7},{6,4},{7,5},{8,10},{9,11},{10,... | collective-permute-start | bytes 393224 | tf_op jit(solution)/shard_map/ppermute | solution.py:23
  40.4 17.7 %copy-start.6 = (bf16[512,256]{1,0:T(8,128)(2,1)}, bf16[512,256]{1,0:T(8,128)(2,1)S(1)}, u32[]{:S(2)}) copy-start(bf16[512,256]{1,0:T(8,128)(2,1)S(1)} %constant_dynamic-update-slice_fusion.refs_0_) | copy-start | bytes 786436
  40.4 10.6 %collective-permute-start.3 = (bf16[512,256]{1,0:T(8,128)(2,1)S(1)}, bf16[512,256]{1,0:T(8,128)(2,1)S(1)}, u32[]{:S(2)}, u32[]{:S(2)}) collective-permute-start(bf16[512,256]{1,0:T(8,128)(2,1)S(1)} %constant_dynamic-update-slice_fusion.refs_0_), channel_id=1, source_target_pairs={{12,0},{13,1},{14,2},{15,3},{0,4},{1,5},{2,6},{3,7},{4,8},{5,9},{6... | collective-permute-start | bytes 786440 | tf_op jit(solution)/shard_map/ppermute | solution.py:33
  43.5 12.6 %collective-permute-start.2 = (bf16[512,256]{1,0:T(8,128)(2,1)S(1)}, bf16[512,256]{1,0:T(8,128)(2,1)S(1)}, u32[]{:S(2)}, u32[]{:S(2)}) collective-permute-start(bf16[512,256]{1,0:T(8,128)(2,1)S(1)} %constant_dynamic-update-slice_fusion.refs_0_), channel_id=1, source_target_pairs={{8,0},{9,1},{10,2},{11,3},{12,4},{13,5},{14,6},{15,7},{0,8},{1,9},... | collective-permute-start | bytes 786440 | tf_op jit(solution)/shard_map/ppermute | solution.py:33
  47.9 10.2 %collective-permute-start.1 = (bf16[512,256]{1,0:T(8,128)(2,1)S(1)}, bf16[512,256]{1,0:T(8,128)(2,1)S(1)}, u32[]{:S(2)}, u32[]{:S(2)}) collective-permute-start(bf16[512,256]{1,0:T(8,128)(2,1)S(1)} %constant_dynamic-update-slice_fusion.refs_0_), channel_id=1, source_target_pairs={{4,0},{5,1},{6,2},{7,3},{8,4},{9,5},{10,6},{11,7},{12,8},{13,9},{1... | collective-permute-start | bytes 786440 | tf_op jit(solution)/shard_map/ppermute | solution.py:33
  51.0 7.1 %copy-start.4 = (bf16[512,256]{1,0:T(8,128)(2,1)}, bf16[512,256]{1,0:T(8,128)(2,1)S(1)}, u32[]{:S(2)}) copy-start(bf16[512,256]{1,0:T(8,128)(2,1)S(1)} %collective-permute-done.3.refs_3_) | copy-start | bytes 786436
  56.1 2.0 %copy-start.7 = (bf16[512,256]{1,0:T(8,128)(2,1)}, bf16[512,256]{1,0:T(8,128)(2,1)S(1)}, u32[]{:S(2)}) copy-start(bf16[512,256]{1,0:T(8,128)(2,1)S(1)} %collective-permute-done.2.refs_2_) | copy-start | bytes 786436
  58.1 0.7 copy-start.8
  61.1 9.8 %collective-permute-start.4 = (bf16[2048,256]{1,0:T(8,128)(2,1)}, bf16[2048,256]{1,0:T(8,128)(2,1)S(1)}, u32[]{:S(2)}, u32[]{:S(2)}) collective-permute-start(bf16[2048,256]{1,0:T(8,128)(2,1)} %assemble.1.near_in), channel_id=1, source_target_pairs={{0,1},{1,0},{2,3},{3,2},{4,5},{5,4},{6,7},{7,6},{8,9},{9,8},{10,11... | collective-permute-start | bytes 3145736 | tf_op jit(solution)/shard_map/ppermute | solution.py:23
  70.8 1.0 copy-start.10
  70.9 1.3 copy-start.3
  78.8 29.4 %all-to-all-start.1 = ((bf16[32,40,256]{2,1,0:T(8,128)(2,1)}), bf16[32,40,256]{2,1,0:T(8,128)(2,1)S(1)}, u32[]{:S(2)}, u32[]{:S(2)}) async-start(bf16[32,40,256]{2,1,0:T(8,128)(2,1)} %get-tuple-element.18), calls=%async_computation.1 | async-start | bytes 1310720 | tf_op jit(solution)/shard_map/all_to_all | solution.py:356
  90.2 3.9 %collective-permute-start.5 = (bf16[1024,256]{1,0:T(8,128)(2,1)S(1)}, bf16[1024,256]{1,0:T(8,128)(2,1)S(1)}, u32[]{:S(2)}, u32[]{:S(2)}) collective-permute-start(bf16[1024,256]{1,0:T(8,128)(2,1)S(1)} %get-tuple-element.17), channel_id=1, source_target_pairs={{0,1},{1,0},{2,3},{3,2},{4,5},{5,4},{6,7},{7,6},{8,9},{9,8},{10,11... | collective-permute-start | bytes 1572872 | tf_op jit(solution)/shard_map/ppermute | solution.py:23
  94.3 23.6 %collective-permute-start.6 = (bf16[256,256]{1,0:T(8,128)(2,1)S(1)}, bf16[256,256]{1,0:T(8,128)(2,1)S(1)}, u32[]{:S(2)}, u32[]{:S(2)}) collective-permute-start(bf16[256,256]{1,0:T(8,128)(2,1)S(1)} %get-tuple-element.21), channel_id=1, source_target_pairs={{0,4},{1,5},{2,6},{3,7},{4,8},{5,9},{6,10},{7,11},{8,12},{9,13},{1... | collective-permute-start | bytes 393224 | tf_op jit(solution)/shard_map/ppermute | solution.py:38
  98.1 19.7 %collective-permute-start.8 = (bf16[256,256]{1,0:T(8,128)(2,1)S(1)}, bf16[256,256]{1,0:T(8,128)(2,1)S(1)}, u32[]{:S(2)}, u32[]{:S(2)}) collective-permute-start(bf16[256,256]{1,0:T(8,128)(2,1)S(1)} %get-tuple-element.22), channel_id=1, source_target_pairs={{0,12},{1,13},{2,14},{3,15},{4,0},{5,1},{6,2},{7,3},{8,4},{9,5},{1... | collective-permute-start | bytes 393224 | tf_op jit(solution)/shard_map/ppermute | solution.py:38
  100.8 17.1 %collective-permute-start.7 = (bf16[256,256]{1,0:T(8,128)(2,1)S(1)}, bf16[256,256]{1,0:T(8,128)(2,1)S(1)}, u32[]{:S(2)}, u32[]{:S(2)}) collective-permute-start(bf16[256,256]{1,0:T(8,128)(2,1)S(1)} %get-tuple-element.23), channel_id=1, source_target_pairs={{0,8},{1,9},{2,10},{3,11},{4,12},{5,13},{6,14},{7,15},{8,0},{9,1},... | collective-permute-start | bytes 393224 | tf_op jit(solution)/shard_map/ppermute | solution.py:38
  109.0 18.6 %all-to-all-start.2 = ((bf16[16,8,256]{2,1,0:T(8,128)(2,1)}), bf16[16,8,256]{2,1,0:T(8,128)(2,1)S(1)}, u32[]{:S(2)}, u32[]{:S(2)}) async-start(bf16[16,8,256]{2,1,0:T(8,128)(2,1)} %broadcast_in_dim.14), calls=%async_computation.2 | async-start | bytes 131072 | tf_op jit(solution)/shard_map/all_to_all | solution.py:19
  117.9 15.8 %collective-permute-start.9 = (bf16[128,256]{1,0:T(8,128)(2,1)S(1)}, bf16[128,256]{1,0:T(8,128)(2,1)S(1)}, u32[]{:S(2)}, u32[]{:S(2)}) collective-permute-start(bf16[128,256]{1,0:T(8,128)(2,1)S(1)} %slice.55), channel_id=1, source_target_pairs={{0,2},{1,3},{2,0},{3,1},{4,6},{5,7},{6,4},{7,5},{8,10},{9,11},{10,... | collective-permute-start | bytes 196616 | tf_op jit(solution)/shard_map/ppermute | solution.py:23
  128.3 15.3 %all-to-all-start.3 = ((bf16[32,8,256]{2,1,0:T(8,128)(2,1)}), bf16[32,8,256]{2,1,0:T(8,128)(2,1)S(1)}, u32[]{:S(2)}, u32[]{:S(2)}) async-start(bf16[32,8,256]{2,1,0:T(8,128)(2,1)} %broadcast_in_dim.15), calls=%async_computation.3 | async-start | bytes 262144 | tf_op jit(solution)/shard_map/all_to_all | solution.py:19

commit v7 on v6

--- a/solution.py
+++ b/solution.py
@@ -9,6 +9,7 @@
 
 slot_block = 16
 unroll = 4
+step = 256
 core_bit = 1
 side_bit = 2
 ring_step = 4
@@ -164,20 +165,36 @@
 
 
 def assemble_kernel(*refs):
-    *parts, near = refs
+    *parts, near, sems = refs
     rows = parts[0].shape[0] // 4
     table = near.shape[0] // 2
+    copies = []
     for index, part in enumerate(parts):
-        for side in range(2):
-            place = (2 * index + side) * rows
-            near[pl.ds(place, rows)] = part[pl.ds(2 * side * rows, rows)]
-            near[pl.ds(table + place, rows)] = part[pl.ds((2 * side + 1) * rows, rows)]
+        for quarter in range(4):
+            side, kind = divmod(quarter, 2)
+            place = kind * table + (2 * index + side) * rows
+            copies.append(
+                pltpu.make_async_copy(
+                    part.at[pl.ds(quarter * rows, rows)],
+                    near.at[pl.ds(place, rows)],
+                    sems.at[4 * index + quarter],
+                )
+            )
+    for copy in copies:
+        copy.start()
+    for copy in copies:
+        copy.wait()
 
 
 def assemble(parts):
     rows, width = parts[0].shape
-    shape = jax.ShapeDtypeStruct((len(parts) * rows, width), parts[0].dtype)
-    return pl.pallas_call(assemble_kernel, out_shape=shape, name="assemble")(*map(in_main, parts))
+    return pl.pallas_call(
+        assemble_kernel,
+        out_shape=jax.ShapeDtypeStruct((len(parts) * rows, width), parts[0].dtype),
+        compiler_params=pltpu.CompilerParams(vmem_limit_bytes=8 << 20),
+        scratch_shapes=[pltpu.SemaphoreType.DMA((4 * len(parts),))],
+        name="assemble",
+    )(*parts)
 
 
 def lay_out_kernel(grad_user, user_emb, grad_item, item_emb, mine, pair, pieces):
@@ -216,48 +233,66 @@
 def finish_kernel(
     dense_near,
     dense_far,
-    item_in,
+    item_rows,
     near_in,
     far_in,
     user_near,
     user_far,
     pieces,
     dense,
-    item_rows,
     sources,
+    users,
     q_turned,
-    sems,
+    source_sems,
+    dense_sems,
+    user_sems,
 ):
     low = jnp.bfloat16
     peers, both_rows, width = item_rows.shape
     piece_rows = both_rows // 2
     half_rows, all_items = dense.shape[1:]
-    step = 256
-    item_copy = pltpu.make_async_copy(item_in, item_rows, sems.at[0])
-    dense_copies = [
-        pltpu.make_async_copy(ref, dense.at[half], sems.at[1 + half])
-        for half, ref in enumerate((dense_near, dense_far))
-    ]
+    tiles = half_rows // step
     source_copies = [
-        pltpu.make_async_copy(ref, sources.at[half], sems.at[3 + half])
+        pltpu.make_async_copy(ref, sources.at[half], source_sems.at[half])
         for half, ref in enumerate((near_in, far_in))
     ]
-    item_copy.start()
+    dense_copies = []
+    user_copies = []
     for half in range(2):
-        dense_copies[half].start()
+        for tile in range(tiles):
+            rows = pl.ds(tile * step, step)
+            index = half * tiles + tile
+            dense_copies.append(
+                pltpu.make_async_copy(
+                    (dense_near, dense_far)[half].at[rows],
+                    dense.at[half, rows],
+                    dense_sems.at[index],
+                )
+            )
+            user_copies.append(
+                pltpu.make_async_copy(
+                    users.at[half, rows],
+                    (user_near, user_far)[half].at[rows],
+                    user_sems.at[index],
+                )
+            )
+    for half in range(2):
+        for copy in dense_copies[half * tiles : (half + 1) * tiles]:
+            copy.start()
         source_copies[half].start()
-    item_copy.wait()
     items = item_rows[:, :piece_rows].reshape(all_items, width)
     weight_term = jnp.zeros((width, width), jnp.float32)
-    for half, user in enumerate((user_near, user_far)):
-        dense_copies[half].wait()
-        for start in range(0, half_rows, step):
-            rows = dense[half, start : start + step]
-            user[start : start + step] = jnp.dot(
-                rows, items, preferred_element_type=jnp.float32
+    for half in range(2):
+        for tile in range(tiles):
+            dense_copies[half * tiles + tile].wait()
+            rows = pl.ds(tile * step, step)
+            users[half, rows] = jnp.dot(
+                dense[half, rows], items, preferred_element_type=jnp.float32
             ).astype(low)
         source_copies[half].wait()
-        weight_term += transposed_product(sources[half, half_rows:], user[...])
+        weight_term += transposed_product(sources[half, half_rows:], users[half])
+        for copy in user_copies[half * tiles : (half + 1) * tiles]:
+            copy.start()
         turned = sources[half, :half_rows].T
         for start in range(0, all_items, step):
             part = jnp.dot(
@@ -272,6 +307,8 @@
     weight_term += jnp.dot(q_low, table, preferred_element_type=jnp.float32).T
     pieces[:, :piece_rows] = q_turned[...].T.astype(low).reshape(peers, piece_rows, width)
     pieces[:, piece_rows:] = weight_term.reshape(peers, width // peers, width).astype(low)
+    for copy in user_copies:
+        copy.wait()
 
 
 def finish(dense_near, dense_far, item_pieces, near, far):
@@ -279,10 +316,13 @@
     peers, both_rows, width = item_pieces.shape
     low = jnp.bfloat16
     strip = both_rows // 2 + width // peers
-    in_place = pl.BlockSpec(memory_space=pltpu.HBM)
+    in_place = pl.BlockSpec(memory_space=pl.ANY)
+    in_core = pl.BlockSpec(memory_space=pltpu.VMEM)
+    tiles = half_rows // step
     return pl.pallas_call(
         finish_kernel,
-        in_specs=[in_place] * 5,
+        in_specs=[in_place, in_place, in_core, in_place, in_place],
+        out_specs=[in_place, in_place, in_core],
         out_shape=[
             jax.ShapeDtypeStruct((half_rows, width), low),
             jax.ShapeDtypeStruct((half_rows, width), low),
@@ -290,10 +330,12 @@
         ],
         scratch_shapes=[
             pltpu.VMEM((2, half_rows, all_items), low),
-            pltpu.VMEM((peers, both_rows, width), low),
             pltpu.VMEM((2, 2 * half_rows, width), low),
+            pltpu.VMEM((2, half_rows, width), low),
             pltpu.VMEM((width, all_items), jnp.float32),
-            pltpu.SemaphoreType.DMA((5,)),
+            pltpu.SemaphoreType.DMA((2,)),
+            pltpu.SemaphoreType.DMA((2 * tiles,)),
+            pltpu.SemaphoreType.DMA((2 * tiles,)),
         ],
         compiler_params=pltpu.CompilerParams(vmem_limit_bytes=32 << 20),
         cost_estimate=pl.CostEstimate(
@@ -302,7 +344,7 @@
             transcendentals=0,
         ),
         name="finish",
-    )(*map(in_main, (dense_near, dense_far, item_pieces, near, far)))
+    )(in_main(dense_near), in_main(dense_far), item_pieces, in_main(near), in_main(far))
 
 
 def product(spec, left, right):

time: 145 us -> 146 us (level)
  Pallas kernels: 15.9 us -> 17.7 us
    pallas_call x2, Pallas kernels: 8.9 us -> 10.6 us  [the longest x1 9.15 us: finish(): pl.pallas_call(finish_kernel, in_specs=[in_place, in_place, in_core, in_p...]
  transfers between devices with their start and end apart: 14 -> 14, of which waited for: 7 -> 7; matrix products, arithmetic and copies ran while one was open for 2% -> 2% of each run, Pallas kernels for 5% -> 4%
where the time goes in v7:
time: 146 us; the launch traced here: 145 us
  starting transfers between devices  79.2 us (54%)
  waiting for transfers between devices  41.5 us (28%)
  Pallas kernels  17.7 us (12%)
  local copies, waits for them, and re-layouts  2.34 us (2%)
  matrix products  1.62 us (1%)
  between operations  1.61 us (1%)
    ppermute x4, waiting for transfers between devices, partner(): lax.ppermute(value, 'ia', [(i, i ^ bit) for i in range(lax.axis_size('ia'...  19.9 us
    ppermute x4, starting transfers between devices, partner(): lax.ppermute(value, 'ia', [(i, i ^ bit) for i in range(lax.axis_size('ia'...  18.4 us
    all_to_all x1, starting transfers between devices, device_step(): lax.all_to_all(item_sent, 'au', split_axis=0, concat_axis=0, tiled=True)  14.4 us
    all_to_all x2, starting transfers between devices, from_everyone(): return lax.all_to_all(copies, axis, split_axis=0, concat_axis=0, tiled=True)  14.3 us
    all_to_all x1, starting transfers between devices, device_step(): lax.all_to_all(pieces, 'au', split_axis=0, concat_axis=0, tiled=True)  11.4 us
    all_to_all x2, waiting for transfers between devices, from_everyone(): return lax.all_to_all(copies, axis, split_axis=0, concat_axis=0, tiled=True)  10.7 us
    ppermute x3, starting transfers between devices, from_ahead(): lax.ppermute(value, 'ia', [(ahead(i, distance), i) for i in range(size)])  10.5 us
    ppermute x3, starting transfers between devices, send_ahead(): lax.ppermute(value, 'ia', [(i, ahead(i, distance)) for i in range(size)])  10.1 us
  transfers between devices with their start and end apart: 14, of which 7 were waited for; matrix products, arithmetic and copies ran while one was open for 2% of the time, Pallas kernels for 4%

profile of v7, /device:TPU:1, one launch (start us, length us, event | category | flops | bytes accessed | tf_op | source)
XLA Modules:
  0.0 145.0 jit_solution(3733849517739757942)
XLA Ops:
  0.6 0.0 copy-start
  0.6 2.1 %lay_out.1 = (bf16[256,256]{1,0:T(8,128)(2,1)}, bf16[512,256]{1,0:T(8,128)(2,1)}, bf16[32,64,256]{2,1,0:T(8,128)(2,1)}) custom-call(bf16[128,256]{1,0:T(8,128)(2,1)} %bitcast.23, bf16[128,256]{1,0:T(8,128)(2,1)} %bitcast.24, bf16[32,256]{1,0:T(8,128)(2,1)} %bitcast.25, bf16[32,256]{1,0:T(8,128)(2,1)} %bitcast.26), custom_call_target="tpu_custom_call" | custom-call | tf_op jit(solution)/shard_map/lay_out/pallas_call | solution.py:216
  2.7 0.0 copy-start.3
  2.7 0.0 copy-start.4
  2.8 14.4 %all-to-all-start = ((bf16[32,64,256]{2,1,0:T(8,128)(2,1)}), bf16[32,64,256]{2,1,0:T(8,128)(2,1)S(1)}, u32[]{:S(2)}, u32[]{:S(2)}) async-start(bf16[32,64,256]{2,1,0:T(8,128)(2,1)} %get-tuple-element.13), calls=%async_computation | async-start | bytes 2097152 | tf_op jit(solution)/shard_map/all_to_all | solution.py:380
  17.2 0.0 copy-done.7
  17.2 4.8 %collective-permute-start = (bf16[256,256]{1,0:T(8,128)(2,1)S(1)}, bf16[256,256]{1,0:T(8,128)(2,1)S(1)}, u32[]{:S(2)}, u32[]{:S(2)}) collective-permute-start(bf16[256,256]{1,0:T(8,128)(2,1)S(1)} %copy-done.7), channel_id=1, source_target_pairs={{0,2},{1,3},{2,0},{3,1},{4,6},{5,7},{6,4},{7,5},{8,10},{9,11},{10,... | collective-permute-start | bytes 393224 | tf_op jit(solution)/shard_map/ppermute | solution.py:24
  22.0 18.4 %collective-permute-done = bf16[256,256]{1,0:T(8,128)(2,1)S(1)} collective-permute-done((bf16[256,256]{1,0:T(8,128)(2,1)S(1)}, bf16[256,256]{1,0:T(8,128)(2,1)S(1)}, u32[]{:S(2)}, u32[]{:S(2)}) %collective-permute-start) | collective-permute-done | bytes 131104 | tf_op jit(solution)/shard_map/ppermute | solution.py:24
  40.4 0.0 copy-done.2
  40.4 3.1 %collective-permute-start.3 = (bf16[512,256]{1,0:T(8,128)(2,1)S(1)}, bf16[512,256]{1,0:T(8,128)(2,1)S(1)}, u32[]{:S(2)}, u32[]{:S(2)}) collective-permute-start(bf16[512,256]{1,0:T(8,128)(2,1)S(1)} %constant_dynamic-update-slice_fusion.refs_0_), channel_id=1, source_target_pairs={{12,0},{13,1},{14,2},{15,3},{0,4},{1,5},{2,6},{3,7},{4,8},{5,9},{6... | collective-permute-start | bytes 786440 | tf_op jit(solution)/shard_map/ppermute | solution.py:34
  43.5 4.4 %collective-permute-start.2 = (bf16[512,256]{1,0:T(8,128)(2,1)S(1)}, bf16[512,256]{1,0:T(8,128)(2,1)S(1)}, u32[]{:S(2)}, u32[]{:S(2)}) collective-permute-start(bf16[512,256]{1,0:T(8,128)(2,1)S(1)} %constant_dynamic-update-slice_fusion.refs_0_), channel_id=1, source_target_pairs={{8,0},{9,1},{10,2},{11,3},{12,4},{13,5},{14,6},{15,7},{0,8},{1,9},... | collective-permute-start | bytes 786440 | tf_op jit(solution)/shard_map/ppermute | solution.py:34
  47.9 3.1 %collective-permute-start.1 = (bf16[512,256]{1,0:T(8,128)(2,1)S(1)}, bf16[512,256]{1,0:T(8,128)(2,1)S(1)}, u32[]{:S(2)}, u32[]{:S(2)}) collective-permute-start(bf16[512,256]{1,0:T(8,128)(2,1)S(1)} %constant_dynamic-update-slice_fusion.refs_0_), channel_id=1, source_target_pairs={{4,0},{5,1},{6,2},{7,3},{8,4},{9,5},{10,6},{11,7},{12,8},{13,9},{1... | collective-permute-start | bytes 786440 | tf_op jit(solution)/shard_map/ppermute | solution.py:34
  50.9 0.0 collective-permute-done.3.refs_3_
  51.0 5.2 %collective-permute-done.2.refs_2_ = bf16[512,256]{1,0:T(8,128)(2,1)S(1)} collective-permute-done((bf16[512,256]{1,0:T(8,128)(2,1)S(1)}, bf16[512,256]{1,0:T(8,128)(2,1)S(1)}, u32[]{:S(2)}, u32[]{:S(2)}) %collective-permute-start.2) | collective-permute-done | bytes 262176 | tf_op jit(solution)/shard_map/ppermute | solution.py:34
  56.1 2.0 %collective-permute-done.1.refs_1_ = bf16[512,256]{1,0:T(8,128)(2,1)S(1)} collective-permute-done((bf16[512,256]{1,0:T(8,128)(2,1)S(1)}, bf16[512,256]{1,0:T(8,128)(2,1)S(1)}, u32[]{:S(2)}, u32[]{:S(2)}) %collective-permute-start.1) | collective-permute-done | bytes 262176 | tf_op jit(solution)/shard_map/ppermute | solution.py:34
  58.1 1.5 %assemble.1.near_in = bf16[2048,256]{1,0:T(8,128)(2,1)S(1)} custom-call(bf16[512,256]{1,0:T(8,128)(2,1)S(1)} %constant_dynamic-update-slice_fusion.refs_0_, bf16[512,256]{1,0:T(8,128)(2,1)S(1)} %collective-permute-done.1.refs_1_, bf16[512,256]{1,0:T(8,128)(2,1)S(1)} %collective-permute-done.2.refs_2_, bf16[512,256]{1,0:T(8,128)(2,1)S(1)} %collective-permute-done.3.refs_3_), custom_call_target="tpu_custom_call" | custom-call | tf_op jit(solution)/shard_map/assemble/pallas_call | solution.py:191
  59.6 0.0 copy-start.1
  59.6 4.1 %collective-permute-start.4 = (bf16[2048,256]{1,0:T(8,128)(2,1)S(1)}, bf16[2048,256]{1,0:T(8,128)(2,1)S(1)}, u32[]{:S(2)}, u32[]{:S(2)}) collective-permute-start(bf16[2048,256]{1,0:T(8,128)(2,1)S(1)} %assemble.1.near_in), channel_id=1, source_target_pairs={{0,1},{1,0},{2,3},{3,2},{4,5},{5,4},{6,7},{7,6},{8,9},{9,8},{10,11... | collective-permute-start | bytes 3145736 | tf_op jit(solution)/shard_map/ppermute | solution.py:24
  64.4 0.0 copy-done.5
  64.4 4.9 %dense_block.1 = (bf16[1024,1024]{1,0:T(8,128)(2,1)}, bf16[1024,1024]{1,0:T(8,128)(2,1)}) custom-call(s32[128]{0:T(128)S(1)} %add_bitcast_fusion.rows, s32[128]{0:T(128)S(1)} %bitcast.20, s32[128]{0:T(128)S(1)} %bitcast.21, s32[1]{0:T(128)} %bitcast.19.count, bf16[128,128,128]{2,1,0:T(8,128)(2,1)} %bitcast.22), custom_call_target="tpu_custom_call" | custom-call | flops 8388608 | bytes 8388608 | tf_op jit(solution)/shard_map/dense_block/pallas_call | solution.py:141
  69.4 0.0 collective-permute-done.4.far_in
  69.4 0.0 all-to-all-done.item_rows
  69.4 1.0 copy-done.6
  70.4 9.1 %finish.1 = (bf16[1024,256]{1,0:T(8,128)(2,1)S(1)}, bf16[1024,256]{1,0:T(8,128)(2,1)S(1)}, bf16[32,40,256]{2,1,0:T(8,128)(2,1)}) custom-call(bf16[1024,1024]{1,0:T(8,128)(2,1)} %get-tuple-element.11.dense_near, bf16[1024,1024]{1,0:T(8,128)(2,1)} %get-tuple-element.12.dense_far, bf16[32,64,256]{2,1,0:T(8,128)(2,1)S(1)} %all-to-all-done.item_rows, ...), custom_call_target="tpu_custom_call" | custom-call | flops 2147483648 | bytes 6291456 | tf_op jit(solution)/shard_map/finish/pallas_call | solution.py:322
  79.5 11.4 %all-to-all-start.1 = ((bf16[32,40,256]{2,1,0:T(8,128)(2,1)}), bf16[32,40,256]{2,1,0:T(8,128)(2,1)S(1)}, u32[]{:S(2)}, u32[]{:S(2)}) async-start(bf16[32,40,256]{2,1,0:T(8,128)(2,1)} %get-tuple-element.18), calls=%async_computation.1 | async-start | bytes 1310720 | tf_op jit(solution)/shard_map/all_to_all | solution.py:398
  90.9 2.4 %collective-permute-start.5 = (bf16[1024,256]{1,0:T(8,128)(2,1)S(1)}, bf16[1024,256]{1,0:T(8,128)(2,1)S(1)}, u32[]{:S(2)}, u32[]{:S(2)}) collective-permute-start(bf16[1024,256]{1,0:T(8,128)(2,1)S(1)} %get-tuple-element.17), channel_id=1, source_target_pairs={{0,1},{1,0},{2,3},{3,2},{4,5},{5,4},{6,7},{7,6},{8,9},{9,8},{10,11... | collective-permute-start | bytes 1572872 | tf_op jit(solution)/shard_map/ppermute | solution.py:24
  93.3 1.5 %collective-permute-done.5 = bf16[1024,256]{1,0:T(8,128)(2,1)S(1)} collective-permute-done((bf16[1024,256]{1,0:T(8,128)(2,1)S(1)}, bf16[1024,256]{1,0:T(8,128)(2,1)S(1)}, u32[]{:S(2)}, u32[]{:S(2)}) %collective-permute-start.5) | collective-permute-done | bytes 524320 | tf_op jit(solution)/shard_map/ppermute | solution.py:24
  94.8 0.1 fusion.5
  95.0 3.8 %collective-permute-start.6 = (bf16[256,256]{1,0:T(8,128)(2,1)S(1)}, bf16[256,256]{1,0:T(8,128)(2,1)S(1)}, u32[]{:S(2)}, u32[]{:S(2)}) collective-permute-start(bf16[256,256]{1,0:T(8,128)(2,1)S(1)} %get-tuple-element.21), channel_id=1, source_target_pairs={{0,4},{1,5},{2,6},{3,7},{4,8},{5,9},{6,10},{7,11},{8,12},{9,13},{1... | collective-permute-start | bytes 393224 | tf_op jit(solution)/shard_map/ppermute | solution.py:39
  98.8 2.7 %collective-permute-start.8 = (bf16[256,256]{1,0:T(8,128)(2,1)S(1)}, bf16[256,256]{1,0:T(8,128)(2,1)S(1)}, u32[]{:S(2)}, u32[]{:S(2)}) collective-permute-start(bf16[256,256]{1,0:T(8,128)(2,1)S(1)} %get-tuple-element.22), channel_id=1, source_target_pairs={{0,12},{1,13},{2,14},{3,15},{4,0},{5,1},{6,2},{7,3},{8,4},{9,5},{1... | collective-permute-start | bytes 393224 | tf_op jit(solution)/shard_map/ppermute | solution.py:39
  101.5 3.6 %collective-permute-start.7 = (bf16[256,256]{1,0:T(8,128)(2,1)S(1)}, bf16[256,256]{1,0:T(8,128)(2,1)S(1)}, u32[]{:S(2)}, u32[]{:S(2)}) collective-permute-start(bf16[256,256]{1,0:T(8,128)(2,1)S(1)} %get-tuple-element.23), channel_id=1, source_target_pairs={{0,8},{1,9},{2,10},{3,11},{4,12},{5,13},{6,14},{7,15},{8,0},{9,1},... | collective-permute-start | bytes 393224 | tf_op jit(solution)/shard_map/ppermute | solution.py:39
  105.1 3.8 %all-to-all-done.1 = bf16[32,40,256]{2,1,0:T(8,128)(2,1)S(1)} async-done(((bf16[32,40,256]{2,1,0:T(8,128)(2,1)}), bf16[32,40,256]{2,1,0:T(8,128)(2,1)S(1)}, u32[]{:S(2)}, u32[]{:S(2)}) %all-to-all-start.1) | async-done | bytes 655392 | tf_op jit(solution)/shard_map/all_to_all | solution.py:398
  108.9 0.1 reduce
  109.0 0.6 broadcast_in_dim.14
  109.7 8.9 %all-to-all-start.2 = ((bf16[16,8,256]{2,1,0:T(8,128)(2,1)}), bf16[16,8,256]{2,1,0:T(8,128)(2,1)S(1)}, u32[]{:S(2)}, u32[]{:S(2)}) async-start(bf16[16,8,256]{2,1,0:T(8,128)(2,1)} %broadcast_in_dim.14), calls=%async_computation.2 | async-start | bytes 131072 | tf_op jit(solution)/shard_map/all_to_all | solution.py:20
  118.5 0.0 collective-permute-done.6
  118.6 0.0 collective-permute-done.8
  118.6 0.0 collective-permute-done.7
  118.6 0.1 slice_add_fusion
  118.7 7.2 %collective-permute-start.9 = (bf16[128,256]{1,0:T(8,128)(2,1)S(1)}, bf16[128,256]{1,0:T(8,128)(2,1)S(1)}, u32[]{:S(2)}, u32[]{:S(2)}) collective-permute-start(bf16[128,256]{1,0:T(8,128)(2,1)S(1)} %slice.55), channel_id=1, source_target_pairs={{0,2},{1,3},{2,0},{3,1},{4,6},{5,7},{6,4},{7,5},{8,10},{9,11},{10,... | collective-permute-start | bytes 196616 | tf_op jit(solution)/shard_map/ppermute | solution.py:24
  125.8 2.4 %all-to-all-done.2 = bf16[16,8,256]{2,1,0:T(8,128)(2,1)S(1)} async-done(((bf16[16,8,256]{2,1,0:T(8,128)(2,1)}), bf16[16,8,256]{2,1,0:T(8,128)(2,1)S(1)}, u32[]{:S(2)}, u32[]{:S(2)}) %all-to-all-start.2) | async-done | bytes 65568 | tf_op jit(solution)/shard_map/all_to_all | solution.py:20
  128.3 0.7 broadcast_in_dim.15
  129.0 5.4 %all-to-all-start.3 = ((bf16[32,8,256]{2,1,0:T(8,128)(2,1)}), bf16[32,8,256]{2,1,0:T(8,128)(2,1)S(1)}, u32[]{:S(2)}, u32[]{:S(2)}) async-start(bf16[32,8,256]{2,1,0:T(8,128)(2,1)} %broadcast_in_dim.15), calls=%async_computation.3 | async-start | bytes 262144 | tf_op jit(solution)/shard_map/all_to_all | solution.py:20
  134.4 0.0 collective-permute-done.9
  134.4 0.8 fusion
  135.3 0.8 fusion.1
  136.0 8.2 %all-to-all-done.3 = bf16[32,8,256]{2,1,0:T(8,128)(2,1)S(1)} async-done(((bf16[32,8,256]{2,1,0:T(8,128)(2,1)}), bf16[32,8,256]{2,1,0:T(8,128)(2,1)S(1)}, u32[]{:S(2)}, u32[]{:S(2)}) %all-to-all-start.3) | async-done | bytes 131104 | tf_op jit(solution)/shard_map/all_to_all | solution.py:20
  144.3 0.7 bitcast_convert_fusion
  (15 shorter events, 0.1 us)
Async XLA Ops:
  0.6 133.8 %copy-start = (bf16[256,256]{1,0:T(8,128)(2,1)S(1)}, bf16[256,256]{1,0:T(8,128)(2,1)}, u32[]{:S(2)}) copy-start(bf16[256,256]{1,0:T(8,128)(2,1)} %param.12) | copy-start | bytes 393220
  2.7 14.5 %copy-start.7 = (bf16[256,256]{1,0:T(8,128)(2,1)S(1)}, bf16[256,256]{1,0:T(8,128)(2,1)}, u32[]{:S(2)}) copy-start(bf16[256,256]{1,0:T(8,128)(2,1)} %get-tuple-element.15) | copy-start | bytes 393220
  2.7 37.6 %copy-start.2 = (bf16[512,256]{1,0:T(8,128)(2,1)S(1)}, bf16[512,256]{1,0:T(8,128)(2,1)}, u32[]{:S(2)}) copy-start(bf16[512,256]{1,0:T(8,128)(2,1)} %get-tuple-element.14) | copy-start | bytes 786436
  2.7 61.7 %copy-start.5 = (s32[1,128]{1,0:T(1,128)S(1)}, s32[1,128]{1,0:T(1,128)}, u32[]{:S(2)}) copy-start(s32[1,128]{1,0:T(1,128)} %param.16) | copy-start | bytes 1540
  2.7 61.7 %copy-start.3 = (s32[1,128]{1,0:T(1,128)S(1)}, s32[1,128]{1,0:T(1,128)}, u32[]{:S(2)}) copy-start(s32[1,128]{1,0:T(1,128)} %param.17) | copy-start | bytes 1540
  2.7 61.7 %copy-start.4 = (s32[1,128]{1,0:T(1,128)S(1)}, s32[1,128]{1,0:T(1,128)}, u32[]{:S(2)}) copy-start(s32[1,128]{1,0:T(1,128)} %param.18) | copy-start | bytes 1540
  2.8 66.7 %all-to-all-start = ((bf16[32,64,256]{2,1,0:T(8,128)(2,1)}), bf16[32,64,256]{2,1,0:T(8,128)(2,1)S(1)}, u32[]{:S(2)}, u32[]{:S(2)}) async-start(bf16[32,64,256]{2,1,0:T(8,128)(2,1)} %get-tuple-element.13), calls=%async_computation | async-start | bytes 2097152 | tf_op jit(solution)/shard_map/all_to_all | solution.py:380
  17.2 23.2 %collective-permute-start = (bf16[256,256]{1,0:T(8,128)(2,1)S(1)}, bf16[256,256]{1,0:T(8,128)(2,1)S(1)}, u32[]{:S(2)}, u32[]{:S(2)}) collective-permute-start(bf16[256,256]{1,0:T(8,128)(2,1)S(1)} %copy-done.7), channel_id=1, source_target_pairs={{0,2},{1,3},{2,0},{3,1},{4,6},{5,7},{6,4},{7,5},{8,10},{9,11},{10,... | collective-permute-start | bytes 393224 | tf_op jit(solution)/shard_map/ppermute | solution.py:24
  40.4 10.6 %collective-permute-start.3 = (bf16[512,256]{1,0:T(8,128)(2,1)S(1)}, bf16[512,256]{1,0:T(8,128)(2,1)S(1)}, u32[]{:S(2)}, u32[]{:S(2)}) collective-permute-start(bf16[512,256]{1,0:T(8,128)(2,1)S(1)} %constant_dynamic-update-slice_fusion.refs_0_), channel_id=1, source_target_pairs={{12,0},{13,1},{14,2},{15,3},{0,4},{1,5},{2,6},{3,7},{4,8},{5,9},{6... | collective-permute-start | bytes 786440 | tf_op jit(solution)/shard_map/ppermute | solution.py:34
  43.5 12.6 %collective-permute-start.2 = (bf16[512,256]{1,0:T(8,128)(2,1)S(1)}, bf16[512,256]{1,0:T(8,128)(2,1)S(1)}, u32[]{:S(2)}, u32[]{:S(2)}) collective-permute-start(bf16[512,256]{1,0:T(8,128)(2,1)S(1)} %constant_dynamic-update-slice_fusion.refs_0_), channel_id=1, source_target_pairs={{8,0},{9,1},{10,2},{11,3},{12,4},{13,5},{14,6},{15,7},{0,8},{1,9},... | collective-permute-start | bytes 786440 | tf_op jit(solution)/shard_map/ppermute | solution.py:34
  47.9 10.2 %collective-permute-start.1 = (bf16[512,256]{1,0:T(8,128)(2,1)S(1)}, bf16[512,256]{1,0:T(8,128)(2,1)S(1)}, u32[]{:S(2)}, u32[]{:S(2)}) collective-permute-start(bf16[512,256]{1,0:T(8,128)(2,1)S(1)} %constant_dynamic-update-slice_fusion.refs_0_), channel_id=1, source_target_pairs={{4,0},{5,1},{6,2},{7,3},{8,4},{9,5},{10,6},{11,7},{12,8},{13,9},{1... | collective-permute-start | bytes 786440 | tf_op jit(solution)/shard_map/ppermute | solution.py:34
  59.6 9.8 %copy-start.1 = (bf16[2048,256]{1,0:T(8,128)(2,1)}, bf16[2048,256]{1,0:T(8,128)(2,1)S(1)}, u32[]{:S(2)}) copy-start(bf16[2048,256]{1,0:T(8,128)(2,1)S(1)} %assemble.1.near_in) | copy-start | bytes 3145732
  59.6 9.8 %collective-permute-start.4 = (bf16[2048,256]{1,0:T(8,128)(2,1)S(1)}, bf16[2048,256]{1,0:T(8,128)(2,1)S(1)}, u32[]{:S(2)}, u32[]{:S(2)}) collective-permute-start(bf16[2048,256]{1,0:T(8,128)(2,1)S(1)} %assemble.1.near_in), channel_id=1, source_target_pairs={{0,1},{1,0},{2,3},{3,2},{4,5},{5,4},{6,7},{7,6},{8,9},{9,8},{10,11... | collective-permute-start | bytes 3145736 | tf_op jit(solution)/shard_map/ppermute | solution.py:24
  69.4 1.0 copy-start.6
  79.5 29.4 %all-to-all-start.1 = ((bf16[32,40,256]{2,1,0:T(8,128)(2,1)}), bf16[32,40,256]{2,1,0:T(8,128)(2,1)S(1)}, u32[]{:S(2)}, u32[]{:S(2)}) async-start(bf16[32,40,256]{2,1,0:T(8,128)(2,1)} %get-tuple-element.18), calls=%async_computation.1 | async-start | bytes 1310720 | tf_op jit(solution)/shard_map/all_to_all | solution.py:398
  90.9 3.9 %collective-permute-start.5 = (bf16[1024,256]{1,0:T(8,128)(2,1)S(1)}, bf16[1024,256]{1,0:T(8,128)(2,1)S(1)}, u32[]{:S(2)}, u32[]{:S(2)}) collective-permute-start(bf16[1024,256]{1,0:T(8,128)(2,1)S(1)} %get-tuple-element.17), channel_id=1, source_target_pairs={{0,1},{1,0},{2,3},{3,2},{4,5},{5,4},{6,7},{7,6},{8,9},{9,8},{10,11... | collective-permute-start | bytes 1572872 | tf_op jit(solution)/shard_map/ppermute | solution.py:24
  95.0 23.6 %collective-permute-start.6 = (bf16[256,256]{1,0:T(8,128)(2,1)S(1)}, bf16[256,256]{1,0:T(8,128)(2,1)S(1)}, u32[]{:S(2)}, u32[]{:S(2)}) collective-permute-start(bf16[256,256]{1,0:T(8,128)(2,1)S(1)} %get-tuple-element.21), channel_id=1, source_target_pairs={{0,4},{1,5},{2,6},{3,7},{4,8},{5,9},{6,10},{7,11},{8,12},{9,13},{1... | collective-permute-start | bytes 393224 | tf_op jit(solution)/shard_map/ppermute | solution.py:39
  98.8 19.7 %collective-permute-start.8 = (bf16[256,256]{1,0:T(8,128)(2,1)S(1)}, bf16[256,256]{1,0:T(8,128)(2,1)S(1)}, u32[]{:S(2)}, u32[]{:S(2)}) collective-permute-start(bf16[256,256]{1,0:T(8,128)(2,1)S(1)} %get-tuple-element.22), channel_id=1, source_target_pairs={{0,12},{1,13},{2,14},{3,15},{4,0},{5,1},{6,2},{7,3},{8,4},{9,5},{1... | collective-permute-start | bytes 393224 | tf_op jit(solution)/shard_map/ppermute | solution.py:39
  101.5 17.1 %collective-permute-start.7 = (bf16[256,256]{1,0:T(8,128)(2,1)S(1)}, bf16[256,256]{1,0:T(8,128)(2,1)S(1)}, u32[]{:S(2)}, u32[]{:S(2)}) collective-permute-start(bf16[256,256]{1,0:T(8,128)(2,1)S(1)} %get-tuple-element.23), channel_id=1, source_target_pairs={{0,8},{1,9},{2,10},{3,11},{4,12},{5,13},{6,14},{7,15},{8,0},{9,1},... | collective-permute-start | bytes 393224 | tf_op jit(solution)/shard_map/ppermute | solution.py:39
  109.7 18.6 %all-to-all-start.2 = ((bf16[16,8,256]{2,1,0:T(8,128)(2,1)}), bf16[16,8,256]{2,1,0:T(8,128)(2,1)S(1)}, u32[]{:S(2)}, u32[]{:S(2)}) async-start(bf16[16,8,256]{2,1,0:T(8,128)(2,1)} %broadcast_in_dim.14), calls=%async_computation.2 | async-start | bytes 131072 | tf_op jit(solution)/shard_map/all_to_all | solution.py:20
  118.7 15.8 %collective-permute-start.9 = (bf16[128,256]{1,0:T(8,128)(2,1)S(1)}, bf16[128,256]{1,0:T(8,128)(2,1)S(1)}, u32[]{:S(2)}, u32[]{:S(2)}) collective-permute-start(bf16[128,256]{1,0:T(8,128)(2,1)S(1)} %slice.55), channel_id=1, source_target_pairs={{0,2},{1,3},{2,0},{3,1},{4,6},{5,7},{6,4},{7,5},{8,10},{9,11},{10,... | collective-permute-start | bytes 196616 | tf_op jit(solution)/shard_map/ppermute | solution.py:24
  129.0 15.3 %all-to-all-start.3 = ((bf16[32,8,256]{2,1,0:T(8,128)(2,1)}), bf16[32,8,256]{2,1,0:T(8,128)(2,1)S(1)}, u32[]{:S(2)}, u32[]{:S(2)}) async-start(bf16[32,8,256]{2,1,0:T(8,128)(2,1)} %broadcast_in_dim.15), calls=%async_computation.3 | async-start | bytes 262144 | tf_op jit(solution)/shard_map/all_to_all | solution.py:20

commit v8 on v6

--- a/solution.py
+++ b/solution.py
@@ -9,6 +9,7 @@
 
 slot_block = 16
 unroll = 4
+step = 256
 core_bit = 1
 side_bit = 2
 ring_step = 4
@@ -164,45 +165,73 @@
 
 
 def assemble_kernel(*refs):
-    *parts, near = refs
+    *parts, near, sems = refs
     rows = parts[0].shape[0] // 4
     table = near.shape[0] // 2
+    copies = []
     for index, part in enumerate(parts):
-        for side in range(2):
-            place = (2 * index + side) * rows
-            near[pl.ds(place, rows)] = part[pl.ds(2 * side * rows, rows)]
-            near[pl.ds(table + place, rows)] = part[pl.ds((2 * side + 1) * rows, rows)]
+        for quarter in range(4):
+            side, kind = divmod(quarter, 2)
+            place = kind * table + (2 * index + side) * rows
+            copies.append(
+                pltpu.make_async_copy(
+                    part.at[pl.ds(quarter * rows, rows)],
+                    near.at[pl.ds(place, rows)],
+                    sems.at[4 * index + quarter],
+                )
+            )
+    for copy in copies:
+        copy.start()
+    for copy in copies:
+        copy.wait()
 
 
 def assemble(parts):
     rows, width = parts[0].shape
-    shape = jax.ShapeDtypeStruct((len(parts) * rows, width), parts[0].dtype)
-    return pl.pallas_call(assemble_kernel, out_shape=shape, name="assemble")(*map(in_main, parts))
-
-
-def lay_out_kernel(grad_user, user_emb, grad_item, item_emb, mine, pair, pieces):
+    return pl.pallas_call(
+        assemble_kernel,
+        out_shape=jax.ShapeDtypeStruct((len(parts) * rows, width), parts[0].dtype),
+        compiler_params=pltpu.CompilerParams(vmem_limit_bytes=8 << 20),
+        scratch_shapes=[pltpu.SemaphoreType.DMA((4 * len(parts),))],
+        name="assemble",
+    )(*parts)
+
+
+def lay_out_kernel(grad_user, user_emb, grad_item, item_emb, mine, pair, pieces, sems):
     rows = grad_user.shape[0]
-    mine[:rows] = grad_user[...]
-    mine[rows:] = user_emb[...]
-    pair[:rows] = grad_user[...]
-    pair[rows : 2 * rows] = user_emb[...]
-    pair[2 * rows :] = jnp.zeros((2 * rows, pair.shape[1]), pair.dtype)
     item_rows = grad_item.shape[0]
+    moves = []
+    for index, source in enumerate((grad_user, user_emb)):
+        for target in (mine, pair):
+            moves.append((source, target.at[pl.ds(index * rows, rows)]))
+    moves.append((grad_user, pair.at[pl.ds(2 * rows, rows)]))
+    moves.append((user_emb, pair.at[pl.ds(3 * rows, rows)]))
     for peer in range(pieces.shape[0]):
-        pieces[peer, :item_rows] = grad_item[...]
-        pieces[peer, item_rows:] = item_emb[...]
+        for index, source in enumerate((grad_item, item_emb)):
+            moves.append((source, pieces.at[peer, pl.ds(index * item_rows, item_rows)]))
+    copies = [
+        pltpu.make_async_copy(source, target, sems.at[index])
+        for index, (source, target) in enumerate(moves)
+    ]
+    for copy in copies:
+        copy.start()
+    for copy in copies:
+        copy.wait()
 
 
 def lay_out(grad_user, user_emb, grad_item, item_emb):
     peers = lax.axis_size("au")
     rows, width = grad_user.shape
+    in_place = pl.BlockSpec(memory_space=pltpu.HBM)
     return pl.pallas_call(
         lay_out_kernel,
+        out_specs=[in_place] * 3,
         out_shape=[
             jax.ShapeDtypeStruct((2 * rows, width), grad_user.dtype),
             jax.ShapeDtypeStruct((4 * rows, width), grad_user.dtype),
             jax.ShapeDtypeStruct((peers, 2 * grad_item.shape[0], width), grad_item.dtype),
         ],
+        scratch_shapes=[pltpu.SemaphoreType.DMA((6 + 2 * peers,))],
         name="lay_out",
     )(grad_user, user_emb, grad_item, item_emb)
 
@@ -216,14 +245,13 @@
 def finish_kernel(
     dense_near,
     dense_far,
-    item_in,
+    item_rows,
     near_in,
     far_in,
     user_near,
     user_far,
     pieces,
     dense,
-    item_rows,
     sources,
     q_turned,
     sems,
@@ -232,21 +260,17 @@
     peers, both_rows, width = item_rows.shape
     piece_rows = both_rows // 2
     half_rows, all_items = dense.shape[1:]
-    step = 256
-    item_copy = pltpu.make_async_copy(item_in, item_rows, sems.at[0])
     dense_copies = [
-        pltpu.make_async_copy(ref, dense.at[half], sems.at[1 + half])
+        pltpu.make_async_copy(ref, dense.at[half], sems.at[half])
         for half, ref in enumerate((dense_near, dense_far))
     ]
     source_copies = [
-        pltpu.make_async_copy(ref, sources.at[half], sems.at[3 + half])
+        pltpu.make_async_copy(ref, sources.at[half], sems.at[2 + half])
         for half, ref in enumerate((near_in, far_in))
     ]
-    item_copy.start()
     for half in range(2):
         dense_copies[half].start()
         source_copies[half].start()
-    item_copy.wait()
     items = item_rows[:, :piece_rows].reshape(all_items, width)
     weight_term = jnp.zeros((width, width), jnp.float32)
     for half, user in enumerate((user_near, user_far)):
@@ -280,9 +304,10 @@
     low = jnp.bfloat16
     strip = both_rows // 2 + width // peers
     in_place = pl.BlockSpec(memory_space=pltpu.HBM)
+    in_core = pl.BlockSpec(memory_space=pltpu.VMEM)
     return pl.pallas_call(
         finish_kernel,
-        in_specs=[in_place] * 5,
+        in_specs=[in_place, in_place, in_core, in_place, in_place],
         out_shape=[
             jax.ShapeDtypeStruct((half_rows, width), low),
             jax.ShapeDtypeStruct((half_rows, width), low),
@@ -290,10 +315,9 @@
         ],
         scratch_shapes=[
             pltpu.VMEM((2, half_rows, all_items), low),
-            pltpu.VMEM((peers, both_rows, width), low),
             pltpu.VMEM((2, 2 * half_rows, width), low),
             pltpu.VMEM((width, all_items), jnp.float32),
-            pltpu.SemaphoreType.DMA((5,)),
+            pltpu.SemaphoreType.DMA((4,)),
         ],
         compiler_params=pltpu.CompilerParams(vmem_limit_bytes=32 << 20),
         cost_estimate=pl.CostEstimate(
@@ -302,7 +326,7 @@
             transcendentals=0,
         ),
         name="finish",
-    )(*map(in_main, (dense_near, dense_far, item_pieces, near, far)))
+    )(in_main(dense_near), in_main(dense_far), item_pieces, in_main(near), in_main(far))
 
 
 def product(spec, left, right):

time: 145 us -> 143 us (0.986)
  no operation moved by 1% of the time
where the time goes in v8:
time: 143 us
  starting transfers between devices  79.2 us (55%)
  waiting for transfers between devices  41.5 us (29%)
  Pallas kernels  15.3 us (11%)
  local copies, waits for them, and re-layouts  2.35 us (2%)
  between operations  1.64 us (1%)
  matrix products  1.62 us (1%)
    ppermute x4, waiting for transfers between devices, partner(): lax.ppermute(value, 'ia', [(i, i ^ bit) for i in range(lax.axis_size('ia'...  19.9 us
    ppermute x4, starting transfers between devices, partner(): lax.ppermute(value, 'ia', [(i, i ^ bit) for i in range(lax.axis_size('ia'...  18.5 us
    all_to_all x1, starting transfers between devices, device_step(): lax.all_to_all(item_sent, 'au', split_axis=0, concat_axis=0, tiled=True)  14.4 us
    all_to_all x2, starting transfers between devices, from_everyone(): return lax.all_to_all(copies, axis, split_axis=0, concat_axis=0, tiled=True)  14.3 us
    all_to_all x1, starting transfers between devices, device_step(): lax.all_to_all(pieces, 'au', split_axis=0, concat_axis=0, tiled=True)  11.4 us
    all_to_all x2, waiting for transfers between devices, from_everyone(): return lax.all_to_all(copies, axis, split_axis=0, concat_axis=0, tiled=True)  10.7 us
    ppermute x3, starting transfers between devices, from_ahead(): lax.ppermute(value, 'ia', [(ahead(i, distance), i) for i in range(size)])  10.5 us
    ppermute x3, starting transfers between devices, send_ahead(): lax.ppermute(value, 'ia', [(i, ahead(i, distance)) for i in range(size)])  10.1 us
  transfers between devices with their start and end apart: 14, of which 7 were waited for; matrix products, arithmetic and copies ran while one was open for 2% of the time, Pallas kernels for 5%

profile of v8, /device:TPU:1, one launch (start us, length us, event | category | flops | bytes accessed | tf_op | source)
XLA Modules:
  0.0 142.7 jit_solution(9608180048165442467)
XLA Ops:
  0.6 0.0 copy-start
  0.6 2.6 %lay_out.1 = (bf16[256,256]{1,0:T(8,128)(2,1)}, bf16[512,256]{1,0:T(8,128)(2,1)}, bf16[32,64,256]{2,1,0:T(8,128)(2,1)}) custom-call(bf16[128,256]{1,0:T(8,128)(2,1)} %bitcast.23, bf16[128,256]{1,0:T(8,128)(2,1)} %bitcast.24, bf16[32,256]{1,0:T(8,128)(2,1)} %bitcast.25, bf16[32,256]{1,0:T(8,128)(2,1)} %bitcast.26), custom_call_target="tpu_custom_call" | custom-call | tf_op jit(solution)/shard_map/lay_out/pallas_call | solution.py:226
  3.3 0.0 copy-start.7
  3.3 0.0 copy-start.2
  3.3 0.0 copy-start.5
  3.3 0.0 copy-start.3
  3.3 0.0 copy-start.4
  3.3 14.4 %all-to-all-start = ((bf16[32,64,256]{2,1,0:T(8,128)(2,1)}), bf16[32,64,256]{2,1,0:T(8,128)(2,1)S(1)}, u32[]{:S(2)}, u32[]{:S(2)}) async-start(bf16[32,64,256]{2,1,0:T(8,128)(2,1)} %get-tuple-element.13), calls=%async_computation | async-start | bytes 2097152 | tf_op jit(solution)/shard_map/all_to_all | solution.py:362
  17.7 0.0 copy-done.7
  17.8 4.8 %collective-permute-start = (bf16[256,256]{1,0:T(8,128)(2,1)S(1)}, bf16[256,256]{1,0:T(8,128)(2,1)S(1)}, u32[]{:S(2)}, u32[]{:S(2)}) collective-permute-start(bf16[256,256]{1,0:T(8,128)(2,1)S(1)} %copy-done.7), channel_id=1, source_target_pairs={{0,2},{1,3},{2,0},{3,1},{4,6},{5,7},{6,4},{7,5},{8,10},{9,11},{10,... | collective-permute-start | bytes 393224 | tf_op jit(solution)/shard_map/ppermute | solution.py:24
  22.5 18.4 %collective-permute-done = bf16[256,256]{1,0:T(8,128)(2,1)S(1)} collective-permute-done((bf16[256,256]{1,0:T(8,128)(2,1)S(1)}, bf16[256,256]{1,0:T(8,128)(2,1)S(1)}, u32[]{:S(2)}, u32[]{:S(2)}) %collective-permute-start) | collective-permute-done | bytes 131104 | tf_op jit(solution)/shard_map/ppermute | solution.py:24
  40.9 3.1 %collective-permute-start.3 = (bf16[512,256]{1,0:T(8,128)(2,1)S(1)}, bf16[512,256]{1,0:T(8,128)(2,1)S(1)}, u32[]{:S(2)}, u32[]{:S(2)}) collective-permute-start(bf16[512,256]{1,0:T(8,128)(2,1)S(1)} %constant_dynamic-update-slice_fusion.refs_0_), channel_id=1, source_target_pairs={{12,0},{13,1},{14,2},{15,3},{0,4},{1,5},{2,6},{3,7},{4,8},{5,9},{6... | collective-permute-start | bytes 786440 | tf_op jit(solution)/shard_map/ppermute | solution.py:34
  44.1 4.4 %collective-permute-start.2 = (bf16[512,256]{1,0:T(8,128)(2,1)S(1)}, bf16[512,256]{1,0:T(8,128)(2,1)S(1)}, u32[]{:S(2)}, u32[]{:S(2)}) collective-permute-start(bf16[512,256]{1,0:T(8,128)(2,1)S(1)} %constant_dynamic-update-slice_fusion.refs_0_), channel_id=1, source_target_pairs={{8,0},{9,1},{10,2},{11,3},{12,4},{13,5},{14,6},{15,7},{0,8},{1,9},... | collective-permute-start | bytes 786440 | tf_op jit(solution)/shard_map/ppermute | solution.py:34
  48.4 3.1 %collective-permute-start.1 = (bf16[512,256]{1,0:T(8,128)(2,1)S(1)}, bf16[512,256]{1,0:T(8,128)(2,1)S(1)}, u32[]{:S(2)}, u32[]{:S(2)}) collective-permute-start(bf16[512,256]{1,0:T(8,128)(2,1)S(1)} %constant_dynamic-update-slice_fusion.refs_0_), channel_id=1, source_target_pairs={{4,0},{5,1},{6,2},{7,3},{8,4},{9,5},{10,6},{11,7},{12,8},{13,9},{1... | collective-permute-start | bytes 786440 | tf_op jit(solution)/shard_map/ppermute | solution.py:34
  51.5 0.0 collective-permute-done.3.refs_3_
  51.5 5.2 %collective-permute-done.2.refs_2_ = bf16[512,256]{1,0:T(8,128)(2,1)S(1)} collective-permute-done((bf16[512,256]{1,0:T(8,128)(2,1)S(1)}, bf16[512,256]{1,0:T(8,128)(2,1)S(1)}, u32[]{:S(2)}, u32[]{:S(2)}) %collective-permute-start.2) | collective-permute-done | bytes 262176 | tf_op jit(solution)/shard_map/ppermute | solution.py:34
  56.7 2.0 %collective-permute-done.1.refs_1_ = bf16[512,256]{1,0:T(8,128)(2,1)S(1)} collective-permute-done((bf16[512,256]{1,0:T(8,128)(2,1)S(1)}, bf16[512,256]{1,0:T(8,128)(2,1)S(1)}, u32[]{:S(2)}, u32[]{:S(2)}) %collective-permute-start.1) | collective-permute-done | bytes 262176 | tf_op jit(solution)/shard_map/ppermute | solution.py:34
  58.6 1.5 %assemble.1.near_in = bf16[2048,256]{1,0:T(8,128)(2,1)S(1)} custom-call(bf16[512,256]{1,0:T(8,128)(2,1)S(1)} %constant_dynamic-update-slice_fusion.refs_0_, bf16[512,256]{1,0:T(8,128)(2,1)S(1)} %collective-permute-done.1.refs_1_, bf16[512,256]{1,0:T(8,128)(2,1)S(1)} %collective-permute-done.2.refs_2_, bf16[512,256]{1,0:T(8,128)(2,1)S(1)} %collective-permute-done.3.refs_3_), custom_call_target="tpu_custom_call" | custom-call | tf_op jit(solution)/shard_map/assemble/pallas_call | solution.py:191
  60.2 4.1 %collective-permute-start.4 = (bf16[2048,256]{1,0:T(8,128)(2,1)S(1)}, bf16[2048,256]{1,0:T(8,128)(2,1)S(1)}, u32[]{:S(2)}, u32[]{:S(2)}) collective-permute-start(bf16[2048,256]{1,0:T(8,128)(2,1)S(1)} %assemble.1.near_in), channel_id=1, source_target_pairs={{0,1},{1,0},{2,3},{3,2},{4,5},{5,4},{6,7},{7,6},{8,9},{9,8},{10,11... | collective-permute-start | bytes 3145736 | tf_op jit(solution)/shard_map/ppermute | solution.py:24
  65.0 4.9 %dense_block.1 = (bf16[1024,1024]{1,0:T(8,128)(2,1)}, bf16[1024,1024]{1,0:T(8,128)(2,1)}) custom-call(s32[128]{0:T(128)S(1)} %add_bitcast_fusion.rows, s32[128]{0:T(128)S(1)} %bitcast.20, s32[128]{0:T(128)S(1)} %bitcast.21, s32[1]{0:T(128)} %bitcast.19.count, bf16[128,128,128]{2,1,0:T(8,128)(2,1)} %bitcast.22), custom_call_target="tpu_custom_call" | custom-call | flops 8388608 | bytes 8388608 | tf_op jit(solution)/shard_map/dense_block/pallas_call | solution.py:141
  70.0 0.0 collective-permute-done.4.far_in
  70.0 0.0 all-to-all-done.item_rows
  70.0 1.0 copy-done.6
  70.9 6.3 %finish.1 = (bf16[1024,256]{1,0:T(8,128)(2,1)S(1)}, bf16[1024,256]{1,0:T(8,128)(2,1)S(1)}, bf16[32,40,256]{2,1,0:T(8,128)(2,1)}) custom-call(bf16[1024,1024]{1,0:T(8,128)(2,1)} %get-tuple-element.11.dense_near, bf16[1024,1024]{1,0:T(8,128)(2,1)} %get-tuple-element.12.dense_far, bf16[32,64,256]{2,1,0:T(8,128)(2,1)S(1)} %all-to-all-done.item_rows, ...), custom_call_target="tpu_custom_call" | custom-call | flops 2147483648 | bytes 6291456 | tf_op jit(solution)/shard_map/finish/pallas_call | solution.py:308
  77.2 11.4 %all-to-all-start.1 = ((bf16[32,40,256]{2,1,0:T(8,128)(2,1)}), bf16[32,40,256]{2,1,0:T(8,128)(2,1)S(1)}, u32[]{:S(2)}, u32[]{:S(2)}) async-start(bf16[32,40,256]{2,1,0:T(8,128)(2,1)} %get-tuple-element.18), calls=%async_computation.1 | async-start | bytes 1310720 | tf_op jit(solution)/shard_map/all_to_all | solution.py:380
  88.6 2.4 %collective-permute-start.5 = (bf16[1024,256]{1,0:T(8,128)(2,1)S(1)}, bf16[1024,256]{1,0:T(8,128)(2,1)S(1)}, u32[]{:S(2)}, u32[]{:S(2)}) collective-permute-start(bf16[1024,256]{1,0:T(8,128)(2,1)S(1)} %get-tuple-element.17), channel_id=1, source_target_pairs={{0,1},{1,0},{2,3},{3,2},{4,5},{5,4},{6,7},{7,6},{8,9},{9,8},{10,11... | collective-permute-start | bytes 1572872 | tf_op jit(solution)/shard_map/ppermute | solution.py:24
  91.0 1.5 %collective-permute-done.5 = bf16[1024,256]{1,0:T(8,128)(2,1)S(1)} collective-permute-done((bf16[1024,256]{1,0:T(8,128)(2,1)S(1)}, bf16[1024,256]{1,0:T(8,128)(2,1)S(1)}, u32[]{:S(2)}, u32[]{:S(2)}) %collective-permute-start.5) | collective-permute-done | bytes 524320 | tf_op jit(solution)/shard_map/ppermute | solution.py:24
  92.5 0.1 fusion.5
  92.7 3.8 %collective-permute-start.6 = (bf16[256,256]{1,0:T(8,128)(2,1)S(1)}, bf16[256,256]{1,0:T(8,128)(2,1)S(1)}, u32[]{:S(2)}, u32[]{:S(2)}) collective-permute-start(bf16[256,256]{1,0:T(8,128)(2,1)S(1)} %get-tuple-element.21), channel_id=1, source_target_pairs={{0,4},{1,5},{2,6},{3,7},{4,8},{5,9},{6,10},{7,11},{8,12},{9,13},{1... | collective-permute-start | bytes 393224 | tf_op jit(solution)/shard_map/ppermute | solution.py:39
  96.5 2.7 %collective-permute-start.8 = (bf16[256,256]{1,0:T(8,128)(2,1)S(1)}, bf16[256,256]{1,0:T(8,128)(2,1)S(1)}, u32[]{:S(2)}, u32[]{:S(2)}) collective-permute-start(bf16[256,256]{1,0:T(8,128)(2,1)S(1)} %get-tuple-element.22), channel_id=1, source_target_pairs={{0,12},{1,13},{2,14},{3,15},{4,0},{5,1},{6,2},{7,3},{8,4},{9,5},{1... | collective-permute-start | bytes 393224 | tf_op jit(solution)/shard_map/ppermute | solution.py:39
  99.2 3.6 %collective-permute-start.7 = (bf16[256,256]{1,0:T(8,128)(2,1)S(1)}, bf16[256,256]{1,0:T(8,128)(2,1)S(1)}, u32[]{:S(2)}, u32[]{:S(2)}) collective-permute-start(bf16[256,256]{1,0:T(8,128)(2,1)S(1)} %get-tuple-element.23), channel_id=1, source_target_pairs={{0,8},{1,9},{2,10},{3,11},{4,12},{5,13},{6,14},{7,15},{8,0},{9,1},... | collective-permute-start | bytes 393224 | tf_op jit(solution)/shard_map/ppermute | solution.py:39
  102.8 3.8 %all-to-all-done.1 = bf16[32,40,256]{2,1,0:T(8,128)(2,1)S(1)} async-done(((bf16[32,40,256]{2,1,0:T(8,128)(2,1)}), bf16[32,40,256]{2,1,0:T(8,128)(2,1)S(1)}, u32[]{:S(2)}, u32[]{:S(2)}) %all-to-all-start.1) | async-done | bytes 655392 | tf_op jit(solution)/shard_map/all_to_all | solution.py:380
  106.6 0.1 reduce
  106.7 0.6 broadcast_in_dim.14
  107.3 8.9 %all-to-all-start.2 = ((bf16[16,8,256]{2,1,0:T(8,128)(2,1)}), bf16[16,8,256]{2,1,0:T(8,128)(2,1)S(1)}, u32[]{:S(2)}, u32[]{:S(2)}) async-start(bf16[16,8,256]{2,1,0:T(8,128)(2,1)} %broadcast_in_dim.14), calls=%async_computation.2 | async-start | bytes 131072 | tf_op jit(solution)/shard_map/all_to_all | solution.py:20
  116.3 0.0 collective-permute-done.6
  116.3 0.0 collective-permute-done.8
  116.3 0.0 collective-permute-done.7
  116.3 0.1 slice_add_fusion
  116.4 7.2 %collective-permute-start.9 = (bf16[128,256]{1,0:T(8,128)(2,1)S(1)}, bf16[128,256]{1,0:T(8,128)(2,1)S(1)}, u32[]{:S(2)}, u32[]{:S(2)}) collective-permute-start(bf16[128,256]{1,0:T(8,128)(2,1)S(1)} %slice.55), channel_id=1, source_target_pairs={{0,2},{1,3},{2,0},{3,1},{4,6},{5,7},{6,4},{7,5},{8,10},{9,11},{10,... | collective-permute-start | bytes 196616 | tf_op jit(solution)/shard_map/ppermute | solution.py:24
  123.5 2.4 %all-to-all-done.2 = bf16[16,8,256]{2,1,0:T(8,128)(2,1)S(1)} async-done(((bf16[16,8,256]{2,1,0:T(8,128)(2,1)}), bf16[16,8,256]{2,1,0:T(8,128)(2,1)S(1)}, u32[]{:S(2)}, u32[]{:S(2)}) %all-to-all-start.2) | async-done | bytes 65568 | tf_op jit(solution)/shard_map/all_to_all | solution.py:20
  126.0 0.7 broadcast_in_dim.15
  126.7 5.4 %all-to-all-start.3 = ((bf16[32,8,256]{2,1,0:T(8,128)(2,1)}), bf16[32,8,256]{2,1,0:T(8,128)(2,1)S(1)}, u32[]{:S(2)}, u32[]{:S(2)}) async-start(bf16[32,8,256]{2,1,0:T(8,128)(2,1)} %broadcast_in_dim.15), calls=%async_computation.3 | async-start | bytes 262144 | tf_op jit(solution)/shard_map/all_to_all | solution.py:20
  132.1 0.0 collective-permute-done.9
  132.1 0.8 fusion
  133.0 0.8 fusion.1
  133.7 8.2 %all-to-all-done.3 = bf16[32,8,256]{2,1,0:T(8,128)(2,1)S(1)} async-done(((bf16[32,8,256]{2,1,0:T(8,128)(2,1)}), bf16[32,8,256]{2,1,0:T(8,128)(2,1)S(1)}, u32[]{:S(2)}, u32[]{:S(2)}) %all-to-all-start.3) | async-done | bytes 131104 | tf_op jit(solution)/shard_map/all_to_all | solution.py:20
  142.0 0.7 bitcast_convert_fusion
  (15 shorter events, 0.1 us)
Async XLA Ops:
  0.6 131.5 %copy-start = (bf16[256,256]{1,0:T(8,128)(2,1)S(1)}, bf16[256,256]{1,0:T(8,128)(2,1)}, u32[]{:S(2)}) copy-start(bf16[256,256]{1,0:T(8,128)(2,1)} %param.12) | copy-start | bytes 393220
  3.3 14.5 %copy-start.7 = (bf16[256,256]{1,0:T(8,128)(2,1)S(1)}, bf16[256,256]{1,0:T(8,128)(2,1)}, u32[]{:S(2)}) copy-start(bf16[256,256]{1,0:T(8,128)(2,1)} %get-tuple-element.15) | copy-start | bytes 393220
  3.3 37.7 %copy-start.2 = (bf16[512,256]{1,0:T(8,128)(2,1)S(1)}, bf16[512,256]{1,0:T(8,128)(2,1)}, u32[]{:S(2)}) copy-start(bf16[512,256]{1,0:T(8,128)(2,1)} %get-tuple-element.14) | copy-start | bytes 786436
  3.3 61.7 %copy-start.5 = (s32[1,128]{1,0:T(1,128)S(1)}, s32[1,128]{1,0:T(1,128)}, u32[]{:S(2)}) copy-start(s32[1,128]{1,0:T(1,128)} %param.16) | copy-start | bytes 1540
  3.3 61.7 %copy-start.3 = (s32[1,128]{1,0:T(1,128)S(1)}, s32[1,128]{1,0:T(1,128)}, u32[]{:S(2)}) copy-start(s32[1,128]{1,0:T(1,128)} %param.17) | copy-start | bytes 1540
  3.3 61.7 %copy-start.4 = (s32[1,128]{1,0:T(1,128)S(1)}, s32[1,128]{1,0:T(1,128)}, u32[]{:S(2)}) copy-start(s32[1,128]{1,0:T(1,128)} %param.18) | copy-start | bytes 1540
  3.3 66.7 %all-to-all-start = ((bf16[32,64,256]{2,1,0:T(8,128)(2,1)}), bf16[32,64,256]{2,1,0:T(8,128)(2,1)S(1)}, u32[]{:S(2)}, u32[]{:S(2)}) async-start(bf16[32,64,256]{2,1,0:T(8,128)(2,1)} %get-tuple-element.13), calls=%async_computation | async-start | bytes 2097152 | tf_op jit(solution)/shard_map/all_to_all | solution.py:362
  17.8 23.2 %collective-permute-start = (bf16[256,256]{1,0:T(8,128)(2,1)S(1)}, bf16[256,256]{1,0:T(8,128)(2,1)S(1)}, u32[]{:S(2)}, u32[]{:S(2)}) collective-permute-start(bf16[256,256]{1,0:T(8,128)(2,1)S(1)} %copy-done.7), channel_id=1, source_target_pairs={{0,2},{1,3},{2,0},{3,1},{4,6},{5,7},{6,4},{7,5},{8,10},{9,11},{10,... | collective-permute-start | bytes 393224 | tf_op jit(solution)/shard_map/ppermute | solution.py:24
  40.9 10.6 %collective-permute-start.3 = (bf16[512,256]{1,0:T(8,128)(2,1)S(1)}, bf16[512,256]{1,0:T(8,128)(2,1)S(1)}, u32[]{:S(2)}, u32[]{:S(2)}) collective-permute-start(bf16[512,256]{1,0:T(8,128)(2,1)S(1)} %constant_dynamic-update-slice_fusion.refs_0_), channel_id=1, source_target_pairs={{12,0},{13,1},{14,2},{15,3},{0,4},{1,5},{2,6},{3,7},{4,8},{5,9},{6... | collective-permute-start | bytes 786440 | tf_op jit(solution)/shard_map/ppermute | solution.py:34
  44.1 12.6 %collective-permute-start.2 = (bf16[512,256]{1,0:T(8,128)(2,1)S(1)}, bf16[512,256]{1,0:T(8,128)(2,1)S(1)}, u32[]{:S(2)}, u32[]{:S(2)}) collective-permute-start(bf16[512,256]{1,0:T(8,128)(2,1)S(1)} %constant_dynamic-update-slice_fusion.refs_0_), channel_id=1, source_target_pairs={{8,0},{9,1},{10,2},{11,3},{12,4},{13,5},{14,6},{15,7},{0,8},{1,9},... | collective-permute-start | bytes 786440 | tf_op jit(solution)/shard_map/ppermute | solution.py:34
  48.4 10.2 %collective-permute-start.1 = (bf16[512,256]{1,0:T(8,128)(2,1)S(1)}, bf16[512,256]{1,0:T(8,128)(2,1)S(1)}, u32[]{:S(2)}, u32[]{:S(2)}) collective-permute-start(bf16[512,256]{1,0:T(8,128)(2,1)S(1)} %constant_dynamic-update-slice_fusion.refs_0_), channel_id=1, source_target_pairs={{4,0},{5,1},{6,2},{7,3},{8,4},{9,5},{10,6},{11,7},{12,8},{13,9},{1... | collective-permute-start | bytes 786440 | tf_op jit(solution)/shard_map/ppermute | solution.py:34
  60.1 9.8 %copy-start.1 = (bf16[2048,256]{1,0:T(8,128)(2,1)}, bf16[2048,256]{1,0:T(8,128)(2,1)S(1)}, u32[]{:S(2)}) copy-start(bf16[2048,256]{1,0:T(8,128)(2,1)S(1)} %assemble.1.near_in) | copy-start | bytes 3145732
  60.2 9.8 %collective-permute-start.4 = (bf16[2048,256]{1,0:T(8,128)(2,1)S(1)}, bf16[2048,256]{1,0:T(8,128)(2,1)S(1)}, u32[]{:S(2)}, u32[]{:S(2)}) collective-permute-start(bf16[2048,256]{1,0:T(8,128)(2,1)S(1)} %assemble.1.near_in), channel_id=1, source_target_pairs={{0,1},{1,0},{2,3},{3,2},{4,5},{5,4},{6,7},{7,6},{8,9},{9,8},{10,11... | collective-permute-start | bytes 3145736 | tf_op jit(solution)/shard_map/ppermute | solution.py:24
  70.0 1.0 copy-start.6
  77.2 29.3 %all-to-all-start.1 = ((bf16[32,40,256]{2,1,0:T(8,128)(2,1)}), bf16[32,40,256]{2,1,0:T(8,128)(2,1)S(1)}, u32[]{:S(2)}, u32[]{:S(2)}) async-start(bf16[32,40,256]{2,1,0:T(8,128)(2,1)} %get-tuple-element.18), calls=%async_computation.1 | async-start | bytes 1310720 | tf_op jit(solution)/shard_map/all_to_all | solution.py:380
  88.6 3.9 %collective-permute-start.5 = (bf16[1024,256]{1,0:T(8,128)(2,1)S(1)}, bf16[1024,256]{1,0:T(8,128)(2,1)S(1)}, u32[]{:S(2)}, u32[]{:S(2)}) collective-permute-start(bf16[1024,256]{1,0:T(8,128)(2,1)S(1)} %get-tuple-element.17), channel_id=1, source_target_pairs={{0,1},{1,0},{2,3},{3,2},{4,5},{5,4},{6,7},{7,6},{8,9},{9,8},{10,11... | collective-permute-start | bytes 1572872 | tf_op jit(solution)/shard_map/ppermute | solution.py:24
  92.7 23.6 %collective-permute-start.6 = (bf16[256,256]{1,0:T(8,128)(2,1)S(1)}, bf16[256,256]{1,0:T(8,128)(2,1)S(1)}, u32[]{:S(2)}, u32[]{:S(2)}) collective-permute-start(bf16[256,256]{1,0:T(8,128)(2,1)S(1)} %get-tuple-element.21), channel_id=1, source_target_pairs={{0,4},{1,5},{2,6},{3,7},{4,8},{5,9},{6,10},{7,11},{8,12},{9,13},{1... | collective-permute-start | bytes 393224 | tf_op jit(solution)/shard_map/ppermute | solution.py:39
  96.5 19.7 %collective-permute-start.8 = (bf16[256,256]{1,0:T(8,128)(2,1)S(1)}, bf16[256,256]{1,0:T(8,128)(2,1)S(1)}, u32[]{:S(2)}, u32[]{:S(2)}) collective-permute-start(bf16[256,256]{1,0:T(8,128)(2,1)S(1)} %get-tuple-element.22), channel_id=1, source_target_pairs={{0,12},{1,13},{2,14},{3,15},{4,0},{5,1},{6,2},{7,3},{8,4},{9,5},{1... | collective-permute-start | bytes 393224 | tf_op jit(solution)/shard_map/ppermute | solution.py:39
  99.2 17.1 %collective-permute-start.7 = (bf16[256,256]{1,0:T(8,128)(2,1)S(1)}, bf16[256,256]{1,0:T(8,128)(2,1)S(1)}, u32[]{:S(2)}, u32[]{:S(2)}) collective-permute-start(bf16[256,256]{1,0:T(8,128)(2,1)S(1)} %get-tuple-element.23), channel_id=1, source_target_pairs={{0,8},{1,9},{2,10},{3,11},{4,12},{5,13},{6,14},{7,15},{8,0},{9,1},... | collective-permute-start | bytes 393224 | tf_op jit(solution)/shard_map/ppermute | solution.py:39
  107.3 18.7 %all-to-all-start.2 = ((bf16[16,8,256]{2,1,0:T(8,128)(2,1)}), bf16[16,8,256]{2,1,0:T(8,128)(2,1)S(1)}, u32[]{:S(2)}, u32[]{:S(2)}) async-start(bf16[16,8,256]{2,1,0:T(8,128)(2,1)} %broadcast_in_dim.14), calls=%async_computation.2 | async-start | bytes 131072 | tf_op jit(solution)/shard_map/all_to_all | solution.py:20
  116.4 15.7 %collective-permute-start.9 = (bf16[128,256]{1,0:T(8,128)(2,1)S(1)}, bf16[128,256]{1,0:T(8,128)(2,1)S(1)}, u32[]{:S(2)}, u32[]{:S(2)}) collective-permute-start(bf16[128,256]{1,0:T(8,128)(2,1)S(1)} %slice.55), channel_id=1, source_target_pairs={{0,2},{1,3},{2,0},{3,1},{4,6},{5,7},{6,4},{7,5},{8,10},{9,11},{10,... | collective-permute-start | bytes 196616 | tf_op jit(solution)/shard_map/ppermute | solution.py:24
  126.7 15.3 %all-to-all-start.3 = ((bf16[32,8,256]{2,1,0:T(8,128)(2,1)}), bf16[32,8,256]{2,1,0:T(8,128)(2,1)S(1)}, u32[]{:S(2)}, u32[]{:S(2)}) async-start(bf16[32,8,256]{2,1,0:T(8,128)(2,1)} %broadcast_in_dim.15), calls=%async_computation.3 | async-start | bytes 262144 | tf_op jit(solution)/shard_map/all_to_all | solution.py:20

commit v9 on v8

--- a/solution.py
+++ b/solution.py
@@ -197,41 +197,29 @@
     )(*parts)
 
 
-def lay_out_kernel(grad_user, user_emb, grad_item, item_emb, mine, pair, pieces, sems):
+def lay_out_kernel(grad_user, user_emb, grad_item, item_emb, mine, pair, pieces):
     rows = grad_user.shape[0]
+    mine[:rows] = grad_user[...]
+    mine[rows:] = user_emb[...]
+    pair[:rows] = grad_user[...]
+    pair[rows : 2 * rows] = user_emb[...]
+    pair[2 * rows :] = jnp.zeros((2 * rows, pair.shape[1]), pair.dtype)
     item_rows = grad_item.shape[0]
-    moves = []
-    for index, source in enumerate((grad_user, user_emb)):
-        for target in (mine, pair):
-            moves.append((source, target.at[pl.ds(index * rows, rows)]))
-    moves.append((grad_user, pair.at[pl.ds(2 * rows, rows)]))
-    moves.append((user_emb, pair.at[pl.ds(3 * rows, rows)]))
     for peer in range(pieces.shape[0]):
-        for index, source in enumerate((grad_item, item_emb)):
-            moves.append((source, pieces.at[peer, pl.ds(index * item_rows, item_rows)]))
-    copies = [
-        pltpu.make_async_copy(source, target, sems.at[index])
-        for index, (source, target) in enumerate(moves)
-    ]
-    for copy in copies:
-        copy.start()
-    for copy in copies:
-        copy.wait()
+        pieces[peer, :item_rows] = grad_item[...]
+        pieces[peer, item_rows:] = item_emb[...]
 
 
 def lay_out(grad_user, user_emb, grad_item, item_emb):
     peers = lax.axis_size("au")
     rows, width = grad_user.shape
-    in_place = pl.BlockSpec(memory_space=pltpu.HBM)
     return pl.pallas_call(
         lay_out_kernel,
-        out_specs=[in_place] * 3,
         out_shape=[
             jax.ShapeDtypeStruct((2 * rows, width), grad_user.dtype),
             jax.ShapeDtypeStruct((4 * rows, width), grad_user.dtype),
             jax.ShapeDtypeStruct((peers, 2 * grad_item.shape[0], width), grad_item.dtype),
         ],
-        scratch_shapes=[pltpu.SemaphoreType.DMA((6 + 2 * peers,))],
         name="lay_out",
     )(grad_user, user_emb, grad_item, item_emb)
 
@@ -260,22 +248,28 @@
     peers, both_rows, width = item_rows.shape
     piece_rows = both_rows // 2
     half_rows, all_items = dense.shape[1:]
-    dense_copies = [
-        pltpu.make_async_copy(ref, dense.at[half], sems.at[half])
-        for half, ref in enumerate((dense_near, dense_far))
+    split = half_rows // 2
+    first = [
+        pltpu.make_async_copy(
+            dense_near.at[pl.ds(start, split)], dense.at[0, pl.ds(start, split)], sems.at[index]
+        )
+        for start, index in ((0, 0), (split, 4))
     ]
+    far_copy = pltpu.make_async_copy(dense_far, dense.at[1], sems.at[1])
     source_copies = [
         pltpu.make_async_copy(ref, sources.at[half], sems.at[2 + half])
         for half, ref in enumerate((near_in, far_in))
     ]
-    for half in range(2):
-        dense_copies[half].start()
-        source_copies[half].start()
+    for copy in (*first, source_copies[0], far_copy, source_copies[1]):
+        copy.start()
     items = item_rows[:, :piece_rows].reshape(all_items, width)
     weight_term = jnp.zeros((width, width), jnp.float32)
     for half, user in enumerate((user_near, user_far)):
-        dense_copies[half].wait()
+        if half == 1:
+            far_copy.wait()
         for start in range(0, half_rows, step):
+            if half == 0 and start % split == 0:
+                first[start // split].wait()
             rows = dense[half, start : start + step]
             user[start : start + step] = jnp.dot(
                 rows, items, preferred_element_type=jnp.float32
@@ -317,7 +311,7 @@
             pltpu.VMEM((2, half_rows, all_items), low),
             pltpu.VMEM((2, 2 * half_rows, width), low),
             pltpu.VMEM((width, all_items), jnp.float32),
-            pltpu.SemaphoreType.DMA((4,)),
+            pltpu.SemaphoreType.DMA((5,)),
         ],
         compiler_params=pltpu.CompilerParams(vmem_limit_bytes=32 << 20),
         cost_estimate=pl.CostEstimate(

time: 143 us -> 143 us (level)
  no operation moved by 1% of the time
where the time goes in v9:
time: 143 us; the launch traced here: 142 us
  starting transfers between devices  79.2 us (55%)
  waiting for transfers between devices  41.5 us (29%)
  Pallas kernels  14.6 us (10%)
  local copies, waits for them, and re-layouts  2.34 us (2%)
  matrix products  1.62 us (1%)
  between operations  1.61 us (1%)
    ppermute x4, waiting for transfers between devices, partner(): lax.ppermute(value, 'ia', [(i, i ^ bit) for i in range(lax.axis_size('ia'...  19.9 us
    ppermute x4, starting transfers between devices, partner(): lax.ppermute(value, 'ia', [(i, i ^ bit) for i in range(lax.axis_size('ia'...  18.5 us
    all_to_all x1, starting transfers between devices, device_step(): lax.all_to_all(item_sent, 'au', split_axis=0, concat_axis=0, tiled=True)  14.4 us
    all_to_all x2, starting transfers between devices, from_everyone(): return lax.all_to_all(copies, axis, split_axis=0, concat_axis=0, tiled=True)  14.3 us
    all_to_all x1, starting transfers between devices, device_step(): lax.all_to_all(pieces, 'au', split_axis=0, concat_axis=0, tiled=True)  11.4 us
    all_to_all x2, waiting for transfers between devices, from_everyone(): return lax.all_to_all(copies, axis, split_axis=0, concat_axis=0, tiled=True)  10.7 us
    ppermute x3, starting transfers between devices, from_ahead(): lax.ppermute(value, 'ia', [(ahead(i, distance), i) for i in range(size)])  10.5 us
    ppermute x3, starting transfers between devices, send_ahead(): lax.ppermute(value, 'ia', [(i, ahead(i, distance)) for i in range(size)])  10.1 us
  transfers between devices with their start and end apart: 14, of which 7 were waited for; matrix products, arithmetic and copies ran while one was open for 2% of the time, Pallas kernels for 5%

profile of v9, /device:TPU:1, one launch (start us, length us, event | category | flops | bytes accessed | tf_op | source)
XLA Modules:
  0.0 141.9 jit_solution(3813970036435648586)
XLA Ops:
  0.6 0.0 copy-start
  0.6 2.1 %lay_out.1 = (bf16[256,256]{1,0:T(8,128)(2,1)}, bf16[512,256]{1,0:T(8,128)(2,1)}, bf16[32,64,256]{2,1,0:T(8,128)(2,1)}) custom-call(bf16[128,256]{1,0:T(8,128)(2,1)} %bitcast.23, bf16[128,256]{1,0:T(8,128)(2,1)} %bitcast.24, bf16[32,256]{1,0:T(8,128)(2,1)} %bitcast.25, bf16[32,256]{1,0:T(8,128)(2,1)} %bitcast.26), custom_call_target="tpu_custom_call" | custom-call | tf_op jit(solution)/shard_map/lay_out/pallas_call | solution.py:216
  2.7 0.0 copy-start.3
  2.7 0.0 copy-start.4
  2.8 14.4 %all-to-all-start = ((bf16[32,64,256]{2,1,0:T(8,128)(2,1)}), bf16[32,64,256]{2,1,0:T(8,128)(2,1)S(1)}, u32[]{:S(2)}, u32[]{:S(2)}) async-start(bf16[32,64,256]{2,1,0:T(8,128)(2,1)} %get-tuple-element.13), calls=%async_computation | async-start | bytes 2097152 | tf_op jit(solution)/shard_map/all_to_all | solution.py:356
  17.2 0.0 copy-done.7
  17.2 4.8 %collective-permute-start = (bf16[256,256]{1,0:T(8,128)(2,1)S(1)}, bf16[256,256]{1,0:T(8,128)(2,1)S(1)}, u32[]{:S(2)}, u32[]{:S(2)}) collective-permute-start(bf16[256,256]{1,0:T(8,128)(2,1)S(1)} %copy-done.7), channel_id=1, source_target_pairs={{0,2},{1,3},{2,0},{3,1},{4,6},{5,7},{6,4},{7,5},{8,10},{9,11},{10,... | collective-permute-start | bytes 393224 | tf_op jit(solution)/shard_map/ppermute | solution.py:24
  22.0 18.4 %collective-permute-done = bf16[256,256]{1,0:T(8,128)(2,1)S(1)} collective-permute-done((bf16[256,256]{1,0:T(8,128)(2,1)S(1)}, bf16[256,256]{1,0:T(8,128)(2,1)S(1)}, u32[]{:S(2)}, u32[]{:S(2)}) %collective-permute-start) | collective-permute-done | bytes 131104 | tf_op jit(solution)/shard_map/ppermute | solution.py:24
  40.4 0.0 copy-done.2
  40.4 3.1 %collective-permute-start.3 = (bf16[512,256]{1,0:T(8,128)(2,1)S(1)}, bf16[512,256]{1,0:T(8,128)(2,1)S(1)}, u32[]{:S(2)}, u32[]{:S(2)}) collective-permute-start(bf16[512,256]{1,0:T(8,128)(2,1)S(1)} %constant_dynamic-update-slice_fusion.refs_0_), channel_id=1, source_target_pairs={{12,0},{13,1},{14,2},{15,3},{0,4},{1,5},{2,6},{3,7},{4,8},{5,9},{6... | collective-permute-start | bytes 786440 | tf_op jit(solution)/shard_map/ppermute | solution.py:34
  43.5 4.4 %collective-permute-start.2 = (bf16[512,256]{1,0:T(8,128)(2,1)S(1)}, bf16[512,256]{1,0:T(8,128)(2,1)S(1)}, u32[]{:S(2)}, u32[]{:S(2)}) collective-permute-start(bf16[512,256]{1,0:T(8,128)(2,1)S(1)} %constant_dynamic-update-slice_fusion.refs_0_), channel_id=1, source_target_pairs={{8,0},{9,1},{10,2},{11,3},{12,4},{13,5},{14,6},{15,7},{0,8},{1,9},... | collective-permute-start | bytes 786440 | tf_op jit(solution)/shard_map/ppermute | solution.py:34
  47.9 3.1 %collective-permute-start.1 = (bf16[512,256]{1,0:T(8,128)(2,1)S(1)}, bf16[512,256]{1,0:T(8,128)(2,1)S(1)}, u32[]{:S(2)}, u32[]{:S(2)}) collective-permute-start(bf16[512,256]{1,0:T(8,128)(2,1)S(1)} %constant_dynamic-update-slice_fusion.refs_0_), channel_id=1, source_target_pairs={{4,0},{5,1},{6,2},{7,3},{8,4},{9,5},{10,6},{11,7},{12,8},{13,9},{1... | collective-permute-start | bytes 786440 | tf_op jit(solution)/shard_map/ppermute | solution.py:34
  50.9 0.0 collective-permute-done.3.refs_3_
  51.0 5.2 %collective-permute-done.2.refs_2_ = bf16[512,256]{1,0:T(8,128)(2,1)S(1)} collective-permute-done((bf16[512,256]{1,0:T(8,128)(2,1)S(1)}, bf16[512,256]{1,0:T(8,128)(2,1)S(1)}, u32[]{:S(2)}, u32[]{:S(2)}) %collective-permute-start.2) | collective-permute-done | bytes 262176 | tf_op jit(solution)/shard_map/ppermute | solution.py:34
  56.1 2.0 %collective-permute-done.1.refs_1_ = bf16[512,256]{1,0:T(8,128)(2,1)S(1)} collective-permute-done((bf16[512,256]{1,0:T(8,128)(2,1)S(1)}, bf16[512,256]{1,0:T(8,128)(2,1)S(1)}, u32[]{:S(2)}, u32[]{:S(2)}) %collective-permute-start.1) | collective-permute-done | bytes 262176 | tf_op jit(solution)/shard_map/ppermute | solution.py:34
  58.1 1.5 %assemble.1.near_in = bf16[2048,256]{1,0:T(8,128)(2,1)S(1)} custom-call(bf16[512,256]{1,0:T(8,128)(2,1)S(1)} %constant_dynamic-update-slice_fusion.refs_0_, bf16[512,256]{1,0:T(8,128)(2,1)S(1)} %collective-permute-done.1.refs_1_, bf16[512,256]{1,0:T(8,128)(2,1)S(1)} %collective-permute-done.2.refs_2_, bf16[512,256]{1,0:T(8,128)(2,1)S(1)} %collective-permute-done.3.refs_3_), custom_call_target="tpu_custom_call" | custom-call | tf_op jit(solution)/shard_map/assemble/pallas_call | solution.py:191
  59.6 4.1 %collective-permute-start.4 = (bf16[2048,256]{1,0:T(8,128)(2,1)S(1)}, bf16[2048,256]{1,0:T(8,128)(2,1)S(1)}, u32[]{:S(2)}, u32[]{:S(2)}) collective-permute-start(bf16[2048,256]{1,0:T(8,128)(2,1)S(1)} %assemble.1.near_in), channel_id=1, source_target_pairs={{0,1},{1,0},{2,3},{3,2},{4,5},{5,4},{6,7},{7,6},{8,9},{9,8},{10,11... | collective-permute-start | bytes 3145736 | tf_op jit(solution)/shard_map/ppermute | solution.py:24
  64.4 0.0 copy-done.5
  64.4 4.9 %dense_block.1 = (bf16[1024,1024]{1,0:T(8,128)(2,1)}, bf16[1024,1024]{1,0:T(8,128)(2,1)}) custom-call(s32[128]{0:T(128)S(1)} %add_bitcast_fusion.rows, s32[128]{0:T(128)S(1)} %bitcast.20, s32[128]{0:T(128)S(1)} %bitcast.21, s32[1]{0:T(128)} %bitcast.19.count, bf16[128,128,128]{2,1,0:T(8,128)(2,1)} %bitcast.22), custom_call_target="tpu_custom_call" | custom-call | flops 8388608 | bytes 8388608 | tf_op jit(solution)/shard_map/dense_block/pallas_call | solution.py:141
  69.4 0.0 collective-permute-done.4.far_in
  69.4 0.0 all-to-all-done.item_rows
  69.4 1.0 copy-done.6
  70.4 6.1 %finish.1 = (bf16[1024,256]{1,0:T(8,128)(2,1)S(1)}, bf16[1024,256]{1,0:T(8,128)(2,1)S(1)}, bf16[32,40,256]{2,1,0:T(8,128)(2,1)}) custom-call(bf16[1024,1024]{1,0:T(8,128)(2,1)} %get-tuple-element.11.dense_near, bf16[1024,1024]{1,0:T(8,128)(2,1)} %get-tuple-element.12.dense_far, bf16[32,64,256]{2,1,0:T(8,128)(2,1)S(1)} %all-to-all-done.item_rows, ...), custom_call_target="tpu_custom_call" | custom-call | flops 2147483648 | bytes 6291456 | tf_op jit(solution)/shard_map/finish/pallas_call | solution.py:302
  76.5 11.4 %all-to-all-start.1 = ((bf16[32,40,256]{2,1,0:T(8,128)(2,1)}), bf16[32,40,256]{2,1,0:T(8,128)(2,1)S(1)}, u32[]{:S(2)}, u32[]{:S(2)}) async-start(bf16[32,40,256]{2,1,0:T(8,128)(2,1)} %get-tuple-element.18), calls=%async_computation.1 | async-start | bytes 1310720 | tf_op jit(solution)/shard_map/all_to_all | solution.py:374
  87.9 2.4 %collective-permute-start.5 = (bf16[1024,256]{1,0:T(8,128)(2,1)S(1)}, bf16[1024,256]{1,0:T(8,128)(2,1)S(1)}, u32[]{:S(2)}, u32[]{:S(2)}) collective-permute-start(bf16[1024,256]{1,0:T(8,128)(2,1)S(1)} %get-tuple-element.17), channel_id=1, source_target_pairs={{0,1},{1,0},{2,3},{3,2},{4,5},{5,4},{6,7},{7,6},{8,9},{9,8},{10,11... | collective-permute-start | bytes 1572872 | tf_op jit(solution)/shard_map/ppermute | solution.py:24
  90.3 1.5 %collective-permute-done.5 = bf16[1024,256]{1,0:T(8,128)(2,1)S(1)} collective-permute-done((bf16[1024,256]{1,0:T(8,128)(2,1)S(1)}, bf16[1024,256]{1,0:T(8,128)(2,1)S(1)}, u32[]{:S(2)}, u32[]{:S(2)}) %collective-permute-start.5) | collective-permute-done | bytes 524320 | tf_op jit(solution)/shard_map/ppermute | solution.py:24
  91.8 0.1 fusion.5
  91.9 3.8 %collective-permute-start.6 = (bf16[256,256]{1,0:T(8,128)(2,1)S(1)}, bf16[256,256]{1,0:T(8,128)(2,1)S(1)}, u32[]{:S(2)}, u32[]{:S(2)}) collective-permute-start(bf16[256,256]{1,0:T(8,128)(2,1)S(1)} %get-tuple-element.21), channel_id=1, source_target_pairs={{0,4},{1,5},{2,6},{3,7},{4,8},{5,9},{6,10},{7,11},{8,12},{9,13},{1... | collective-permute-start | bytes 393224 | tf_op jit(solution)/shard_map/ppermute | solution.py:39
  95.8 2.7 %collective-permute-start.8 = (bf16[256,256]{1,0:T(8,128)(2,1)S(1)}, bf16[256,256]{1,0:T(8,128)(2,1)S(1)}, u32[]{:S(2)}, u32[]{:S(2)}) collective-permute-start(bf16[256,256]{1,0:T(8,128)(2,1)S(1)} %get-tuple-element.22), channel_id=1, source_target_pairs={{0,12},{1,13},{2,14},{3,15},{4,0},{5,1},{6,2},{7,3},{8,4},{9,5},{1... | collective-permute-start | bytes 393224 | tf_op jit(solution)/shard_map/ppermute | solution.py:39
  98.5 3.6 %collective-permute-start.7 = (bf16[256,256]{1,0:T(8,128)(2,1)S(1)}, bf16[256,256]{1,0:T(8,128)(2,1)S(1)}, u32[]{:S(2)}, u32[]{:S(2)}) collective-permute-start(bf16[256,256]{1,0:T(8,128)(2,1)S(1)} %get-tuple-element.23), channel_id=1, source_target_pairs={{0,8},{1,9},{2,10},{3,11},{4,12},{5,13},{6,14},{7,15},{8,0},{9,1},... | collective-permute-start | bytes 393224 | tf_op jit(solution)/shard_map/ppermute | solution.py:39
  102.1 3.8 %all-to-all-done.1 = bf16[32,40,256]{2,1,0:T(8,128)(2,1)S(1)} async-done(((bf16[32,40,256]{2,1,0:T(8,128)(2,1)}), bf16[32,40,256]{2,1,0:T(8,128)(2,1)S(1)}, u32[]{:S(2)}, u32[]{:S(2)}) %all-to-all-start.1) | async-done | bytes 655392 | tf_op jit(solution)/shard_map/all_to_all | solution.py:374
  105.8 0.1 reduce
  105.9 0.6 broadcast_in_dim.14
  106.6 8.9 %all-to-all-start.2 = ((bf16[16,8,256]{2,1,0:T(8,128)(2,1)}), bf16[16,8,256]{2,1,0:T(8,128)(2,1)S(1)}, u32[]{:S(2)}, u32[]{:S(2)}) async-start(bf16[16,8,256]{2,1,0:T(8,128)(2,1)} %broadcast_in_dim.14), calls=%async_computation.2 | async-start | bytes 131072 | tf_op jit(solution)/shard_map/all_to_all | solution.py:20
  115.5 0.0 collective-permute-done.6
  115.5 0.0 collective-permute-done.8
  115.5 0.0 collective-permute-done.7
  115.5 0.1 slice_add_fusion
  115.6 7.2 %collective-permute-start.9 = (bf16[128,256]{1,0:T(8,128)(2,1)S(1)}, bf16[128,256]{1,0:T(8,128)(2,1)S(1)}, u32[]{:S(2)}, u32[]{:S(2)}) collective-permute-start(bf16[128,256]{1,0:T(8,128)(2,1)S(1)} %slice.55), channel_id=1, source_target_pairs={{0,2},{1,3},{2,0},{3,1},{4,6},{5,7},{6,4},{7,5},{8,10},{9,11},{10,... | collective-permute-start | bytes 196616 | tf_op jit(solution)/shard_map/ppermute | solution.py:24
  122.8 2.4 %all-to-all-done.2 = bf16[16,8,256]{2,1,0:T(8,128)(2,1)S(1)} async-done(((bf16[16,8,256]{2,1,0:T(8,128)(2,1)}), bf16[16,8,256]{2,1,0:T(8,128)(2,1)S(1)}, u32[]{:S(2)}, u32[]{:S(2)}) %all-to-all-start.2) | async-done | bytes 65568 | tf_op jit(solution)/shard_map/all_to_all | solution.py:20
  125.3 0.7 broadcast_in_dim.15
  125.9 5.4 %all-to-all-start.3 = ((bf16[32,8,256]{2,1,0:T(8,128)(2,1)}), bf16[32,8,256]{2,1,0:T(8,128)(2,1)S(1)}, u32[]{:S(2)}, u32[]{:S(2)}) async-start(bf16[32,8,256]{2,1,0:T(8,128)(2,1)} %broadcast_in_dim.15), calls=%async_computation.3 | async-start | bytes 262144 | tf_op jit(solution)/shard_map/all_to_all | solution.py:20
  131.4 0.0 collective-permute-done.9
  131.4 0.0 copy-done
  131.4 0.8 fusion
  132.2 0.8 fusion.1
  133.0 8.2 %all-to-all-done.3 = bf16[32,8,256]{2,1,0:T(8,128)(2,1)S(1)} async-done(((bf16[32,8,256]{2,1,0:T(8,128)(2,1)}), bf16[32,8,256]{2,1,0:T(8,128)(2,1)S(1)}, u32[]{:S(2)}, u32[]{:S(2)}) %all-to-all-start.3) | async-done | bytes 131104 | tf_op jit(solution)/shard_map/all_to_all | solution.py:20
  141.2 0.7 bitcast_convert_fusion
  (15 shorter events, 0.1 us)
Async XLA Ops:
  0.6 130.7 %copy-start = (bf16[256,256]{1,0:T(8,128)(2,1)S(1)}, bf16[256,256]{1,0:T(8,128)(2,1)}, u32[]{:S(2)}) copy-start(bf16[256,256]{1,0:T(8,128)(2,1)} %param.12) | copy-start | bytes 393220
  2.7 14.5 %copy-start.7 = (bf16[256,256]{1,0:T(8,128)(2,1)S(1)}, bf16[256,256]{1,0:T(8,128)(2,1)}, u32[]{:S(2)}) copy-start(bf16[256,256]{1,0:T(8,128)(2,1)} %get-tuple-element.15) | copy-start | bytes 393220
  2.7 37.6 %copy-start.2 = (bf16[512,256]{1,0:T(8,128)(2,1)S(1)}, bf16[512,256]{1,0:T(8,128)(2,1)}, u32[]{:S(2)}) copy-start(bf16[512,256]{1,0:T(8,128)(2,1)} %get-tuple-element.14) | copy-start | bytes 786436
  2.7 61.7 %copy-start.5 = (s32[1,128]{1,0:T(1,128)S(1)}, s32[1,128]{1,0:T(1,128)}, u32[]{:S(2)}) copy-start(s32[1,128]{1,0:T(1,128)} %param.16) | copy-start | bytes 1540
  2.7 61.7 %copy-start.3 = (s32[1,128]{1,0:T(1,128)S(1)}, s32[1,128]{1,0:T(1,128)}, u32[]{:S(2)}) copy-start(s32[1,128]{1,0:T(1,128)} %param.17) | copy-start | bytes 1540
  2.7 61.7 %copy-start.4 = (s32[1,128]{1,0:T(1,128)S(1)}, s32[1,128]{1,0:T(1,128)}, u32[]{:S(2)}) copy-start(s32[1,128]{1,0:T(1,128)} %param.18) | copy-start | bytes 1540
  2.8 66.7 %all-to-all-start = ((bf16[32,64,256]{2,1,0:T(8,128)(2,1)}), bf16[32,64,256]{2,1,0:T(8,128)(2,1)S(1)}, u32[]{:S(2)}, u32[]{:S(2)}) async-start(bf16[32,64,256]{2,1,0:T(8,128)(2,1)} %get-tuple-element.13), calls=%async_computation | async-start | bytes 2097152 | tf_op jit(solution)/shard_map/all_to_all | solution.py:356
  17.2 23.2 %collective-permute-start = (bf16[256,256]{1,0:T(8,128)(2,1)S(1)}, bf16[256,256]{1,0:T(8,128)(2,1)S(1)}, u32[]{:S(2)}, u32[]{:S(2)}) collective-permute-start(bf16[256,256]{1,0:T(8,128)(2,1)S(1)} %copy-done.7), channel_id=1, source_target_pairs={{0,2},{1,3},{2,0},{3,1},{4,6},{5,7},{6,4},{7,5},{8,10},{9,11},{10,... | collective-permute-start | bytes 393224 | tf_op jit(solution)/shard_map/ppermute | solution.py:24
  40.4 10.6 %collective-permute-start.3 = (bf16[512,256]{1,0:T(8,128)(2,1)S(1)}, bf16[512,256]{1,0:T(8,128)(2,1)S(1)}, u32[]{:S(2)}, u32[]{:S(2)}) collective-permute-start(bf16[512,256]{1,0:T(8,128)(2,1)S(1)} %constant_dynamic-update-slice_fusion.refs_0_), channel_id=1, source_target_pairs={{12,0},{13,1},{14,2},{15,3},{0,4},{1,5},{2,6},{3,7},{4,8},{5,9},{6... | collective-permute-start | bytes 786440 | tf_op jit(solution)/shard_map/ppermute | solution.py:34
  43.5 12.6 %collective-permute-start.2 = (bf16[512,256]{1,0:T(8,128)(2,1)S(1)}, bf16[512,256]{1,0:T(8,128)(2,1)S(1)}, u32[]{:S(2)}, u32[]{:S(2)}) collective-permute-start(bf16[512,256]{1,0:T(8,128)(2,1)S(1)} %constant_dynamic-update-slice_fusion.refs_0_), channel_id=1, source_target_pairs={{8,0},{9,1},{10,2},{11,3},{12,4},{13,5},{14,6},{15,7},{0,8},{1,9},... | collective-permute-start | bytes 786440 | tf_op jit(solution)/shard_map/ppermute | solution.py:34
  47.9 10.2 %collective-permute-start.1 = (bf16[512,256]{1,0:T(8,128)(2,1)S(1)}, bf16[512,256]{1,0:T(8,128)(2,1)S(1)}, u32[]{:S(2)}, u32[]{:S(2)}) collective-permute-start(bf16[512,256]{1,0:T(8,128)(2,1)S(1)} %constant_dynamic-update-slice_fusion.refs_0_), channel_id=1, source_target_pairs={{4,0},{5,1},{6,2},{7,3},{8,4},{9,5},{10,6},{11,7},{12,8},{13,9},{1... | collective-permute-start | bytes 786440 | tf_op jit(solution)/shard_map/ppermute | solution.py:34
  59.6 9.8 %copy-start.1 = (bf16[2048,256]{1,0:T(8,128)(2,1)}, bf16[2048,256]{1,0:T(8,128)(2,1)S(1)}, u32[]{:S(2)}) copy-start(bf16[2048,256]{1,0:T(8,128)(2,1)S(1)} %assemble.1.near_in) | copy-start | bytes 3145732
  59.6 9.8 %collective-permute-start.4 = (bf16[2048,256]{1,0:T(8,128)(2,1)S(1)}, bf16[2048,256]{1,0:T(8,128)(2,1)S(1)}, u32[]{:S(2)}, u32[]{:S(2)}) collective-permute-start(bf16[2048,256]{1,0:T(8,128)(2,1)S(1)} %assemble.1.near_in), channel_id=1, source_target_pairs={{0,1},{1,0},{2,3},{3,2},{4,5},{5,4},{6,7},{7,6},{8,9},{9,8},{10,11... | collective-permute-start | bytes 3145736 | tf_op jit(solution)/shard_map/ppermute | solution.py:24
  69.4 1.0 copy-start.6
  76.5 29.3 %all-to-all-start.1 = ((bf16[32,40,256]{2,1,0:T(8,128)(2,1)}), bf16[32,40,256]{2,1,0:T(8,128)(2,1)S(1)}, u32[]{:S(2)}, u32[]{:S(2)}) async-start(bf16[32,40,256]{2,1,0:T(8,128)(2,1)} %get-tuple-element.18), calls=%async_computation.1 | async-start | bytes 1310720 | tf_op jit(solution)/shard_map/all_to_all | solution.py:374
  87.9 3.9 %collective-permute-start.5 = (bf16[1024,256]{1,0:T(8,128)(2,1)S(1)}, bf16[1024,256]{1,0:T(8,128)(2,1)S(1)}, u32[]{:S(2)}, u32[]{:S(2)}) collective-permute-start(bf16[1024,256]{1,0:T(8,128)(2,1)S(1)} %get-tuple-element.17), channel_id=1, source_target_pairs={{0,1},{1,0},{2,3},{3,2},{4,5},{5,4},{6,7},{7,6},{8,9},{9,8},{10,11... | collective-permute-start | bytes 1572872 | tf_op jit(solution)/shard_map/ppermute | solution.py:24
  91.9 23.6 %collective-permute-start.6 = (bf16[256,256]{1,0:T(8,128)(2,1)S(1)}, bf16[256,256]{1,0:T(8,128)(2,1)S(1)}, u32[]{:S(2)}, u32[]{:S(2)}) collective-permute-start(bf16[256,256]{1,0:T(8,128)(2,1)S(1)} %get-tuple-element.21), channel_id=1, source_target_pairs={{0,4},{1,5},{2,6},{3,7},{4,8},{5,9},{6,10},{7,11},{8,12},{9,13},{1... | collective-permute-start | bytes 393224 | tf_op jit(solution)/shard_map/ppermute | solution.py:39
  95.8 19.7 %collective-permute-start.8 = (bf16[256,256]{1,0:T(8,128)(2,1)S(1)}, bf16[256,256]{1,0:T(8,128)(2,1)S(1)}, u32[]{:S(2)}, u32[]{:S(2)}) collective-permute-start(bf16[256,256]{1,0:T(8,128)(2,1)S(1)} %get-tuple-element.22), channel_id=1, source_target_pairs={{0,12},{1,13},{2,14},{3,15},{4,0},{5,1},{6,2},{7,3},{8,4},{9,5},{1... | collective-permute-start | bytes 393224 | tf_op jit(solution)/shard_map/ppermute | solution.py:39
  98.5 17.1 %collective-permute-start.7 = (bf16[256,256]{1,0:T(8,128)(2,1)S(1)}, bf16[256,256]{1,0:T(8,128)(2,1)S(1)}, u32[]{:S(2)}, u32[]{:S(2)}) collective-permute-start(bf16[256,256]{1,0:T(8,128)(2,1)S(1)} %get-tuple-element.23), channel_id=1, source_target_pairs={{0,8},{1,9},{2,10},{3,11},{4,12},{5,13},{6,14},{7,15},{8,0},{9,1},... | collective-permute-start | bytes 393224 | tf_op jit(solution)/shard_map/ppermute | solution.py:39
  106.6 18.7 %all-to-all-start.2 = ((bf16[16,8,256]{2,1,0:T(8,128)(2,1)}), bf16[16,8,256]{2,1,0:T(8,128)(2,1)S(1)}, u32[]{:S(2)}, u32[]{:S(2)}) async-start(bf16[16,8,256]{2,1,0:T(8,128)(2,1)} %broadcast_in_dim.14), calls=%async_computation.2 | async-start | bytes 131072 | tf_op jit(solution)/shard_map/all_to_all | solution.py:20
  115.6 15.7 %collective-permute-start.9 = (bf16[128,256]{1,0:T(8,128)(2,1)S(1)}, bf16[128,256]{1,0:T(8,128)(2,1)S(1)}, u32[]{:S(2)}, u32[]{:S(2)}) collective-permute-start(bf16[128,256]{1,0:T(8,128)(2,1)S(1)} %slice.55), channel_id=1, source_target_pairs={{0,2},{1,3},{2,0},{3,1},{4,6},{5,7},{6,4},{7,5},{8,10},{9,11},{10,... | collective-permute-start | bytes 196616 | tf_op jit(solution)/shard_map/ppermute | solution.py:24
  125.9 15.3 %all-to-all-start.3 = ((bf16[32,8,256]{2,1,0:T(8,128)(2,1)}), bf16[32,8,256]{2,1,0:T(8,128)(2,1)S(1)}, u32[]{:S(2)}, u32[]{:S(2)}) async-start(bf16[32,8,256]{2,1,0:T(8,128)(2,1)} %broadcast_in_dim.15), calls=%async_computation.3 | async-start | bytes 262144 | tf_op jit(solution)/shard_map/all_to_all | solution.py:20
